TPU v7x, 32 devices: a whole 2x2x4 slice. The times are simulated.
32 devices in a mesh: dp: 2 (over y), row: 4 (over x, core), col: 4 (over z).
Axes of the slice: x: 2, y: 2, z: 4, core: 2. Of those that a mesh axis runs over, the one named last changes fastest.
Arguments:
- tokens: bfloat16 [10240, 2048], P(('dp', 'col'), 'row'), may hold values from -6 to 6
- cotangent: bfloat16 [10240, 2048], P(('dp', 'col'), 'row'), may hold values from -6 to 6
- attention_norm_gain: float32 [2048], P('row'), may hold values from 0.5 to 1.5
- feedfwd_norm_gain: float32 [2048], P('row'), may hold values from 0.5 to 1.5
- query_norm_gain: float32 [128], replicated, may hold values from 0.8 to 2
- key_norm_gain: float32 [128], replicated, may hold values from 0.8 to 2
- query_matrix: bfloat16 [2048, 2048], P('row', 'col'), may hold values from -0.125 to 0.125
- key_matrix: bfloat16 [2048, 1024], P('row', 'col'), may hold values from -0.125 to 0.125
- value_matrix: bfloat16 [2048, 1024], P('row', 'col'), may hold values from -0.125 to 0.125
- output_matrix: bfloat16 [2048, 2048], P('col', 'row'), may hold values from -0.5 to 0.5
- gate_matrix: bfloat16 [2048, 6144], P('row', 'col'), may hold values from -0.125 to 0.125
- up_matrix: bfloat16 [2048, 6144], P('row', 'col'), may hold values from -0.125 to 0.125
- down_matrix: bfloat16 [6144, 2048], P('col', 'row'), may hold values from -0.078125 to 0.078125
- query_adapter_inmaps: bfloat16 [2048, 128], P('row'), may hold values from -0.125 to 0.125
- query_adapter_outmaps: bfloat16 [128, 2048], P(None, 'col'), may hold values from -0.75 to 0.75
- key_adapter_inmaps: bfloat16 [2048, 128], P('row'), may hold values from -0.125 to 0.125
- key_adapter_outmaps: bfloat16 [128, 1024], P(None, 'col'), may hold values from -0.75 to 0.75
- value_adapter_inmaps: bfloat16 [2048, 128], P('row'), may hold values from -0.125 to 0.125
- value_adapter_outmaps: bfloat16 [128, 1024], P(None, 'col'), may hold values from -0.75 to 0.75
- output_adapter_inmaps: bfloat16 [2048, 128], P('col'), may hold values from -0.5 to 0.5
- output_adapter_outmaps: bfloat16 [128, 2048], P(None, 'row'), may hold values from -0.75 to 0.75
- gate_adapter_inmaps: bfloat16 [2048, 128], P('row'), may hold values from -0.125 to 0.125
- gate_adapter_outmaps: bfloat16 [128, 6144], P(None, 'col'), may hold values from -0.75 to 0.75
- up_adapter_inmaps: bfloat16 [2048, 128], P('row'), may hold values from -0.125 to 0.125
- up_adapter_outmaps: bfloat16 [128, 6144], P(None, 'col'), may hold values from -0.75 to 0.75
- down_adapter_inmaps: bfloat16 [6144, 128], P('col'), may hold values from -0.078125 to 0.078125
- down_adapter_outmaps: bfloat16 [128, 2048], P(None, 'row'), may hold values from -0.75 to 0.75
- segment: int32 [10240], P('dp'), may hold values from 0 to 12, as said below
- depth: int32 [10240], P('dp'), may hold values from 0 to 2559, as said below
- parent: int32 [2, 13], P('dp'), may hold values from 0 to 4, as said below
- adapter: int32 [2], P('dp'), may hold values from 0 to 7
Outputs:
- output: bfloat16 [10240, 2048], P(('dp', 'col'), 'row')
- input_gradient: float32 [10240, 2048], P(('dp', 'col'), 'row')
- grad_a_q: float32 [2048, 128], P('row')
- grad_b_q: float32 [128, 2048], P(None, 'col')
- grad_a_k: float32 [2048, 128], P('row')
- grad_b_k: float32 [128, 1024], P(None, 'col')
- grad_a_v: float32 [2048, 128], P('row')
- grad_b_v: float32 [128, 1024], P(None, 'col')
- grad_a_o: float32 [2048, 128], P('col')
- grad_b_o: float32 [128, 2048], P(None, 'row')
- grad_a_gate: float32 [2048, 128], P('row')
- grad_b_gate: float32 [128, 6144], P(None, 'col')
- grad_a_up: float32 [2048, 128], P('row')
- grad_b_up: float32 [128, 6144], P(None, 'col')
- grad_a_down: float32 [6144, 128], P('col')
- grad_b_down: float32 [128, 2048], P(None, 'row')
Inputs may be any that keep to these rules, and one draw needn't show every extreme that they name: `segment`: in each tree, the first 2048 tokens are node 0, the trunk; the rest are 12 blocks of 256 tokens, one block for each of the nodes 1 to 4 (branches) and 5 onward (leaves), in any order. Trunk tokens have depth 0 to 2047 in order, a branch's tokens 2048 onward, a leaf's tokens 2048 + 256 onward, in order within the block. The trunk and every branch have parent 0; every leaf's parent is a branch, each branch having 8 // 4 leaves.
All inputs are finite; a program needn't handle non-finite values.
Results may differ from a plain program's by a relative error of at most 0.017.
The roundings to bfloat16 on the way count: a program that leaves them out, or rounds other values in their place, can miss the bound.
Values may be sent and summed in bfloat16 or wider, within the bound.
No kernel may reach another device: no remote copies, remote signals or barrier semaphores. Data moves between devices by JAX's collectives and lax.ppermute only.
A program may use at most 384 MiB of HBM per device.

v0:
```python
import jax
import jax.numpy as jnp
from jax import lax
from jax.sharding import PartitionSpec as P

MODEL_WIDTH = 2048
HEAD_SIZE = 128
ADAPTER_RANK = 16
TREE_LEN = 5120


EPSILON = 1e-06
THETA = 1000000.0
ADAPTER_FACTOR = 2.0
HIGH = lax.Precision.HIGHEST
NEGATIVE = -1e30


def matrix_product(left, right):
    return jnp.dot(left, right, preferred_element_type=jnp.float32)


def precise(left, right):
    return jnp.dot(left, right, precision=HIGH, preferred_element_type=jnp.float32)


def multiply_transposed(left, right):
    return lax.dot_general(
        left, right, (((1,), (1,)), ((), ())), preferred_element_type=jnp.float32
    )


def exact_transpose_product(left, right):
    return lax.dot_general(
        left, right, (((1,), (1,)), ((), ())), precision=HIGH, preferred_element_type=jnp.float32
    )


def precise_inner(left, right):
    return lax.dot_general(
        left, right, (((0,), (0,)), ((), ())), precision=HIGH, preferred_element_type=jnp.float32
    )


def lookup(table, index):
    hits = index[:, None] == jnp.arange(table.shape[0])[None, :]
    return jnp.sum(jnp.where(hits, table[None, :], 0), axis=1)


def gather_cols(local):
    return lax.all_gather(local, "col", axis=0, tiled=True)


def gather_rows(local):
    return lax.all_gather(local, "row", axis=0, tiled=True)


def row_totals(term, total):
    return lax.psum_scatter(
        term(jnp.int32(0), total // lax.axis_size("row") * lax.axis_size("row")),
        "row",
        scatter_dimension=0,
        tiled=True,
    )


def column_totals(term, total):
    return lax.psum_scatter(
        term(jnp.int32(0), total // lax.axis_size("col") * lax.axis_size("col")),
        "col",
        scatter_dimension=0,
        tiled=True,
    )


def feature_sum(values):
    return lax.psum(values, "row")


def norm_back(values, scale, gain, gradient_tuple):
    weighted = gain * gradient_tuple
    inner_sum = feature_sum(jnp.sum(weighted * values, axis=1))[:, None]
    return scale * weighted - values * scale**3 * inner_sum / MODEL_WIDTH


def ahead_summation(
    whole_rows,
    weight_tuple,
    adapter_inmap_list,
    adapter_outmap_list,
    select_adapter,
    reduce_function,
):
    weight_matrix = jnp.concatenate(weight_tuple, axis=1)
    adapter_inmap = jnp.concatenate(adapter_inmap_list, axis=1)
    spread_columns = select_adapter.shape[1]
    masked_rows = matrix_product(whole_rows, adapter_inmap) * jnp.tile(
        select_adapter, (1, len(adapter_inmap_list))
    )
    outmaps_spread = [make_array.astype(jnp.float32) for make_array in adapter_outmap_list]

    def term(start, count):
        extra = jnp.concatenate(
            [
                precise(
                    masked_rows[:, place_rows * spread_columns : (place_rows + 1) * spread_columns],
                    outmaps_spread[place_rows],
                )
                for place_rows in range(len(outmaps_spread))
            ],
            axis=1,
        )
        return matrix_product(whole_rows, weight_matrix) + ADAPTER_FACTOR * extra

    return (masked_rows, reduce_function(term, whole_rows.shape[0]))


def reverse_summation(
    gradient_tuple,
    weight_tuple,
    adapter_inmap_list,
    adapter_outmap_list,
    select_adapter,
    reduce_function,
):
    weight_matrix = jnp.concatenate(weight_tuple, axis=1)
    adapter_inmap = jnp.concatenate(adapter_inmap_list, axis=1).astype(jnp.float32)
    pieces = []
    column_offset = 0
    for place_rows in range(len(weight_tuple)):
        column_width = weight_tuple[place_rows].shape[1]
        pieces.append(
            ADAPTER_FACTOR
            * multiply_transposed(
                gradient_tuple[:, column_offset : column_offset + column_width],
                adapter_outmap_list[place_rows],
            )
            * select_adapter
        )
        column_offset = column_offset + column_width
    inner_product = jnp.concatenate(pieces, axis=1)

    def term(start, count):
        return multiply_transposed(gradient_tuple, weight_matrix) + exact_transpose_product(
            inner_product, adapter_inmap
        )

    return (inner_product, reduce_function(term, gradient_tuple.shape[0]))


def adapter_grads(input_rows, masked_rows, gradient_tuple, inner_product, widths, spread_columns):
    left = precise_inner(input_rows.astype(jnp.float32), inner_product)
    grads_in = [
        left[:, place_rows * spread_columns : (place_rows + 1) * spread_columns]
        for place_rows in range(len(widths))
    ]
    grads_out = []
    column_offset = 0
    for place_rows in range(len(widths)):
        grads_out.append(
            ADAPTER_FACTOR
            * precise_inner(
                masked_rows[:, place_rows * spread_columns : (place_rows + 1) * spread_columns],
                gradient_tuple[:, column_offset : column_offset + widths[place_rows]].astype(
                    jnp.float32
                ),
            )
        )
        column_offset = column_offset + widths[place_rows]
    return (grads_in, grads_out)


def rotate(values, positions):
    half = HEAD_SIZE // 2
    freqs = THETA ** (-2.0 * jnp.arange(half).astype(jnp.float32) / HEAD_SIZE)
    angle = positions[:, None, None] * freqs[None, None, :]
    cosine = jnp.cos(angle)
    sine = jnp.sin(angle)
    first = values[..., :half]
    second = values[..., half:]
    return jnp.concatenate(
        [first * cosine - second * sine, second * cosine + first * sine], axis=-1
    )


def head_shape(gain, positions):

    def shaped(flat):
        lines = flat.reshape(flat.shape[0], -1, HEAD_SIZE)
        normed = lines * lax.rsqrt(jnp.mean(lines * lines, axis=-1, keepdims=True) + EPSILON) * gain
        return rotate(normed, positions).reshape(flat.shape[0], -1)

    return shaped


def on_device(
    tokens,
    cotangent,
    attention_norm_gain,
    feedfwd_norm_gain,
    query_norm_gain,
    key_norm_gain,
    query_matrix,
    key_matrix,
    value_matrix,
    output_matrix,
    gate_matrix,
    up_matrix,
    down_matrix,
    query_adapter_inmaps,
    query_adapter_outmaps,
    key_adapter_inmaps,
    key_adapter_outmaps,
    value_adapter_inmaps,
    value_adapter_outmaps,
    output_adapter_inmaps,
    output_adapter_outmaps,
    gate_adapter_inmaps,
    gate_adapter_outmaps,
    up_adapter_inmaps,
    up_adapter_outmaps,
    down_adapter_inmaps,
    down_adapter_outmaps,
    segment,
    depth,
    parent,
    adapter,
):
    resid = tokens.astype(jnp.float32)
    scale_one = lax.rsqrt(feature_sum(jnp.sum(resid * resid, axis=1)) / MODEL_WIDTH + EPSILON)[
        :, None
    ]
    hidden_state = (resid * scale_one * attention_norm_gain).astype(jnp.bfloat16)
    gathered = gather_cols(hidden_state)
    total = gathered.shape[0]
    spread_columns = query_adapter_inmaps.shape[1]
    chosen = lookup(adapter, jnp.arange(total) // TREE_LEN)
    select_adapter = (
        chosen[:, None] == jnp.arange(spread_columns)[None, :] // ADAPTER_RANK
    ).astype(jnp.float32)
    masked_qkv, projected = ahead_summation(
        gathered,
        [query_matrix, key_matrix, value_matrix],
        [query_adapter_inmaps, key_adapter_inmaps, value_adapter_inmaps],
        [query_adapter_outmaps, key_adapter_outmaps, value_adapter_outmaps],
        select_adapter,
        row_totals,
    )
    own = projected.shape[0]
    start_row = lax.axis_index("row") * own
    node_count = parent.shape[1]
    q_width = query_matrix.shape[1]
    kv_width = key_matrix.shape[1]
    query_before_norm = projected[:, :q_width]
    key_before_norm = projected[:, q_width : q_width + kv_width]
    value_projected = projected[:, q_width + kv_width :]
    own_seg = lax.dynamic_slice_in_dim(segment, start_row, own, 0)
    own_depth = lax.dynamic_slice_in_dim(depth, start_row, own, 0)
    own_tree = (start_row + jnp.arange(own)) // TREE_LEN
    flat_parent = parent.reshape(-1)
    first_up = lookup(flat_parent, own_tree * node_count + own_seg)
    second_up = lookup(flat_parent, own_tree * node_count + first_up)
    positions = own_depth.astype(jnp.float32)
    query_full, query_back = jax.vjp(head_shape(query_norm_gain, positions), query_before_norm)
    key_full, key_back = jax.vjp(head_shape(key_norm_gain, positions), key_before_norm)
    key_rows, value_rows = (
        lax.all_gather(key_full.astype(jnp.bfloat16), "row", axis=0, tiled=True),
        lax.all_gather(value_projected.astype(jnp.bfloat16), "row", axis=0, tiled=True),
    )
    span = max(own, TREE_LEN)
    key_start = start_row // span * span
    blocks = span // own
    groups_kv = kv_width // HEAD_SIZE
    per_group = q_width // kv_width
    query_heads = query_full.astype(jnp.bfloat16).reshape(own, groups_kv, per_group, HEAD_SIZE)
    key_blocks = key_rows.reshape(blocks, own, groups_kv, HEAD_SIZE)
    value_blocks = value_rows.reshape(blocks, own, groups_kv, HEAD_SIZE)
    seg_blocks = segment.reshape(blocks, own)
    depth_blocks = depth.reshape(blocks, own)
    tree_blocks = ((key_start + jnp.arange(span)) // TREE_LEN).reshape(blocks, own)
    block_items = (key_blocks, value_blocks, seg_blocks, depth_blocks, tree_blocks)
    scale = HEAD_SIZE ** (-0.5)

    def scores_of(key_block, seg_block, depth_block, tree_block):
        scores = (
            jnp.einsum("qigd,kid->igqk", query_heads, key_block, preferred_element_type=jnp.float32)
            * scale
        )
        visible = (
            (tree_block[None, :] == own_tree[:, None])
            & (
                (seg_block[None, :] == own_seg[:, None])
                | (seg_block[None, :] == first_up[:, None])
                | (seg_block[None, :] == second_up[:, None])
            )
            & (depth_block[None, :] <= own_depth[:, None])
        )
        return (scores, visible[None, None])

    def max_step(carry, items):
        running, totals = carry
        key_block, value_block, seg_block, depth_block, tree_block = items
        scores, visible = scores_of(key_block, seg_block, depth_block, tree_block)
        newest = jnp.maximum(running, jnp.max(jnp.where(visible, scores, NEGATIVE), axis=-1))
        totals = totals * jnp.exp(running - newest) + jnp.sum(
            jnp.where(visible, jnp.exp(scores - newest[..., None]), 0.0), axis=-1
        )
        return ((newest, totals), None)

    stat_shape = (groups_kv, per_group, own)
    (running, totals), unused = lax.scan(
        max_step,
        (jnp.full(stat_shape, NEGATIVE, jnp.float32), jnp.zeros(stat_shape, jnp.float32)),
        block_items,
    )
    log_total = running + jnp.log(totals)

    def value_step(carry, items):
        key_block, value_block, seg_block, depth_block, tree_block = items
        scores, visible = scores_of(key_block, seg_block, depth_block, tree_block)
        probs = jnp.where(visible, jnp.exp(scores - log_total[..., None]), 0.0)
        return (
            carry
            + jnp.einsum(
                "igqk,kid->qigd",
                probs.astype(jnp.bfloat16),
                value_block,
                preferred_element_type=jnp.float32,
            ),
            None,
        )

    attended_full, unused = lax.scan(
        value_step, jnp.zeros((own, groups_kv, per_group, HEAD_SIZE), jnp.float32), block_items
    )
    attended_low = attended_full.reshape(own, q_width).astype(jnp.bfloat16)
    collected_attention = gather_rows(attended_low)
    masked_o, branch_index = ahead_summation(
        collected_attention,
        [output_matrix],
        [output_adapter_inmaps],
        [output_adapter_outmaps],
        select_adapter,
        column_totals,
    )
    middle_values = resid + branch_index
    scale_two = lax.rsqrt(
        feature_sum(jnp.sum(middle_values * middle_values, axis=1)) / MODEL_WIDTH + EPSILON
    )[:, None]
    feedfwd_hidden_state = (middle_values * scale_two * feedfwd_norm_gain).astype(jnp.bfloat16)
    gathered_ffn = gather_cols(feedfwd_hidden_state)
    ffn_width = gate_matrix.shape[1]
    masked_ffn, gate_up = ahead_summation(
        gathered_ffn,
        [gate_matrix, up_matrix],
        [gate_adapter_inmaps, up_adapter_inmaps],
        [gate_adapter_outmaps, up_adapter_outmaps],
        select_adapter,
        row_totals,
    )
    gate_values = gate_up[:, :ffn_width]
    upward_pass = gate_up[:, ffn_width:]
    sigma = jax.nn.sigmoid(gate_values)
    swish = gate_values * sigma
    swish_output = (swish * upward_pass).astype(jnp.bfloat16)
    collected_swish = gather_rows(swish_output)
    masked_down, last = ahead_summation(
        collected_swish,
        [down_matrix],
        [down_adapter_inmaps],
        [down_adapter_outmaps],
        select_adapter,
        column_totals,
    )
    output = (middle_values + last).astype(jnp.bfloat16)
    grad_out = cotangent.astype(jnp.float32)
    collected_gradient = gather_cols(cotangent)
    inner_down, grad_act = reverse_summation(
        collected_gradient,
        [down_matrix],
        [down_adapter_inmaps],
        [down_adapter_outmaps],
        select_adapter,
        row_totals,
    )
    in_down, out_down = adapter_grads(
        collected_swish,
        masked_down,
        collected_gradient,
        inner_down,
        [down_matrix.shape[1]],
        spread_columns,
    )
    slope = sigma * (1.0 + gate_values * (1.0 - sigma))
    grad_gate_up = jnp.concatenate(
        [grad_act * upward_pass * slope, grad_act * swish], axis=1
    ).astype(jnp.bfloat16)
    gathered_gu = gather_rows(grad_gate_up)
    inner_ffn, grad_hidden_ffn = reverse_summation(
        gathered_gu,
        [gate_matrix, up_matrix],
        [gate_adapter_inmaps, up_adapter_inmaps],
        [gate_adapter_outmaps, up_adapter_outmaps],
        select_adapter,
        column_totals,
    )
    in_ffn, out_ffn = adapter_grads(
        gathered_ffn, masked_ffn, gathered_gu, inner_ffn, [ffn_width, ffn_width], spread_columns
    )
    grad_middle = grad_out + norm_back(middle_values, scale_two, feedfwd_norm_gain, grad_hidden_ffn)
    collected_middle = gather_cols(grad_middle.astype(jnp.bfloat16))
    inner_o, grad_attended = reverse_summation(
        collected_middle,
        [output_matrix],
        [output_adapter_inmaps],
        [output_adapter_outmaps],
        select_adapter,
        row_totals,
    )
    in_o, out_o = adapter_grads(
        collected_attention,
        masked_o,
        collected_middle,
        inner_o,
        [output_matrix.shape[1]],
        spread_columns,
    )
    grad_low = grad_attended.astype(jnp.bfloat16)
    grad_heads = grad_low.reshape(own, groups_kv, per_group, HEAD_SIZE)
    delta = jnp.transpose(
        jnp.sum(grad_heads.astype(jnp.float32) * attended_full, axis=-1), (1, 2, 0)
    )

    def grad_step(carry, items):
        key_block, value_block, seg_block, depth_block, tree_block = items
        scores, visible = scores_of(key_block, seg_block, depth_block, tree_block)
        probs = jnp.where(visible, jnp.exp(scores - log_total[..., None]), 0.0)
        grad_probs = jnp.einsum(
            "qigd,kid->igqk", grad_heads, value_block, preferred_element_type=jnp.float32
        )
        grad_scores = (probs * (grad_probs - delta[..., None])).astype(jnp.bfloat16)
        carry = (
            carry
            + jnp.einsum(
                "igqk,kid->qigd", grad_scores, key_block, preferred_element_type=jnp.float32
            )
            * scale
        )
        grad_keys = (
            jnp.einsum(
                "igqk,qigd->kid", grad_scores, query_heads, preferred_element_type=jnp.float32
            )
            * scale
        )
        grad_values = jnp.einsum(
            "igqk,qigd->kid",
            probs.astype(jnp.bfloat16),
            grad_heads,
            preferred_element_type=jnp.float32,
        )
        return (carry, (grad_keys, grad_values))

    grad_query_heads, (key_parts, value_parts) = lax.scan(
        grad_step, jnp.zeros((own, groups_kv, per_group, HEAD_SIZE), jnp.float32), block_items
    )
    key_whole = key_parts.reshape(span, kv_width)
    value_whole = value_parts.reshape(span, kv_width)
    grad_keys_own, grad_values_own = (
        lax.psum_scatter(key_whole, "row", scatter_dimension=0, tiled=True),
        lax.psum_scatter(value_whole, "row", scatter_dimension=0, tiled=True),
    )
    grad_query_pre = query_back(grad_query_heads.reshape(own, q_width))[0]
    grad_key_pre = key_back(grad_keys_own)[0]
    grad_qkv = jnp.concatenate([grad_query_pre, grad_key_pre, grad_values_own], axis=1).astype(
        jnp.bfloat16
    )
    gathered_qkv = gather_rows(grad_qkv)
    inner_qkv, grad_hidden = reverse_summation(
        gathered_qkv,
        [query_matrix, key_matrix, value_matrix],
        [query_adapter_inmaps, key_adapter_inmaps, value_adapter_inmaps],
        [query_adapter_outmaps, key_adapter_outmaps, value_adapter_outmaps],
        select_adapter,
        column_totals,
    )
    in_qkv, out_qkv = adapter_grads(
        gathered, masked_qkv, gathered_qkv, inner_qkv, [q_width, kv_width, kv_width], spread_columns
    )
    input_gradient = grad_middle + norm_back(resid, scale_one, attention_norm_gain, grad_hidden)
    by_cols = lax.psum(
        (in_qkv[0], in_qkv[1], in_qkv[2], in_ffn[0], in_ffn[1], out_o[0], out_down[0]),
        ("dp", "col"),
    )
    by_rows = lax.psum(
        (out_qkv[0], out_qkv[1], out_qkv[2], out_ffn[0], out_ffn[1], in_o[0], in_down[0]),
        ("dp", "row"),
    )
    return (
        output,
        input_gradient,
        by_cols[0],
        by_rows[0],
        by_cols[1],
        by_rows[1],
        by_cols[2],
        by_rows[2],
        by_rows[5],
        by_cols[5],
        by_cols[3],
        by_rows[3],
        by_cols[4],
        by_rows[4],
        by_rows[6],
        by_cols[6],
    )


def solution(mesh):
    return jax.shard_map(
        on_device,
        mesh=mesh,
        in_specs=(
            P(("dp", "col"), "row"),
            P(("dp", "col"), "row"),
            P("row"),
            P("row"),
            P(),
            P(),
            P("row", "col"),
            P("row", "col"),
            P("row", "col"),
            P("col", "row"),
            P("row", "col"),
            P("row", "col"),
            P("col", "row"),
            P("row", None),
            P(None, "col"),
            P("row", None),
            P(None, "col"),
            P("row", None),
            P(None, "col"),
            P("col", None),
            P(None, "row"),
            P("row", None),
            P(None, "col"),
            P("row", None),
            P(None, "col"),
            P("col", None),
            P(None, "row"),
            P("dp"),
            P("dp"),
            P("dp", None),
            P("dp"),
        ),
        out_specs=(
            P(("dp", "col"), "row"),
            P(("dp", "col"), "row"),
            P("row", None),
            P(None, "col"),
            P("row", None),
            P(None, "col"),
            P("row", None),
            P(None, "col"),
            P("col", None),
            P(None, "row"),
            P("row", None),
            P(None, "col"),
            P("row", None),
            P(None, "col"),
            P("col", None),
            P(None, "row"),
        ),
        check_vma=False,
    )
```

profile of v0, /device:TPU:0, one launch (start us, length us, event | category | flops | bytes accessed | tf_op | source)
XLA Modules:
  0.0 4036.2 jit_solution(14569572773216615195)
XLA Ops:
  47.5 72.5 %all-gather.11.cloned.1.call-done = bf16[5120,512]{1,0:T(8,128)(2,1)} async-done(((bf16[1280,512]{1,0:T(8,128)(2,1)}), bf16[5120,512]{1,0:T(8,128)(2,1)}) %all-gather.11.cloned.1.call-update) | async-done | bytes 5242896 | tf_op jit(solution)/shard_map/all_gather | solution.py:51
  143.8 28.3 fusion.53
  176.5 147.2 %reduce-scatter.10.cloned.1.call-done = f32[1280,1024]{1,0:T(8,128)} async-done(((f32[5120,1024]{1,0:T(8,128)}), f32[1280,1024]{1,0:T(8,128)}) %reduce-scatter.10.cloned.1.call-update) | async-done | bytes 5242896 | tf_op jit(solution)/shard_map/reduce_scatter | solution.py:59
  380.7 116.1 %while.39 = (s32[]{:T(128)}, f32[2,2,1280]{2,1,0:T(2,128)S(1)}, f32[2,2,1280]{2,1,0:T(2,128)S(1)}, s32[4,1280]{1,0:T(4,128)}, s32[4,1280]{1,0:T(4,128)}, /*index...) while((s32[]{:T(128)}, f32[2,2,1280]{2,1,0:T(2,128)S(1)}, ...), condition=%wide.region_10.11_spmd.clone, body=%wide.region_7.10_spmd.clone.sunk | while | flops 1731825920 | bytes 59653792 | solution.py:311
  501.8 74.9 %while.40 = (s32[]{:T(128)}, f32[1280,2,2,128]{0,3,2,1:T(8,128)}, bf16[4,1280,2,128]{3,2,1,0:T(2,128)(2,1)}, s32[4,1280]{1,0:T(4,128)}, s32[4,1280]{1,0:T(4,128)...) while((s32[]{:T(128)}, f32[1280,2,2,128]{0,3,2,1:T(8,128)}, ...), condition=%wide.region_12.13_spmd.clone, body=%wide.region_11.12_spmd.clone.sunk | while | flops 3397725440 | bytes 13860527 | solution.py:333
  579.9 40.4 %all-gather.17.cloned.1.call-done = bf16[5120,512]{0,1:T(8,128)(2,1)} async-done(((bf16[1280,512]{0,1:T(8,128)(2,1)}), bf16[5120,512]{0,1:T(8,128)(2,1)}) %all-gather.17.cloned.1.call-update) | async-done | bytes 5242896 | tf_op jit(solution)/shard_map/all_gather | solution.py:55
  639.0 177.4 %reduce-scatter.12.cloned.1.call-done = f32[1280,512]{1,0:T(8,128)} async-done(((f32[5120,512]{1,0:T(8,128)}), f32[1280,512]{1,0:T(8,128)}) %reduce-scatter.12.cloned.1.call-update) | async-done | bytes 2621456 | tf_op jit(solution)/shard_map/reduce_scatter | solution.py:68
  829.8 87.4 %all-gather.23.cloned.1.call-done = bf16[5120,512]{1,0:T(8,128)(2,1)} async-done(((bf16[1280,512]{1,0:T(8,128)(2,1)}), bf16[5120,512]{1,0:T(8,128)(2,1)}) %all-gather.23.cloned.1.call-update) | async-done | bytes 5242896 | tf_op jit(solution)/shard_map/all_gather | solution.py:51
  970.9 44.9 %all-gather.19.cloned.1.call-done = bf16[5120,512]{1,0:T(8,128)(2,1)} async-done(((bf16[1280,512]{1,0:T(8,128)(2,1)}), bf16[5120,512]{1,0:T(8,128)(2,1)}) %all-gather.19.cloned.1.call-update) | async-done | bytes 5242896 | tf_op jit(solution)/shard_map/all_gather | solution.py:51
  1062.6 45.9 %fusion.52 = f32[5120,3072]{1,0:T(8,128)} fusion(f32[5120,1536]{1,0:T(8,128)} %fusion.95, f32[5120,1536]{1,0:T(8,128)} %fusion.98, bf16[5120,512]{1,0:T(8,128)(2,1)} %all-gather.19.cloned.1.call-done, bf16[512,3072]{1,0:T(8,128)(2,1)} %constant_dynamic-update-slice_fusion.6), kind=kOutput, calls=%fused_computation.86 | convolution fusion | flops 16153313280 | bytes 134217728 | tf_op jit(solution)/shard_map/dot_general | solution.py:20
  1110.4 128.2 %reduce-scatter.16.cloned.1.call-done = f32[1280,1536]{1,0:T(8,128)} async-done(((f32[5120,1536]{1,0:T(8,128)}), f32[1280,1536]{1,0:T(8,128)}) %reduce-scatter.16.cloned.1.call-update) | async-done | bytes 7864336 | tf_op jit(solution)/shard_map/reduce_scatter | solution.py:59
  1238.6 1032.3 %all-reduce.11.cloned.1.call-done = f32[5120,3072]{1,0:T(8,128)} async-done(((f32[5120,3072]{1,0:T(8,128)}), f32[5120,3072]{1,0:T(8,128)}) %all-reduce.11.cloned.1.call-update) | async-done | bytes 62914576
  2292.0 189.4 %all-gather.25.cloned.1.call-done = bf16[5120,3072]{1,0:T(8,128)(2,1)} async-done(((bf16[1280,3072]{1,0:T(8,128)(2,1)}), bf16[5120,3072]{1,0:T(8,128)(2,1)}) %all-gather.25.cloned.1.call-update) | async-done | bytes 31457296 | tf_op jit(solution)/shard_map/all_gather | solution.py:55
  2535.0 47.9 %all-gather.21.cloned.1.call-done = bf16[5120,1536]{1,0:T(8,128)(2,1)} async-done(((bf16[1280,1536]{1,0:T(8,128)(2,1)}), bf16[5120,1536]{1,0:T(8,128)(2,1)}) %all-gather.21.cloned.1.call-update) | async-done | bytes 15728656 | tf_op jit(solution)/shard_map/all_gather | solution.py:55
  2614.7 148.8 %reduce-scatter.18.cloned.1.call-done = f32[1280,512]{1,0:T(8,128)} async-done(((f32[5120,512]{1,0:T(8,128)}), f32[1280,512]{1,0:T(8,128)}) %reduce-scatter.18.cloned.1.call-update) | async-done | bytes 2621456 | tf_op jit(solution)/shard_map/reduce_scatter | solution.py:68
  2773.4 171.4 %reduce-scatter.14.cloned.1.call-done = f32[1280,512]{1,0:T(8,128)} async-done(((f32[5120,512]{1,0:T(8,128)}), f32[1280,512]{1,0:T(8,128)}) %reduce-scatter.14.cloned.1.call-update) | async-done | bytes 2621456 | tf_op jit(solution)/shard_map/reduce_scatter | solution.py:68
  2950.4 99.2 %all-gather.27.cloned.1.call-done = bf16[5120,512]{1,0:T(8,128)(2,1)} async-done(((bf16[1280,512]{1,0:T(8,128)(2,1)}), bf16[5120,512]{1,0:T(8,128)(2,1)}) %all-gather.27.cloned.1.call-update) | async-done | bytes 5242896 | tf_op jit(solution)/shard_map/all_gather | solution.py:51
  3065.0 83.8 %reduce-scatter.20.cloned.1.call-done = f32[1280,512]{1,0:T(8,128)} async-done(((f32[5120,512]{1,0:T(8,128)}), f32[1280,512]{1,0:T(8,128)}) %reduce-scatter.20.cloned.1.call-update) | async-done | bytes 2621456 | tf_op jit(solution)/shard_map/reduce_scatter | solution.py:59
  3157.4 278.4 %while.41 = (s32[]{:T(128)}, f32[1280,2,2,128]{0,3,2,1:T(8,128)}, f32[4,1280,2,128]{3,2,1,0:T(2,128)}, f32[4,1280,2,128]{3,2,1,0:T(2,128)}, bf16[4,1280,2,128]{3...) while((s32[]{:T(128)}, f32[1280,2,2,128]{0,3,2,1:T(8,128)}, ...), condition=%wide.region_25.26_spmd.clone, body=%wide.region_24.25_spmd.clone.sunk | while | flops 8451533824 | bytes 142987984 | solution.py:463
  3511.7 34.6 reduce-scatter.24.cloned.1.call-done
  3549.7 70.3 %all-gather.29.cloned.1.call-done = bf16[5120,1024]{1,0:T(8,128)(2,1)} async-done(((bf16[1280,1024]{1,0:T(8,128)(2,1)}), bf16[5120,1024]{1,0:T(8,128)(2,1)}) %all-gather.29.cloned.1.call-update) | async-done | bytes 10485776 | tf_op jit(solution)/shard_map/all_gather | solution.py:55
  3749.1 81.2 %reduce-scatter.26.cloned.1.call-done = f32[1280,512]{1,0:T(8,128)} async-done(((f32[5120,512]{1,0:T(8,128)}), f32[1280,512]{1,0:T(8,128)}) %reduce-scatter.26.cloned.1.call-update) | async-done | bytes 2621456 | tf_op jit(solution)/shard_map/reduce_scatter | solution.py:68
  3843.6 64.6 %all-reduce.15.cloned.1.call-done = (f32[128,512]{1,0:T(8,128)}, f32[128,256]{1,0:T(8,128)}, f32[128,256]{1,0:T(8,128)}, f32[512,128]{1,0:T(8,128)}, f32[128,153...) async-done(((f32[128,512]{1,0:T(8,128)}, f32[128,256]{1,0:T(8,128)}, f32[128,256]{1,0:T(8,128)}, f32[512,128]{1,0:T(8,128)}, f32[128,1536]{1,0:T(8,128)}, ...) | async-done | bytes 3145744 | tf_op jit(solution)/shard_map/psum | solution.py:494
  3908.2 104.7 %all-reduce.13.cloned.1.call-done = (f32[512,128]{1,0:T(8,128)}, f32[512,128]{1,0:T(8,128)}, f32[512,128]{1,0:T(8,128)}, f32[128,512]{1,0:T(8,128)}, f32[512,128...) async-done(((f32[512,128]{1,0:T(8,128)}, f32[512,128]{1,0:T(8,128)}, f32[512,128]{1,0:T(8,128)}, f32[128,512]{1,0:T(8,128)}, f32[512,128]{1,0:T(8,128)}, ...) | async-done | bytes 1835024 | tf_op jit(solution)/shard_map/psum | solution.py:490
  (583 shorter events, 1117.4 us)
Async XLA Ops:
  7.2 932.1 %copy-start = (bf16[1536,512]{1,0:T(8,128)(2,1)S(1)}, bf16[1536,512]{1,0:T(8,128)(2,1)}, u32[]{:S(2)}) copy-start(bf16[1536,512]{1,0:T(8,128)(2,1)} %param.49) | copy-start | bytes 4718596
  7.2 112.8 %all-gather.11.cloned.1.call-start = ((), (), s32[]{:S(2)}) async-start(), calls=%async_computation.9 | async-start | bytes 6553600 | tf_op jit(solution)/shard_map/all_gather | solution.py:51
  21.5 302.3 %reduce-scatter.10.cloned.1.call-start = ((), (), s32[]{:S(2)}) async-start(), calls=%async_computation.10 | async-start | bytes 26214400 | tf_op jit(solution)/shard_map/reduce_scatter | solution.py:59
  172.1 199.4 %all-gather.15.cloned.1.call-start = ((), (), s32[]{:S(2)}) async-start(), calls=%async_computation.12 | async-start | bytes 3276800 | tf_op jit(solution)/shard_map/all_gather | solution.py:267
  344.6 152.3 %all-gather.13.cloned.1.call-start = ((), (), s32[]{:S(2)}) async-start(), calls=%async_computation.11 | async-start | bytes 3276800 | tf_op jit(solution)/shard_map/all_gather | solution.py:268
  371.4 248.9 %all-gather.17.cloned.1.call-start = ((), (), s32[]{:S(2)}) async-start(), calls=%async_computation.13 | async-start | bytes 6553600 | tf_op jit(solution)/shard_map/all_gather | solution.py:55
  579.8 236.5 %reduce-scatter.12.cloned.1.call-start = ((), (), s32[]{:S(2)}) async-start(), calls=%async_computation.14 | async-start | bytes 13107200 | tf_op jit(solution)/shard_map/reduce_scatter | solution.py:68
  638.2 278.9 %all-gather.23.cloned.1.call-start = ((), (), s32[]{:S(2)}) async-start(), calls=%async_computation.18 | async-start | bytes 6553600 | tf_op jit(solution)/shard_map/all_gather | solution.py:51
  638.9 376.9 %all-gather.19.cloned.1.call-start = ((), (), s32[]{:S(2)}) async-start(), calls=%async_computation.15 | async-start | bytes 6553600 | tf_op jit(solution)/shard_map/all_gather | solution.py:51
  829.7 408.8 %reduce-scatter.16.cloned.1.call-start = ((), (), s32[]{:S(2)}) async-start(), calls=%async_computation.19 | async-start | bytes 39321600 | tf_op jit(solution)/shard_map/reduce_scatter | solution.py:59
  966.1 1304.7 %all-reduce.11.cloned.1.call-start = ((), (), s32[]{:S(2)}) async-start(), calls=%async_computation.28 | async-start | bytes 125829120
  1108.5 1372.9 %all-gather.25.cloned.1.call-start = ((), (), s32[]{:S(2)}) async-start(), calls=%async_computation.20 | async-start | bytes 39321600 | tf_op jit(solution)/shard_map/all_gather | solution.py:55
  2291.4 291.5 %all-gather.21.cloned.1.call-start = ((), (), s32[]{:S(2)}) async-start(), calls=%async_computation.16 | async-start | bytes 19660800 | tf_op jit(solution)/shard_map/all_gather | solution.py:55
  2292.0 471.5 %reduce-scatter.18.cloned.1.call-start = ((), (), s32[]{:S(2)}) async-start(), calls=%async_computation.21 | async-start | bytes 13107200 | tf_op jit(solution)/shard_map/reduce_scatter | solution.py:68
  2535.0 409.9 %reduce-scatter.14.cloned.1.call-start = ((), (), s32[]{:S(2)}) async-start(), calls=%async_computation.17 | async-start | bytes 13107200 | tf_op jit(solution)/shard_map/reduce_scatter | solution.py:68
  2614.6 330.3 %copy-start.33 = (bf16[1280,512]{1,0:T(8,128)(2,1)S(1)}, bf16[1280,512]{1,0:T(8,128)(2,1)}, u32[]{:S(2)}) copy-start(bf16[1280,512]{1,0:T(8,128)(2,1)} %param.38) | copy-start | bytes 3932164
  2614.6 435.0 %all-gather.27.cloned.1.call-start = ((), (), s32[]{:S(2)}) async-start(), calls=%async_computation.22 | async-start | bytes 6553600 | tf_op jit(solution)/shard_map/all_gather | solution.py:51
  2950.4 198.4 %reduce-scatter.20.cloned.1.call-start = ((), (), s32[]{:S(2)}) async-start(), calls=%async_computation.23 | async-start | bytes 13107200 | tf_op jit(solution)/shard_map/reduce_scatter | solution.py:59
  3064.9 427.6 %reduce-scatter.22.cloned.1.call-start = ((), (), s32[]{:S(2)}) async-start(), calls=%async_computation.24 | async-start | bytes 6553600 | tf_op jit(solution)/shard_map/reduce_scatter | solution.py:469
  3441.0 105.4 %reduce-scatter.24.cloned.1.call-start = ((), (), s32[]{:S(2)}) async-start(), calls=%async_computation.25 | async-start | bytes 6553600 | tf_op jit(solution)/shard_map/reduce_scatter | solution.py:470
  3446.3 173.7 %all-gather.29.cloned.1.call-start = ((), (), s32[]{:S(2)}) async-start(), calls=%async_computation.26 | async-start | bytes 13107200 | tf_op jit(solution)/shard_map/all_gather | solution.py:55
  3549.7 280.6 %reduce-scatter.26.cloned.1.call-start = ((), (), s32[]{:S(2)}) async-start(), calls=%async_computation.27 | async-start | bytes 13107200 | tf_op jit(solution)/shard_map/reduce_scatter | solution.py:68
  3652.1 256.1 %all-reduce.15.cloned.1.call-start = ((), (), s32[]{:S(2)}) async-start(), calls=%async_computation.30 | async-start | bytes 6291456 | tf_op jit(solution)/shard_map/psum | solution.py:494
  3728.8 284.2 %all-reduce.13.cloned.1.call-start = ((), (), s32[]{:S(2)}) async-start(), calls=%async_computation.29 | async-start | bytes 3670016 | tf_op jit(solution)/shard_map/psum | solution.py:490
  (128 other events, 4019.9 us)
Sparse Core Ops, SparseCore 0:
  21.6 98.3 all-gather.10
  172.2 151.4 reduce-scatter.9
  344.7 25.5 all-gather.14
  372.4 25.5 all-gather.12
  579.9 40.3 all-gather.16
  638.3 177.9 reduce-scatter.11
  818.0 99.0 all-gather.22
  919.3 96.4 all-gather.18
  1018.6 219.9 reduce-scatter.15
  1240.9 1029.8 all-reduce.10
  2291.5 189.8 all-gather.24
  2482.9 99.9 all-gather.20
  2585.4 177.9 reduce-scatter.17
  2765.8 179.0 reduce-scatter.13
  2950.5 99.0 all-gather.26
  3065.0 83.6 reduce-scatter.19
  3441.1 51.3 reduce-scatter.21
  3494.9 51.3 reduce-scatter.23
  3549.8 70.1 all-gather.28
  3652.2 177.9 reduce-scatter.25
  3836.0 72.2 all-reduce.14
  3913.9 98.9 all-reduce.12
where the time goes:
time: 4050 us; the launch traced here: 4040 us
  waiting for transfers between devices  2850 us (70%)
  matrix products  745 us (18%)
  other arithmetic  208 us (5%)
  local copies, waits for them, and re-layouts  186 us (5%)
    unnamed x23, waiting for transfers between devices  1030 us
    reduce_scatter x4, waiting for transfers between devices, column_totals(): lax.psum_scatter(term(jnp.int32(0), total // lax.axis_size('col') * lax.a...  579 us
    reduce_scatter x3, waiting for transfers between devices, row_totals(): lax.psum_scatter(term(jnp.int32(0), total // lax.axis_size('row') * lax.a...  359 us
    all_gather x4, waiting for transfers between devices, gather_rows(): return lax.all_gather(local, 'row', axis=0, tiled=True)  348 us
    all_gather x4, waiting for transfers between devices, gather_cols(): return lax.all_gather(local, 'col', axis=0, tiled=True)  304 us
    dot_general x8, matrix products, matrix_product(): return jnp.dot(left, right, preferred_element_type=jnp.float32)  114 us
    psum x1, waiting for transfers between devices, on_device(): lax.psum((in_qkv[0], in_qkv[1], in_qkv[2], in_ffn[0], in_ffn[1], out_o[0]...  105 us
    dot_general x11, matrix products, multiply_transposed(): lax.dot_general(left, right, (((1,), (1,)), ((), ())), preferred_element_...  103 us
  transfers between devices with their start and end apart: 22, of which 20 were waited for; matrix products, arithmetic and copies ran while one was open for 14% of the time, Pallas kernels for 0%

commit v1 on v0

v1 whole, which is shorter than its diff:
```python
import functools
import math

import jax
import jax.numpy as jnp
from jax import lax
from jax.experimental import pallas as pl
from jax.experimental.pallas import tpu as pltpu
from jax.sharding import PartitionSpec as P

MODEL_WIDTH = 2048
QUERY_HEADS = 16
KEY_VALUE_HEADS = 8
HEAD_SIZE = 128
ADAPTER_RANK = 16
TREE_LEN = 5120
TRUNK = 2048
SEG_LEN = 256
FFN_CHUNKS = 3

EPSILON = 1e-06
THETA = 1000000.0
ADAPTER_FACTOR = 2.0
BF = jnp.bfloat16
F32 = jnp.float32
SCALE = HEAD_SIZE ** (-0.5)
SCALE_LOG2 = SCALE * math.log2(math.e)
PLANE = ("col", "row")
LANES = 128
VMEM_LIMIT = 60 * 1024 * 1024


def dot(left, right):
    return jnp.dot(left, right, preferred_element_type=F32)


def dot_nt(left, right):
    return lax.dot_general(left, right, (((1,), (1,)), ((), ())), preferred_element_type=F32)


def dot_tn(left, right):
    return lax.dot_general(left, right, (((0,), (0,)), ((), ())), preferred_element_type=F32)


def attention_forward_kernel(parent_ref, q_ref, k_ref, v_ref, o_ref, l_ref, acc_ref):
    index = pl.program_id(0)
    trunk_blocks = TRUNK // SEG_LEN
    query = q_ref[...]
    acc_ref[...] = jnp.zeros_like(acc_ref)

    def step(start, size, causal=False):
        rows = pl.ds(start, size)
        scores = dot_nt(query, k_ref[rows, :])
        probs = jnp.exp2(scores * SCALE_LOG2)
        if causal:
            ahead = lax.broadcasted_iota(jnp.int32, probs.shape, 0)
            behind = lax.broadcasted_iota(jnp.int32, probs.shape, 1)
            probs = jnp.where(behind <= ahead, probs, 0.0)
        acc_ref[...] += dot(probs.astype(BF), v_ref[rows, :])

    @pl.when(index < trunk_blocks)
    def _():
        @pl.loop(0, index)
        def _(block):
            step(pl.multiple_of(block * SEG_LEN, SEG_LEN), SEG_LEN)

    @pl.when(index >= trunk_blocks)
    def _():
        size = 512
        for part in range(TRUNK // size):
            step(part * size, size)

        above = parent_ref[index]

        @pl.when(above >= 0)
        def _():
            step(pl.multiple_of(above * SEG_LEN, SEG_LEN), SEG_LEN)

    step(pl.multiple_of(index * SEG_LEN, SEG_LEN), SEG_LEN, True)
    total = acc_ref[:, HEAD_SIZE : HEAD_SIZE + 1]
    o_ref[...] = acc_ref[:, :HEAD_SIZE] / total
    spread = jnp.broadcast_to(total, (SEG_LEN, LANES))
    l_ref[0] = jnp.transpose(spread)[:8, :]


def attention_forward(parent_block, query, key, value):
    length = query.shape[0]
    blocks = length // SEG_LEN
    ones = (jnp.arange(HEAD_SIZE) == 0).astype(BF)
    widened = jnp.concatenate([value, jnp.broadcast_to(ones, value.shape)], axis=1)
    whole = lambda i, p: (0, 0)
    return pl.pallas_call(
        attention_forward_kernel,
        grid_spec=pltpu.PrefetchScalarGridSpec(
            num_scalar_prefetch=1,
            grid=(blocks,),
            in_specs=[
                pl.BlockSpec((SEG_LEN, HEAD_SIZE), lambda i, p: (i, 0)),
                pl.BlockSpec((length, HEAD_SIZE), whole),
                pl.BlockSpec((length, 2 * HEAD_SIZE), whole),
            ],
            out_specs=[
                pl.BlockSpec((SEG_LEN, HEAD_SIZE), lambda i, p: (i, 0)),
                pl.BlockSpec((1, 8, SEG_LEN), lambda i, p: (i, 0, 0)),
            ],
            scratch_shapes=[pltpu.VMEM((SEG_LEN, 2 * HEAD_SIZE), F32)],
        ),
        out_shape=[
            jax.ShapeDtypeStruct((length, HEAD_SIZE), F32),
            jax.ShapeDtypeStruct((blocks, 8, SEG_LEN), F32),
        ],
        compiler_params=pltpu.CompilerParams(vmem_limit_bytes=VMEM_LIMIT),
        cost_estimate=pl.CostEstimate(
            flops=160 * SEG_LEN * SEG_LEN * HEAD_SIZE * 4,
            bytes_accessed=length * HEAD_SIZE * 12,
            transcendentals=160 * SEG_LEN * SEG_LEN,
        ),
        name="attention_forward",
    )(parent_block, query, key, widened)


def attention_backward_kernel(
    parent_ref, q_ref, g_ref, o_ref, l_ref, k_ref, v_ref, kt_ref, dq_ref, dk_ref, dv_ref, acc_ref
):
    index = pl.program_id(0)
    trunk_blocks = TRUNK // SEG_LEN

    @pl.when(index == 0)
    def _():
        dk_ref[...] = jnp.zeros_like(dk_ref)
        dv_ref[...] = jnp.zeros_like(dv_ref)

    query = q_ref[...]
    grad = g_ref[...]
    delta = jnp.sum(grad.astype(F32) * o_ref[...], axis=1, keepdims=True)
    delta = jnp.transpose(jnp.broadcast_to(delta, (SEG_LEN, LANES)))[:1, :]
    inverse = 1.0 / l_ref[0, :1, :]
    acc_ref[...] = jnp.zeros_like(acc_ref)

    def step(start, size, causal=False):
        rows = pl.ds(start, size)
        probs = jnp.exp2(dot_nt(k_ref[rows, :], query) * SCALE_LOG2) * inverse
        if causal:
            behind = lax.broadcasted_iota(jnp.int32, probs.shape, 0)
            ahead = lax.broadcasted_iota(jnp.int32, probs.shape, 1)
            probs = jnp.where(behind <= ahead, probs, 0.0)
        dprobs = dot_nt(v_ref[rows, :], grad)
        dscores = (probs * (dprobs - delta)).astype(BF)
        dv_ref[rows, :] += dot(probs.astype(BF), grad)
        dk_ref[rows, :] += dot(dscores, query)
        acc_ref[...] += dot(kt_ref[:, rows], dscores)

    @pl.when(index < trunk_blocks)
    def _():
        @pl.loop(0, index)
        def _(block):
            step(pl.multiple_of(block * SEG_LEN, SEG_LEN), SEG_LEN)

    @pl.when(index >= trunk_blocks)
    def _():
        size = 512
        for part in range(TRUNK // size):
            step(part * size, size)

        above = parent_ref[index]

        @pl.when(above >= 0)
        def _():
            step(pl.multiple_of(above * SEG_LEN, SEG_LEN), SEG_LEN)

    step(pl.multiple_of(index * SEG_LEN, SEG_LEN), SEG_LEN, True)
    dq_ref[...] = jnp.transpose(acc_ref[...]) * SCALE


def attention_backward(parent_block, query, grad, attended, totals, key, value):
    length = query.shape[0]
    blocks = length // SEG_LEN
    whole = lambda i, p: (0, 0)
    part = lambda i, p: (i, 0)
    return pl.pallas_call(
        attention_backward_kernel,
        grid_spec=pltpu.PrefetchScalarGridSpec(
            num_scalar_prefetch=1,
            grid=(blocks,),
            in_specs=[
                pl.BlockSpec((SEG_LEN, HEAD_SIZE), part),
                pl.BlockSpec((SEG_LEN, HEAD_SIZE), part),
                pl.BlockSpec((SEG_LEN, HEAD_SIZE), part),
                pl.BlockSpec((1, 8, SEG_LEN), lambda i, p: (i, 0, 0)),
                pl.BlockSpec((length, HEAD_SIZE), whole),
                pl.BlockSpec((length, HEAD_SIZE), whole),
                pl.BlockSpec((HEAD_SIZE, length), whole),
            ],
            out_specs=[
                pl.BlockSpec((SEG_LEN, HEAD_SIZE), part),
                pl.BlockSpec((length, HEAD_SIZE), whole),
                pl.BlockSpec((length, HEAD_SIZE), whole),
            ],
            scratch_shapes=[pltpu.VMEM((HEAD_SIZE, SEG_LEN), F32)],
        ),
        out_shape=[jax.ShapeDtypeStruct((length, HEAD_SIZE), F32)] * 3,
        compiler_params=pltpu.CompilerParams(vmem_limit_bytes=VMEM_LIMIT),
        cost_estimate=pl.CostEstimate(
            flops=160 * SEG_LEN * SEG_LEN * HEAD_SIZE * 10,
            bytes_accessed=length * HEAD_SIZE * 24,
            transcendentals=160 * SEG_LEN * SEG_LEN,
        ),
        name="attention_backward",
    )(parent_block, query, grad, attended, totals, key, value, jnp.transpose(key))


def feed_forward_kernel(
    first,
    h_ref,
    c_ref,
    mg_ref,
    mu_ref,
    nd_ref,
    mgt_ref,
    mut_ref,
    ndt_ref,
    w_ref,
    bg_ref,
    bu_ref,
    ad_ref,
    *refs,
):
    if first:
        previous = None
        outs = refs
    else:
        previous = refs[:5]
        outs = refs[5:]
    accs = outs[:5]
    pa_ref, pg_ref, pu_ref = outs[5:8]
    out_acc, gh_acc, md_acc, ig_acc, iu_acc = scratch = outs[8:13]
    sems = outs[13]
    index = pl.program_id(0)
    width = w_ref.shape[-1]
    row_blocks = w_ref.shape[1]
    depth = MODEL_WIDTH // row_blocks
    pieces = depth // width

    @pl.when(index == 0)
    def _():
        if first:
            for ref in scratch:
                ref[...] = jnp.zeros_like(ref)
        else:
            copies = [
                pltpu.make_async_copy(previous[i], scratch[i], sems.at[i]) for i in range(5)
            ]
            for copy in copies:
                copy.start()
            for copy in copies:
                copy.wait()

    gate = dot_nt(mg_ref[...], bg_ref[0])
    upward = dot_nt(mu_ref[...], bu_ref[0])
    grad_act = dot_nt(nd_ref[...], ad_ref[0])
    for row in range(row_blocks):
        block = h_ref[:, row * depth : (row + 1) * depth]
        gate += dot(block, w_ref[0, row, :depth, :])
        upward += dot(block, w_ref[0, row, depth : 2 * depth, :])
        for piece in range(pieces):
            at = row * depth + piece * width
            down = w_ref[0, row, 2 * depth + piece * width : 2 * depth + (piece + 1) * width, :]
            grad_act += dot_nt(c_ref[:, at : at + width], down)
    sigma = 1.0 / (1.0 + jnp.exp(-gate))
    swish = gate * sigma
    act = (swish * upward).astype(BF)
    grad_gate = (grad_act * upward * (sigma * (1.0 + gate * (1.0 - sigma)))).astype(BF)
    grad_up = (grad_act * swish).astype(BF)
    for row in range(row_blocks):
        gh_acc[:, row * depth : (row + 1) * depth] += dot_nt(
            grad_gate, w_ref[0, row, :depth, :]
        ) + dot_nt(grad_up, w_ref[0, row, depth : 2 * depth, :])
        for piece in range(pieces):
            at = row * depth + piece * width
            down = w_ref[0, row, 2 * depth + piece * width : 2 * depth + (piece + 1) * width, :]
            out_acc[:, at : at + width] += dot(act, down)
    md_acc[...] += dot(act, ad_ref[0])
    ig_acc[...] += dot(grad_gate, bg_ref[0])
    iu_acc[...] += dot(grad_up, bu_ref[0])
    pa_ref[0] = dot(ndt_ref[...], act)
    pg_ref[0] = dot(mgt_ref[...], grad_gate)
    pu_ref[0] = dot(mut_ref[...], grad_up)

    @pl.when(index == pl.num_programs(0) - 1)
    def _():
        copies = [pltpu.make_async_copy(scratch[i], accs[i], sems.at[i]) for i in range(5)]
        for copy in copies:
            copy.start()
        for copy in copies:
            copy.wait()


def feed_forward_chunk(hidden, cotangent, masks, weights, maps, previous):
    first = previous is None
    rows = hidden.shape[0]
    cols, row_blocks, tall, width = weights.shape
    whole = lambda i: (0, 0)
    step = lambda i: (i, 0, 0)
    mask_rows = masks[3].shape[0]
    acc_shapes = [(rows, MODEL_WIDTH)] * 2 + [(rows, LANES)] * 3
    in_specs = (
        [pl.BlockSpec((rows, MODEL_WIDTH), whole)] * 2
        + [pl.BlockSpec((rows, LANES), whole)] * 3
        + [pl.BlockSpec((mask_rows, rows), whole)] * 3
        + [pl.BlockSpec((1, row_blocks, tall, width), lambda i: (i, 0, 0, 0))]
        + [pl.BlockSpec((1, width, LANES), step)] * 3
    )
    operands = [hidden, cotangent, *masks, weights, *maps]
    aliases = {}
    if not first:
        aliases = {len(operands) + i: i for i in range(5)}
        in_specs = in_specs + [pl.BlockSpec(memory_space=pl.ANY)] * 5
        operands = operands + list(previous)
    outs = pl.pallas_call(
        functools.partial(feed_forward_kernel, first),
        grid=(cols,),
        in_specs=in_specs,
        out_specs=[pl.BlockSpec(memory_space=pl.ANY)] * 5
        + [pl.BlockSpec((1, mask_rows, width), step)] * 3,
        out_shape=[jax.ShapeDtypeStruct(s, F32) for s in acc_shapes]
        + [jax.ShapeDtypeStruct((cols, mask_rows, width), F32)] * 3,
        scratch_shapes=[pltpu.VMEM(s, F32) for s in acc_shapes]
        + [pltpu.SemaphoreType.DMA((5,))],
        input_output_aliases=aliases,
        compiler_params=pltpu.CompilerParams(vmem_limit_bytes=VMEM_LIMIT),
        cost_estimate=pl.CostEstimate(
            flops=12 * rows * MODEL_WIDTH * cols * width,
            bytes_accessed=cols * row_blocks * tall * width * 2,
            transcendentals=rows * cols * width,
        ),
        name="feed_forward",
    )(*operands)
    return outs[:5], outs[5:]


def rotate(values, positions):
    half = HEAD_SIZE // 2
    freqs = THETA ** (-2.0 * jnp.arange(half).astype(F32) / HEAD_SIZE)
    angle = positions[:, None, None] * freqs[None, None, :]
    cosine = jnp.cos(angle)
    sine = jnp.sin(angle)
    first = values[..., :half]
    second = values[..., half:]
    return jnp.concatenate(
        [first * cosine - second * sine, second * cosine + first * sine], axis=-1
    )


def head_shape(gain, positions):
    def shaped(lines):
        normed = lines * lax.rsqrt(jnp.mean(lines * lines, axis=-1, keepdims=True) + EPSILON) * gain
        return rotate(normed, positions)

    return shaped


def norm_back(values, scale, gain, gradient):
    weighted = gain * gradient
    inner_sum = jnp.sum(weighted * values, axis=1, keepdims=True)
    return scale * weighted - values * scale**3 * inner_sum / MODEL_WIDTH


def lane_pad(values):
    return jnp.pad(values, ((0, 0),) * (values.ndim - 1) + ((0, LANES - values.shape[-1]),))


def place(own, own_at, other, other_at, columns):
    index = jnp.arange(columns)[None, :] // ADAPTER_RANK
    copies = columns // ADAPTER_RANK
    return jnp.where(index == own_at, jnp.tile(own, (1, copies)), 0.0) + jnp.where(
        index == other_at, jnp.tile(other, (1, copies)), 0.0
    )


def on_device(
    tokens,
    cotangent,
    attention_norm_gain,
    feedfwd_norm_gain,
    query_norm_gain,
    key_norm_gain,
    query_matrix,
    key_matrix,
    value_matrix,
    output_matrix,
    gate_matrix,
    up_matrix,
    down_matrix,
    query_adapter_inmaps,
    query_adapter_outmaps,
    key_adapter_inmaps,
    key_adapter_outmaps,
    value_adapter_inmaps,
    value_adapter_outmaps,
    output_adapter_inmaps,
    output_adapter_outmaps,
    gate_adapter_inmaps,
    gate_adapter_outmaps,
    up_adapter_inmaps,
    up_adapter_outmaps,
    down_adapter_inmaps,
    down_adapter_outmaps,
    segment,
    depth,
    parent,
    adapter,
):
    rows = lax.axis_size("row")
    cols = lax.axis_size("col")
    devices = rows * cols
    repeat = devices // QUERY_HEADS
    plane = lax.axis_index("dp")
    row = lax.axis_index("row")
    col = lax.axis_index("col")
    length = segment.shape[0]
    own = tokens.shape[0] // rows
    columns = query_adapter_inmaps.shape[1]
    rank = ADAPTER_RANK
    swap = [(0, 1), (1, 0)]
    pairs = [(r, r ^ repeat) for r in range(rows)]

    own_adapter = adapter[0]
    other_adapter = lax.ppermute(adapter, "dp", swap)[0]

    def inmap(table, at):
        return lax.dynamic_slice_in_dim(table, at * rank, rank, 1)

    def outmap(table, at):
        return jnp.transpose(lax.dynamic_slice_in_dim(table, at * rank, rank, 0))

    both = (own_adapter, other_adapter)
    ffn_half = gate_matrix.shape[1] // 2
    half_start = plane * ffn_half

    def half_of(table):
        return lax.dynamic_slice_in_dim(table, half_start, ffn_half, 0)

    row_pack = jnp.concatenate(
        [
            inmap(query_adapter_inmaps, own_adapter),
            inmap(key_adapter_inmaps, own_adapter),
            inmap(value_adapter_inmaps, own_adapter),
            *[inmap(gate_adapter_inmaps, a) for a in both],
            *[inmap(up_adapter_inmaps, a) for a in both],
            *[outmap(down_adapter_outmaps, a) for a in both],
            outmap(output_adapter_outmaps, own_adapter),
        ],
        axis=1,
    )
    col_attn = jnp.concatenate(
        [
            inmap(output_adapter_inmaps, own_adapter),
            outmap(query_adapter_outmaps, own_adapter),
            jnp.concatenate(
                [
                    outmap(key_adapter_outmaps, own_adapter),
                    outmap(value_adapter_outmaps, own_adapter),
                ],
                axis=0,
            ),
        ],
        axis=1,
    )
    col_ffn = half_of(
        jnp.concatenate(
            [
                *[inmap(down_adapter_inmaps, a) for a in both],
                *[outmap(gate_adapter_outmaps, a) for a in both],
                *[outmap(up_adapter_outmaps, a) for a in both],
            ],
            axis=1,
        )
    )
    attn_rows = col_attn.shape[0]
    col_pack = jnp.concatenate(
        [jnp.pad(col_attn, ((0, 0), (0, col_ffn.shape[1] - col_attn.shape[1]))), col_ffn], axis=0
    )
    row_maps = lax.all_gather(row_pack, "row", axis=0, tiled=True)
    col_maps = lax.all_gather(col_pack, "col", axis=0, tiled=False)
    in_qkv = row_maps[:, : 3 * rank]
    in_gu = row_maps[:, 3 * rank : 7 * rank]
    out_down = row_maps[:, 7 * rank : 9 * rank]
    out_o = row_maps[:, 9 * rank : 10 * rank]
    col_attn = col_maps[:, :attn_rows]
    col_ffn = col_maps[:, attn_rows:]
    in_o = col_attn[:, :, :rank].reshape(-1, rank)
    out_q = col_attn[:, :, rank : 2 * rank].reshape(-1, rank)
    kv_local = key_matrix.shape[1]
    out_k = col_attn[:, :kv_local, 2 * rank : 3 * rank].reshape(-1, rank)
    out_v = col_attn[:, kv_local:, 2 * rank : 3 * rank].reshape(-1, rank)

    qkv_local = jnp.concatenate([query_matrix, key_matrix, value_matrix], axis=1)
    weights_qkv = lax.all_gather(qkv_local, PLANE, axis=0, tiled=True).reshape(
        cols, MODEL_WIDTH, -1
    )
    weights_o = lax.all_gather(output_matrix, ("row", "col"), axis=0, tiled=True).reshape(
        rows, QUERY_HEADS * HEAD_SIZE, -1
    )
    q_local = query_matrix.shape[1]
    width = ffn_half // FFN_CHUNKS
    depth_rows = gate_matrix.shape[0]
    ffn_weights = []
    for chunk in range(FFN_CHUNKS):
        start = half_start + chunk * width
        down = lax.dynamic_slice_in_dim(down_matrix, start, width, 0)
        pack = jnp.concatenate(
            [
                lax.dynamic_slice_in_dim(gate_matrix, start, width, 1),
                lax.dynamic_slice_in_dim(up_matrix, start, width, 1),
                *[
                    down[:, piece * width : (piece + 1) * width]
                    for piece in range(depth_rows // width)
                ],
            ],
            axis=0,
        )
        ffn_weights.append(
            lax.all_gather(pack, PLANE, axis=0, tiled=True).reshape(cols, rows, -1, width)
        )

    own_tokens = lax.all_to_all(tokens, "row", 0, 1, tiled=True)
    own_cotangent = lax.all_to_all(cotangent, "row", 0, 1, tiled=True)
    other_cotangent = lax.ppermute(own_cotangent, "dp", swap)
    gain_pair = lax.all_gather(
        jnp.stack([attention_norm_gain, feedfwd_norm_gain], axis=1), "row", axis=0, tiled=True
    )
    gain_one = gain_pair[:, 0]
    gain_two = gain_pair[:, 1]
    resid = own_tokens.astype(F32)
    scale_one = lax.rsqrt(jnp.mean(resid * resid, axis=1, keepdims=True) + EPSILON)
    hidden = (resid * scale_one * gain_one).astype(BF)

    masked_qkv = dot(hidden, in_qkv).astype(BF)
    projected = [dot(hidden, weights_qkv[c]) for c in range(cols)]
    query_pre = jnp.concatenate([p[:, :q_local] for p in projected], axis=1)
    key_pre = jnp.concatenate([p[:, q_local : q_local + kv_local] for p in projected], axis=1)
    value_pre = jnp.concatenate([p[:, q_local + kv_local :] for p in projected], axis=1)
    query_pre = query_pre + ADAPTER_FACTOR * dot_nt(masked_qkv[:, :rank], out_q)
    key_pre = key_pre + ADAPTER_FACTOR * dot_nt(masked_qkv[:, rank : 2 * rank], out_k)
    value_pre = value_pre + ADAPTER_FACTOR * dot_nt(masked_qkv[:, 2 * rank :], out_v)
    token_start = (col * rows + row) * own
    positions = lax.dynamic_slice_in_dim(depth, token_start, own, 0).astype(F32)
    query, query_back = jax.vjp(
        head_shape(query_norm_gain, positions), query_pre.reshape(own, QUERY_HEADS, HEAD_SIZE)
    )
    key, key_back = jax.vjp(
        head_shape(key_norm_gain, positions), key_pre.reshape(own, KEY_VALUE_HEADS, HEAD_SIZE)
    )
    value = value_pre.reshape(own, KEY_VALUE_HEADS, HEAD_SIZE)
    key_value = jnp.stack([key.astype(BF), value.astype(BF)], axis=2).reshape(
        own, QUERY_HEADS, HEAD_SIZE
    )

    def to_heads(lines):
        sent = jnp.transpose(lines, (1, 0, 2))
        if repeat > 1:
            sent = jnp.repeat(sent, repeat, axis=0)
        return lax.all_to_all(sent, PLANE, 0, 0, tiled=True).reshape(length, lines.shape[2])

    def to_tokens(lines):
        got = lax.all_to_all(
            lines.reshape(devices, own, lines.shape[1]), PLANE, 0, 0, tiled=True
        )
        if repeat > 1:
            got = got[::repeat]
        return jnp.transpose(got, (1, 0, 2))

    got = to_heads(jnp.concatenate([query.astype(BF), key_value], axis=2))
    head_query = got[:, :HEAD_SIZE]
    mine = got[:, HEAD_SIZE:]
    theirs = lax.ppermute(mine, "row", pairs)
    has_key = (row // repeat) % 2 == 0
    head_key = jnp.where(has_key, mine, theirs)
    head_value = jnp.where(has_key, theirs, mine)

    block_node = segment.reshape(-1, SEG_LEN)[:, 0]
    nodes = jnp.arange(parent.shape[1])
    node_parent = jnp.sum(jnp.where(block_node[:, None] == nodes, parent.reshape(1, -1), 0), axis=1)
    block_index = jnp.arange(block_node.shape[0])
    parent_block = jnp.max(
        jnp.where(node_parent[:, None] == block_node[None, :], block_index[None, :], 0), axis=1
    )
    parent_block = jnp.where(node_parent > 0, parent_block, -1).astype(jnp.int32)
    head_attended, totals = attention_forward(parent_block, head_query, head_key, head_value)
    attended = to_tokens(head_attended.astype(BF)).reshape(own, -1)

    masked_o = dot(attended, in_o).astype(BF)
    branch = jnp.concatenate([dot(attended, weights_o[r]) for r in range(rows)], axis=1)
    middle = resid + branch + ADAPTER_FACTOR * dot_nt(masked_o, out_o)
    scale_two = lax.rsqrt(jnp.mean(middle * middle, axis=1, keepdims=True) + EPSILON)
    hidden_ffn = (middle * scale_two * gain_two).astype(BF)

    other_ffn = lax.ppermute(hidden_ffn, "dp", swap)
    hidden_both = jnp.concatenate([hidden_ffn, other_ffn], axis=0)
    cot_both = jnp.concatenate([own_cotangent, other_cotangent], axis=0)
    tree_mask = (
        jnp.arange(2 * own)[:, None] // own == (jnp.arange(2 * rank)[None, :] // rank)
    ).astype(F32)
    masked_gu = dot(hidden_both, in_gu) * jnp.tile(tree_mask, (1, 2))
    masked_g = masked_gu[:, : 2 * rank].astype(BF)
    masked_u = masked_gu[:, 2 * rank :].astype(BF)
    inner_d = (ADAPTER_FACTOR * dot(cot_both, out_down) * tree_mask).astype(BF)
    masks = [
        lane_pad((ADAPTER_FACTOR * masked_g.astype(F32)).astype(BF)),
        lane_pad((ADAPTER_FACTOR * masked_u.astype(F32)).astype(BF)),
        lane_pad(inner_d),
        jnp.transpose(masked_g),
        jnp.transpose(masked_u),
        jnp.transpose(inner_d),
    ]
    accs = None
    parts = []
    for chunk in range(FFN_CHUNKS):
        maps = [
            lane_pad(
                col_ffn[
                    :, chunk * width : (chunk + 1) * width, 2 * rank * kind : 2 * rank * (kind + 1)
                ]
            )
            for kind in (1, 2, 0)
        ]
        accs, part = feed_forward_chunk(
            hidden_both, cot_both, masks, ffn_weights[chunk], maps, accs
        )
        parts.append(part)
    out_acc, gh_acc, md_acc, ig_acc, iu_acc = accs
    masked_down = (md_acc[:, : 2 * rank] * tree_mask).astype(BF)
    inner_gu = (
        ADAPTER_FACTOR
        * jnp.concatenate([ig_acc[:, : 2 * rank], iu_acc[:, : 2 * rank]], axis=1)
        * jnp.tile(tree_mask, (1, 2))
    ).astype(BF)
    gh_acc = gh_acc + dot_nt(inner_gu, in_gu)
    out_acc = out_acc + ADAPTER_FACTOR * dot_nt(masked_down, out_down)
    gh_other = lax.ppermute(gh_acc[own:].astype(BF), "dp", swap)
    out_other = lax.ppermute(out_acc[own:].astype(BF), "dp", swap)
    output = (middle + out_acc[:own] + out_other.astype(F32)).astype(BF)
    output = lax.all_to_all(output, "row", 1, 0, tiled=True)
    grad_hidden_ffn = gh_acc[:own] + gh_other.astype(F32)
    grad_middle = own_cotangent.astype(F32) + norm_back(middle, scale_two, gain_two, grad_hidden_ffn)
    grad_middle_low = grad_middle.astype(BF)

    inner_o = (ADAPTER_FACTOR * dot(grad_middle_low, out_o)).astype(BF)
    o_local = weights_o.shape[2]
    grad_attended = dot_nt(inner_o, in_o)
    for r in range(rows):
        grad_attended = grad_attended + dot_nt(
            grad_middle_low[:, r * o_local : (r + 1) * o_local], weights_o[r]
        )
    grad_low = grad_attended.astype(BF).reshape(own, QUERY_HEADS, HEAD_SIZE)
    head_grad = to_heads(grad_low)

    dq, dk, dv = attention_backward(
        parent_block, head_query, head_grad, head_attended, totals, head_key, head_value
    )
    dk = dk * SCALE
    kept = jnp.where(has_key, dk, dv)
    given = jnp.where(has_key, dv, dk)
    kept = kept + lax.ppermute(given, "row", pairs)
    returned = to_tokens(jnp.concatenate([dq.astype(BF), kept.astype(BF)], axis=1))
    grad_kv = returned[:, :, HEAD_SIZE:].reshape(own, KEY_VALUE_HEADS, 2, HEAD_SIZE)
    grad_q = query_back(returned[:, :, :HEAD_SIZE].astype(F32))[0].astype(BF).reshape(own, -1)
    grad_k = key_back(grad_kv[:, :, 0].astype(F32))[0].astype(BF).reshape(own, -1)
    grad_v = grad_kv[:, :, 1].reshape(own, -1)

    inner_qkv = (
        ADAPTER_FACTOR
        * jnp.concatenate([dot(grad_q, out_q), dot(grad_k, out_k), dot(grad_v, out_v)], axis=1)
    ).astype(BF)
    grad_hidden = dot_nt(inner_qkv, in_qkv)
    for c in range(cols):
        grad_c = jnp.concatenate(
            [
                grad_q[:, c * q_local : (c + 1) * q_local],
                grad_k[:, c * kv_local : (c + 1) * kv_local],
                grad_v[:, c * kv_local : (c + 1) * kv_local],
            ],
            axis=1,
        )
        grad_hidden = grad_hidden + dot_nt(grad_c, weights_qkv[c])
    input_gradient = grad_middle + norm_back(resid, scale_one, gain_one, grad_hidden)
    input_gradient = lax.all_to_all(input_gradient.astype(BF), "row", 1, 0, tiled=True).astype(F32)

    def over_rows(values):
        mine = lax.psum_scatter(values, "row", scatter_dimension=0, tiled=True)
        return lax.psum(mine, "col")

    def over_cols(values):
        mine = lax.psum_scatter(values, "col", scatter_dimension=0, tiled=True)
        return lax.psum(mine, "row")

    f = ADAPTER_FACTOR
    row_mid = over_rows(
        jnp.concatenate(
            [
                dot_tn(hidden_both, inner_gu),
                f * dot_tn(cot_both, masked_down),
                f * dot_tn(grad_middle_low, masked_o),
            ],
            axis=1,
        )
    )
    ffn_parts = jnp.concatenate(
        [jnp.concatenate([part[kind] for part in parts], axis=2) for kind in range(3)], axis=1
    )
    o_parts = dot_tn(attended, inner_o).reshape(cols, -1)
    col_mid = over_cols(
        jnp.concatenate([ffn_parts.reshape(cols, -1), o_parts], axis=1)
    ).reshape(-1)
    row_end = over_rows(dot_tn(hidden, inner_qkv))
    end_parts = [
        (f * dot_tn(grad, masked_qkv[:, i * rank : (i + 1) * rank])).reshape(cols, -1)
        for i, grad in enumerate((grad_q, grad_k, grad_v))
    ]
    col_end = over_cols(jnp.concatenate(end_parts, axis=1)).reshape(-1)
    row_all = jnp.concatenate([row_mid, row_end], axis=1)
    row_got = lax.ppermute(row_all, "dp", swap)
    col_all = jnp.concatenate([col_mid, col_end])
    col_got = lax.ppermute(col_all, "dp", swap)

    def placed(first, second):
        return place(first, own_adapter, second, other_adapter, columns)

    def row_sum(at):
        first = row_all[:, at : at + rank] + row_got[:, at + rank : at + 2 * rank]
        second = row_all[:, at + rank : at + 2 * rank] + row_got[:, at : at + rank]
        return placed(first, second)

    def row_own(at):
        return placed(row_all[:, at : at + rank], row_got[:, at : at + rank])

    grad_a_gate = row_sum(0)
    grad_a_up = row_sum(2 * rank)
    grad_b_down = row_sum(4 * rank).T
    grad_b_o = row_own(6 * rank).T
    grad_a_q, grad_a_k, grad_a_v = (row_own((7 + i) * rank) for i in range(3))

    block = 6 * rank * ffn_half
    here = col_all[:block].reshape(3, 2 * rank, ffn_half)
    there = col_got[:block].reshape(3, 2 * rank, ffn_half)
    there = jnp.concatenate([there[:, rank:], there[:, :rank]], axis=1)
    low_half = jnp.where(plane == 0, here, there)
    high_half = jnp.where(plane == 0, there, here)
    ffn_full = jnp.concatenate([low_half, high_half], axis=2)

    def ffn_placed(kind, factor):
        full = factor * ffn_full[kind]
        return placed(full[:rank].T, full[rank:].T)

    grad_a_down = ffn_placed(0, 1.0)
    grad_b_gate = ffn_placed(1, f).T
    grad_b_up = ffn_placed(2, f).T

    def col_own(at, count):
        first = col_all[at : at + count * rank].reshape(count, rank)
        second = col_got[at : at + count * rank].reshape(count, rank)
        return placed(first, second)

    o_rows = output_matrix.shape[0]
    grad_a_o = col_own(block, o_rows)
    block = block + o_rows * rank
    grad_b_q = col_own(block, q_local).T
    block = block + q_local * rank
    grad_b_k = col_own(block, kv_local).T
    block = block + kv_local * rank
    grad_b_v = col_own(block, kv_local).T

    return (
        output,
        input_gradient,
        grad_a_q,
        grad_b_q,
        grad_a_k,
        grad_b_k,
        grad_a_v,
        grad_b_v,
        grad_a_o,
        grad_b_o,
        grad_a_gate,
        grad_b_gate,
        grad_a_up,
        grad_b_up,
        grad_a_down,
        grad_b_down,
    )


def solution(mesh):
    return jax.shard_map(
        on_device,
        mesh=mesh,
        in_specs=(
            P(("dp", "col"), "row"),
            P(("dp", "col"), "row"),
            P("row"),
            P("row"),
            P(),
            P(),
            P("row", "col"),
            P("row", "col"),
            P("row", "col"),
            P("col", "row"),
            P("row", "col"),
            P("row", "col"),
            P("col", "row"),
            P("row", None),
            P(None, "col"),
            P("row", None),
            P(None, "col"),
            P("row", None),
            P(None, "col"),
            P("col", None),
            P(None, "row"),
            P("row", None),
            P(None, "col"),
            P("row", None),
            P(None, "col"),
            P("col", None),
            P(None, "row"),
            P("dp"),
            P("dp"),
            P("dp", None),
            P("dp"),
        ),
        out_specs=(
            P(("dp", "col"), "row"),
            P(("dp", "col"), "row"),
            P("row", None),
            P(None, "col"),
            P("row", None),
            P(None, "col"),
            P("row", None),
            P(None, "col"),
            P("col", None),
            P(None, "row"),
            P("row", None),
            P(None, "col"),
            P("row", None),
            P(None, "col"),
            P("col", None),
            P(None, "row"),
        ),
        check_vma=False,
    )
```

time: 4050 us -> 1130 us (0.28)
  waiting for transfers between devices: 2850 us -> 407 us
  matrix products: 745 us -> 77.9 us
  Pallas kernels: 0 us -> 196 us
  blocking collectives: 29.4 us -> 169 us
  other arithmetic: 208 us -> 74.6 us
  local copies, waits for them, and re-layouts: 186 us -> 132 us
  starting transfers between devices: 1.08 us -> 47.4 us
    unnamed x23 -> x9, waiting for transfers between devices: 1030 us -> 0.83 us
    reduce_scatter x9 -> x2, waiting for transfers between devices: 992 us -> 6.61 us  [over_rows(): mine = lax.psum_scatter(values, 'row', scatter_dimension=0, tiled=True)]
    dot_general x69 -> x40, matrix products: 745 us -> 77.9 us  [the longest x16 39.5 us: dot_nt(): lax.dot_general(left, right, (((1,), (1,)), ((), ())), preferred_element_...]
    all_gather x10 -> x5, waiting for transfers between devices: 652 us -> 113 us  [the longest x3 84.2 us: on_device(): lax.all_gather(pack, PLANE, axis=0, tiled=True)]
    pallas_call x0 -> x5, Pallas kernels: none -> 196 us  [the longest x3 110 us: feed_forward_chunk(): pl.pallas_call(functools.partial(feed_forward_kernel, first), grid=(cols,...]
    all_to_all x0 -> x7, waiting for transfers between devices: none -> 130 us  [the longest x2 89.3 us: to_tokens(): lax.all_to_all(lines.reshape(devices, own, lines.shape[1]), PLANE, 0, 0,...]
    all_to_all x0 -> x1, blocking collectives: none -> 91.6 us  [to_heads(): lax.all_to_all(sent, PLANE, 0, 0, tiled=True)]
    psum x2, waiting for transfers between devices: 169 us -> 84.4 us  [the longest x1 54.3 us: over_rows(): return lax.psum(mine, 'col')]
  transfers between devices with their start and end apart: 22 -> 25, of which waited for: 20 -> 14; matrix products, arithmetic and copies ran while one was open for 14% -> 20% of each run, Pallas kernels for 0% -> 10%
where the time goes in v1:
time: 1130 us; the launch traced here: 1120 us
  waiting for transfers between devices  407 us (36%)
  Pallas kernels  196 us (17%)
  blocking collectives  169 us (15%)
  local copies, waits for them, and re-layouts  132 us (12%)
  matrix products  77.9 us (7%)
  other arithmetic  74.6 us (7%)
  starting transfers between devices  47.4 us (4%)
  between operations  17.5 us (2%)
    pallas_call x3, Pallas kernels, feed_forward_chunk(): pl.pallas_call(functools.partial(feed_forward_kernel, first), grid=(cols,...  110 us
    all_to_all x1, blocking collectives, to_heads(): lax.all_to_all(sent, PLANE, 0, 0, tiled=True)  91.6 us
    all_to_all x2, waiting for transfers between devices, to_tokens(): lax.all_to_all(lines.reshape(devices, own, lines.shape[1]), PLANE, 0, 0,...  89.3 us
    all_gather x3, waiting for transfers between devices, on_device(): lax.all_gather(pack, PLANE, axis=0, tiled=True)  84.2 us
    psum x1, waiting for transfers between devices, over_rows(): return lax.psum(mine, 'col')  54.3 us
    pallas_call x1, Pallas kernels, attention_backward(): pl.pallas_call(attention_backward_kernel, grid_spec=pltpu.PrefetchScalarG...  51.1 us
    unnamed x265, local copies, waits for them, and re-layouts  49.2 us
    all_gather x1, blocking collectives, on_device(): col_maps = lax.all_gather(col_pack, 'col', axis=0, tiled=False)  41.1 us
  transfers between devices with their start and end apart: 25, of which 14 were waited for; matrix products, arithmetic and copies ran while one was open for 20% of the time, Pallas kernels for 10%

profile of v1, /device:TPU:0, one launch (start us, length us, event | category | flops | bytes accessed | tf_op | source)
XLA Modules:
  0.0 1121.6 jit_solution(17002529105740700185)
XLA Ops:
  25.3 24.7 %all_gather.27 = f32[2048,2]{0,1:T(2,128)S(1)} all-gather(f32[512,2]{0,1:T(2,128)S(1)} %pad_maximum_fusion.15), channel_id=1, replica_groups=mesh['dp'=2,'row'=4,'col'=4] {'row'}, dimensions={0}, use_global_device_ids=true | all-gather | bytes 20480 | tf_op jit(solution)/shard_map/all_gather | solution.py:529
  59.8 41.1 %all-gather = bf16[5120,96]{1,0:T(8,128)(2,1)S(1)} all-gather(bf16[1280,96]{1,0:T(8,128)(2,1)S(1)} %fusion.100), channel_id=2, replica_groups=mesh['dp'=2,'row'=4,'col'=4] {'col'}, dimensions={0}, use_global_device_ids=true | all-gather | bytes 1228800 | tf_op jit(solution)/shard_map/all_gather | solution.py:484
  108.9 11.6 %all_gather.29 = bf16[2048,160]{0,1:T(8,128)(2,1)S(1)} all-gather(bf16[512,160]{0,1:T(8,128)(2,1)} %constant_dynamic-update-slice_fusion), channel_id=1, replica_groups=mesh['dp'=2,'row'=4,'col'=4] {'row'}, dimensions={0}, use_global_device_ids=true | all-gather | bytes 819200 | tf_op jit(solution)/shard_map/all_gather | solution.py:483
  127.6 29.1 %all-gather.7.cloned.1.call-done = bf16[8192,1024]{1,0:T(8,128)(2,1)} async-done(((bf16[512,1024]{1,0:T(8,128)(2,1)}), bf16[8192,1024]{1,0:T(8,128)(2,1)}) %all-gather.7.cloned.1.call-update) | async-done | bytes 16777232 | tf_op jit(solution)/shard_map/all_gather | solution.py:498
  190.5 91.6 %all_to_all.84 = bf16[16,320,256]{2,1,0:T(8,128)(2,1)S(1)} all-to-all(bf16[16,320,256]{2,1,0:T(8,128)(2,1)S(1)} %maximum_bitcast_fusion), channel_id=1, replica_groups=mesh['dp'=2,'row'=4,'col'=4] {'col','row'}, dimensions={0} | all-to-all | bytes 5242880 | tf_op jit(solution)/shard_map/all_to_all | solution.py:563
  304.6 35.1 %attention_forward.1 = (f32[5120,128]{1,0:T(8,128)}, f32[20,8,256]{2,1,0:T(8,128)}) custom-call(s32[20]{0:T(128)} %compare_select_fusion.2.parent_ref, bf16[5120,128]{1,0:T(8,128)(2,1)} %get-tuple-element.206.q_ref, bf16[5120,128]{1,0:T(8,128)(2,1)} %copy.520.k_ref, bf16[5120,256]{1,0:T(8,128)(2,1)} %copy.521.v_ref), custom_call_target="tpu_custom_call" | custom-call | flops 5368709120 | bytes 7864320 | tf_op jit(solution)/shard_map/attention_forward/pallas_call | solution.py:92
  352.3 41.7 %all-to-all-done.2 = bf16[16,320,128]{2,1,0:T(8,128)(2,1)} async-done(((bf16[16,320,128]{2,1,0:T(8,128)(2,1)}), bf16[16,320,128]{2,1,0:T(8,128)(2,1)}, u32[]{:S(2)}, u32[]{:S(2)}) %all-to-all-start.2) | async-done | bytes 1310752 | tf_op jit(solution)/shard_map/all_to_all | solution.py:566
  424.3 15.5 %collective-permute-done.2 = bf16[320,2048]{1,0:T(8,128)(2,1)} collective-permute-done((bf16[320,2048]{1,0:T(8,128)(2,1)}, bf16[320,2048]{1,0:T(8,128)(2,1)}, u32[]{:S(2)}, u32[]{:S(2)}) %collective-permute-start.2) | collective-permute-done | bytes 1310752 | tf_op jit(solution)/shard_map/ppermute | solution.py:598
  446.0 34.4 %feed_forward.3 = (f32[640,2048]{1,0:T(8,128)}, f32[640,2048]{1,0:T(8,128)}, f32[640,128]{1,0:T(8,128)}, f32[640,128]{1,0:T(8,128)}, f32[640,128]{1,0:T(8,128)},...) custom-call(bf16[640,2048]{1,0:T(8,128)(2,1)} %copy-done.12, bf16[640,2048]{1,0:T(8,128)(2,1)} %copy-done.19, ...), custom_call_target="tpu_custom_call" | custom-call | flops 16106127360 | bytes 12582912 | tf_op jit(solution)/shard_map/feed_forward/pallas_call | solution.py:319
  480.4 20.4 %all-gather.13.cloned.1.call-done = bf16[24576,256]{1,0:T(8,128)(2,1)} async-done(((bf16[1536,256]{1,0:T(8,128)(2,1)}), bf16[24576,256]{1,0:T(8,128)(2,1)}) %all-gather.13.cloned.1.call-update) | async-done | bytes 12582928 | tf_op jit(solution)/shard_map/all_gather | solution.py:523
  500.8 37.8 %feed_forward.4 = (f32[640,2048]{1,0:T(8,128)}, f32[640,2048]{1,0:T(8,128)}, f32[640,128]{1,0:T(8,128)}, f32[640,128]{1,0:T(8,128)}, f32[640,128]{1,0:T(8,128)},...) custom-call(bf16[640,2048]{1,0:T(8,128)(2,1)} %copy-done.12, ...), custom_call_target="tpu_custom_call", output_to_operand_aliasing={{0}: (12, {}), {1}: (13, {}), {2}: (14, {}), {3}: (15, {}),... | custom-call | flops 16106127360 | bytes 12582912 | tf_op jit(solution)/shard_map/feed_forward/pallas_call | solution.py:319
  538.6 63.8 %all-gather.11.cloned.1.call-done = bf16[24576,256]{1,0:T(8,128)(2,1)} async-done(((bf16[1536,256]{1,0:T(8,128)(2,1)}), bf16[24576,256]{1,0:T(8,128)(2,1)}) %all-gather.11.cloned.1.call-update) | async-done | bytes 12582928 | tf_op jit(solution)/shard_map/all_gather | solution.py:523
  602.5 38.0 %feed_forward.5 = (f32[640,2048]{1,0:T(8,128)}, f32[640,2048]{1,0:T(8,128)}, f32[640,128]{1,0:T(8,128)}, f32[640,128]{1,0:T(8,128)}, f32[640,128]{1,0:T(8,128)},...) custom-call(bf16[640,2048]{1,0:T(8,128)(2,1)} %copy-done.12, ...), custom_call_target="tpu_custom_call", output_to_operand_aliasing={{0}: (12, {}), {1}: (13, {}), {2}: (14, {}), {3}: (15, {}),... | custom-call | flops 16106127360 | bytes 12582912 | tf_op jit(solution)/shard_map/feed_forward/pallas_call | solution.py:319
  655.4 25.7 %collective-permute-done.5 = bf16[320,2048]{1,0:T(8,128)(2,1)S(1)} collective-permute-done((bf16[320,2048]{1,0:T(8,128)(2,1)S(1)}, bf16[320,2048]{1,0:T(8,128)(2,1)S(1)}, u32[]{:S(2)}, u32[]{:S(2)}) %collective-permute-start.5) | collective-permute-done | bytes 1310752 | tf_op jit(solution)/shard_map/ppermute | solution.py:640
  682.1 26.4 %collective-permute-done.4 = bf16[320,2048]{1,0:T(8,128)(2,1)S(1)} collective-permute-done((bf16[320,2048]{1,0:T(8,128)(2,1)S(1)}, bf16[320,2048]{1,0:T(8,128)(2,1)S(1)}, u32[]{:S(2)}, u32[]{:S(2)}) %collective-permute-start.4) | collective-permute-done | bytes 1310752 | tf_op jit(solution)/shard_map/ppermute | solution.py:641
  724.5 25.4 %all-to-all-done.5 = bf16[16,320,128]{2,1,0:T(8,128)(2,1)S(1)} async-done(((bf16[16,320,128]{2,1,0:T(8,128)(2,1)}), bf16[16,320,128]{2,1,0:T(8,128)(2,1)S(1)}, u32[]{:S(2)}, u32[]{:S(2)}) %all-to-all-start.5) | async-done | bytes 1310752 | tf_op jit(solution)/shard_map/all_to_all | solution.py:563
  751.0 51.1 %attention_backward.1 = (f32[5120,128]{1,0:T(8,128)}, f32[5120,128]{1,0:T(8,128)}, f32[5120,128]{1,0:T(8,128)}) custom-call(s32[20]{0:T(128)} %compare_select_fusion.2.parent_ref, bf16[5120,128]{1,0:T(8,128)(2,1)} %get-tuple-element.206.q_ref, bf16[5120,128]{1,0:T(8,128)(2,1)} %bitcast.429, f32[5120,128]{1,0:T(8,128)} %get-tuple-element.45.o_ref, ...), custom_call_target="tpu_custom_call" | custom-call | flops 13421772800 | bytes 15728640 | tf_op jit(solution)/shard_map/attention_backward/pallas_call | solution.py:180
  833.3 9.0 all-to-all-start.6
  845.0 47.6 %all-to-all-done.6 = bf16[16,320,256]{2,1,0:T(8,128)(2,1)S(1)} async-done(((bf16[16,320,256]{2,1,0:T(8,128)(2,1)}), bf16[16,320,256]{2,1,0:T(8,128)(2,1)S(1)}, u32[]{:S(2)}, u32[]{:S(2)}) %all-to-all-start.6) | async-done | bytes 2621472 | tf_op jit(solution)/shard_map/all_to_all | solution.py:566
  892.6 5.7 all-to-all-start.4
  960.3 6.6 reduce-scatter.3.cloned.1.call-done
  979.3 15.7 %all-to-all-done.7 = bf16[320,4,512]{2,0,1:T(8,128)(2,1)S(1)} async-done(((bf16[320,4,512]{2,0,1:T(8,128)(2,1)}), bf16[320,4,512]{2,0,1:T(8,128)(2,1)S(1)}, u32[]{:S(2)}, u32[]{:S(2)}) %all-to-all-start.7) | async-done | bytes 1310752 | tf_op jit(solution)/shard_map/all_to_all | solution.py:687
  996.8 54.3 %all-reduce.24.cloned.1.call-done = (f32[512,48]{0,1:T(8,128)}, f32[512,112]{0,1:T(8,128)}, f32[4,16384]{1,0:T(4,128)}, f32[4,81920]{1,0:T(4,128)}) async-done(((f32[512,48]{0,1:T(8,128)}, f32[512,112]{0,1:T(8,128)}, f32[4,16384]{1,0:T(4,128)}, f32[4,81920]{1,0:T(4,128)}), (f32[512,48]{0,1:T(8,128)}, f32[512,112]{0,1:T(8,128)}, f32[4,16384]{1,0:T(4,128)}, ...) | async-done | bytes 1900560 | tf_op jit(solution)/shard_map/psum | solution.py:691
  1059.8 30.1 %all-reduce.26.cloned.1.call-done = (f32[1,16384]{1,0:T(1,128)}, f32[1,81920]{1,0:T(1,128)}) async-done(((f32[1,16384]{1,0:T(1,128)}, f32[1,81920]{1,0:T(1,128)}), (f32[1,16384]{1,0:T(1,128)}, f32[1,81920]{1,0:T(1,128)})) %all-reduce.26.cloned.1.call-update) | async-done | bytes 393232 | tf_op jit(solution)/shard_map/psum | solution.py:695
  (535 shorter events, 321.8 us)
Async XLA Ops:
  7.2 149.5 %all-gather.7.cloned.1.call-start = ((), (), s32[]{:S(2)}) async-start(), calls=%async_computation.10 | async-start | bytes 17825792 | tf_op jit(solution)/shard_map/all_gather | solution.py:498
  9.7 386.1 %all-gather.9.cloned.1.call-start = ((), (), s32[]{:S(2)}) async-start(), calls=%async_computation.11 | async-start | bytes 8912896 | tf_op jit(solution)/shard_map/all_gather | solution.py:501
  10.5 435.5 %all-gather.15.cloned.1.call-start = ((), (), s32[]{:S(2)}) async-start(), calls=%async_computation.14 | async-start | bytes 13369344 | tf_op jit(solution)/shard_map/all_gather | solution.py:523
  13.0 487.7 %all-gather.13.cloned.1.call-start = ((), (), s32[]{:S(2)}) async-start(), calls=%async_computation.13 | async-start | bytes 13369344 | tf_op jit(solution)/shard_map/all_gather | solution.py:523
  14.1 39.4 %collective-permute-start = (s32[1]{0:T(128)}, s32[1]{0:T(128)}, u32[]{:S(2)}, u32[]{:S(2)}) collective-permute-start(s32[1]{0:T(128)} %param.61), channel_id=1, source_target_pairs={{0,16},{16,0},{1,17},{17,1},{2,18},{18,2},{3,19},{19,3},{4,20},{20... | collective-permute-start | bytes 20 | tf_op jit(solution)/shard_map/ppermute | solution.py:428
  17.1 104.6 %all-to-all-start = ((bf16[4,320,512]{2,1,0:T(8,128)(2,1)}), bf16[4,320,512]{2,1,0:T(8,128)(2,1)S(1)}, u32[]{:S(2)}, u32[]{:S(2)}) async-start(bf16[4,320,512]{2,1,0:T(8,128)(2,1)} %bitcast), calls=%async_computation | async-start | bytes 2621440 | tf_op jit(solution)/shard_map/all_to_all | solution.py:526
  20.7 581.8 %all-gather.11.cloned.1.call-start = ((), (), s32[]{:S(2)}) async-start(), calls=%async_computation.12 | async-start | bytes 13369344 | tf_op jit(solution)/shard_map/all_gather | solution.py:523
  286.5 56.1 %all-to-all-start.3 = ((bf16[4,320,512]{2,1,0:T(8,128)(2,1)}), bf16[4,320,512]{2,1,0:T(8,128)(2,1)}, u32[]{:S(2)}, u32[]{:S(2)}) async-start(bf16[4,320,512]{2,1,0:T(8,128)(2,1)} %bitcast.428), calls=%async_computation.3 | async-start | bytes 2621440 | tf_op jit(solution)/shard_map/all_to_all | solution.py:527
  342.6 51.3 %all-to-all-start.2 = ((bf16[16,320,128]{2,1,0:T(8,128)(2,1)}), bf16[16,320,128]{2,1,0:T(8,128)(2,1)}, u32[]{:S(2)}, u32[]{:S(2)}) async-start(bf16[16,320,128]{2,1,0:T(8,128)(2,1)} %bitcast.415), calls=%async_computation.2 | async-start | bytes 2621440 | tf_op jit(solution)/shard_map/all_to_all | solution.py:566
  350.8 68.1 %collective-permute-start.3 = (bf16[320,2048]{1,0:T(8,128)(2,1)}, bf16[320,2048]{1,0:T(8,128)(2,1)}, u32[]{:S(2)}, u32[]{:S(2)}) collective-permute-start(bf16[320,2048]{1,0:T(8,128)(2,1)} %bitcast.129), channel_id=1, source_target_pairs={{0,16},{16,0},{1,17},{17,1},{2,18},{18,2},{3,19},{19,3},{4,20},{20... | collective-permute-start | bytes 3932168 | tf_op jit(solution)/shard_map/ppermute | solution.py:528
  408.7 31.1 %collective-permute-start.2 = (bf16[320,2048]{1,0:T(8,128)(2,1)}, bf16[320,2048]{1,0:T(8,128)(2,1)}, u32[]{:S(2)}, u32[]{:S(2)}) collective-permute-start(bf16[320,2048]{1,0:T(8,128)(2,1)} %multiply_convert_fusion), channel_id=1, source_target_pairs={{0,16},{16,0},{1,17},{17,1},{2,18},{18,2},{3,19},{19,3},{4,20},{20... | collective-permute-start | bytes 3932168 | tf_op jit(solution)/shard_map/ppermute | solution.py:598
  649.4 31.7 %collective-permute-start.5 = (bf16[320,2048]{1,0:T(8,128)(2,1)S(1)}, bf16[320,2048]{1,0:T(8,128)(2,1)S(1)}, u32[]{:S(2)}, u32[]{:S(2)}) collective-permute-start(bf16[320,2048]{1,0:T(8,128)(2,1)S(1)} %slice.898), channel_id=1, source_target_pairs={{0,16},{16,0},{1,17},{17,1},{2,18},{18,2},{3,19},{19,3},{4,20},{20... | collective-permute-start | bytes 3932168 | tf_op jit(solution)/shard_map/ppermute | solution.py:640
  654.8 53.7 %collective-permute-start.4 = (bf16[320,2048]{1,0:T(8,128)(2,1)S(1)}, bf16[320,2048]{1,0:T(8,128)(2,1)S(1)}, u32[]{:S(2)}, u32[]{:S(2)}) collective-permute-start(bf16[320,2048]{1,0:T(8,128)(2,1)S(1)} %slice.899), channel_id=1, source_target_pairs={{0,16},{16,0},{1,17},{17,1},{2,18},{18,2},{3,19},{19,3},{4,20},{20... | collective-permute-start | bytes 3932168 | tf_op jit(solution)/shard_map/ppermute | solution.py:641
  718.9 31.1 %all-to-all-start.5 = ((bf16[16,320,128]{2,1,0:T(8,128)(2,1)}), bf16[16,320,128]{2,1,0:T(8,128)(2,1)S(1)}, u32[]{:S(2)}, u32[]{:S(2)}) async-start(bf16[16,320,128]{2,1,0:T(8,128)(2,1)} %bitcast.381), calls=%async_computation.5 | async-start | bytes 2621440 | tf_op jit(solution)/shard_map/all_to_all | solution.py:563
  722.6 237.7 %reduce-scatter.5.cloned.1.call-start = ((), (), s32[]{:S(2)}) async-start(), calls=%async_computation.16 | async-start | bytes 1146880 | tf_op jit(solution)/shard_map/reduce_scatter | solution.py:690
  811.4 16.8 %collective-permute-start.6 = (f32[5120,128]{0,1:T(8,128)}, f32[5120,128]{0,1:T(8,128)}, u32[]{:S(2)}, u32[]{:S(2)}) collective-permute-start(f32[5120,128]{0,1:T(8,128)} %multiply_select_fusion), channel_id=1, source_target_pairs={{0,4},{4,0},{8,12},{12,8},{1,5},{5,1},{9,13},{13,9},{2,6},{6,2},{1... | collective-permute-start | bytes 7864328 | tf_op jit(solution)/shard_map/ppermute | solution.py:664
  833.3 59.3 %all-to-all-start.6 = ((bf16[16,320,256]{2,1,0:T(8,128)(2,1)}), bf16[16,320,256]{2,1,0:T(8,128)(2,1)S(1)}, u32[]{:S(2)}, u32[]{:S(2)}) async-start(bf16[16,320,256]{2,1,0:T(8,128)(2,1)} %bitcast.398), calls=%async_computation.6 | async-start | bytes 5242880 | tf_op jit(solution)/shard_map/all_to_all | solution.py:566
  892.6 81.6 %all-to-all-start.4 = ((bf16[320,4,512]{2,0,1:T(8,128)(2,1)}), bf16[320,4,512]{2,0,1:T(8,128)(2,1)}, u32[]{:S(2)}, u32[]{:S(2)}) async-start(bf16[320,4,512]{2,0,1:T(8,128)(2,1)} %bitcast.410), calls=%async_computation.4 | async-start | bytes 2621440 | tf_op jit(solution)/shard_map/all_to_all | solution.py:643
  898.3 68.6 %reduce-scatter.3.cloned.1.call-start = ((), (), s32[]{:S(2)}) async-start(), calls=%async_computation.15 | async-start | bytes 491520 | tf_op jit(solution)/shard_map/reduce_scatter | solution.py:690
  937.8 113.3 %all-reduce.24.cloned.1.call-start = ((), (), s32[]{:S(2)}) async-start(), calls=%async_computation.17 | async-start | bytes 3801088 | tf_op jit(solution)/shard_map/psum | solution.py:691
  974.2 20.8 %all-to-all-start.7 = ((bf16[320,4,512]{2,0,1:T(8,128)(2,1)}), bf16[320,4,512]{2,0,1:T(8,128)(2,1)S(1)}, u32[]{:S(2)}, u32[]{:S(2)}) async-start(bf16[320,4,512]{2,0,1:T(8,128)(2,1)} %bitcast.379), calls=%async_computation.7 | async-start | bytes 2621440 | tf_op jit(solution)/shard_map/all_to_all | solution.py:687
  977.7 112.1 %all-reduce.26.cloned.1.call-start = ((), (), s32[]{:S(2)}) async-start(), calls=%async_computation.18 | async-start | bytes 786432 | tf_op jit(solution)/shard_map/psum | solution.py:695
  1057.4 40.2 %collective-permute-start.7 = (f32[512,160]{0,1:T(8,128)S(1)}, f32[512,160]{0,1:T(8,128)S(1)}, u32[]{:S(2)}, u32[]{:S(2)}) collective-permute-start(f32[512,160]{0,1:T(8,128)S(1)} %pad_maximum_fusion.11), channel_id=1, source_target_pairs={{0,16},{16,0},{1,17},{17,1},{2,18},{18,2},{3,19},{19,3},{4,20},{20... | collective-permute-start | bytes 983048 | tf_op jit(solution)/shard_map/ppermute | solution.py:722
  1092.6 9.6 collective-permute-start.8
  (114 other events, 1639.2 us)
Sparse Core Ops, SparseCore 0:
  10.8 145.8 all-gather.6
  158.9 113.0 all-gather.8
  274.8 122.0 all-gather.14
  399.6 101.1 all-gather.12
  503.5 98.9 all-gather.10
  823.0 39.8 reduce-scatter.4
  937.9 28.9 reduce-scatter.2
  970.2 80.8 all-reduce.23
  1059.1 30.7 all-reduce.25

commit v2 on v1

v2 whole, which is shorter than its diff:
```python
import functools
import math

import jax
import jax.numpy as jnp
from jax import lax
from jax.experimental import pallas as pl
from jax.experimental.pallas import tpu as pltpu
from jax.sharding import PartitionSpec as P

MODEL_WIDTH = 2048
QUERY_HEADS = 16
KEY_VALUE_HEADS = 8
HEAD_SIZE = 128
ADAPTER_RANK = 16
TREE_LEN = 5120
TRUNK = 2048
SEG_LEN = 256

EPSILON = 1e-06
THETA = 1000000.0
ADAPTER_FACTOR = 2.0
BF = jnp.bfloat16
F32 = jnp.float32
SCALE = HEAD_SIZE ** (-0.5)
SCALE_LOG2 = SCALE * math.log2(math.e)
PLANE = ("col", "row")
LANES = 128
VMEM_LIMIT = 63 * 1024 * 1024


def dot(left, right):
    return jnp.dot(left, right, preferred_element_type=F32)


def dot_nt(left, right):
    return lax.dot_general(left, right, (((1,), (1,)), ((), ())), preferred_element_type=F32)


def dot_tn(left, right):
    return lax.dot_general(left, right, (((0,), (0,)), ((), ())), preferred_element_type=F32)


def attention_forward_kernel(
    parent_ref, flag_ref, q_ref, mine_ref, theirs_ref, o_ref, low_ref, l_ref, k_ref, v_ref, acc_ref
):
    index = pl.program_id(0)
    trunk_blocks = TRUNK // SEG_LEN

    @pl.when(index == 0)
    def _():
        lane = lax.broadcasted_iota(jnp.int32, (v_ref.shape[0], HEAD_SIZE), 1)
        v_ref[:, HEAD_SIZE:] = jnp.where(lane == 0, 1.0, 0.0).astype(BF)

        @pl.when(flag_ref[0] == 1)
        def _():
            k_ref[...] = mine_ref[...]
            v_ref[:, :HEAD_SIZE] = theirs_ref[...]

        @pl.when(flag_ref[0] != 1)
        def _():
            k_ref[...] = theirs_ref[...]
            v_ref[:, :HEAD_SIZE] = mine_ref[...]

    query = q_ref[...]
    acc_ref[...] = jnp.zeros_like(acc_ref)

    def step(start, size, causal=False):
        rows = pl.ds(start, size)
        scores = dot_nt(query, k_ref[rows, :])
        probs = jnp.exp2(scores * SCALE_LOG2)
        if causal:
            ahead = lax.broadcasted_iota(jnp.int32, probs.shape, 0)
            behind = lax.broadcasted_iota(jnp.int32, probs.shape, 1)
            probs = jnp.where(behind <= ahead, probs, 0.0)
        acc_ref[...] += dot(probs.astype(BF), v_ref[rows, :])

    @pl.when(index < trunk_blocks)
    def _():
        @pl.loop(0, index)
        def _(block):
            step(pl.multiple_of(block * SEG_LEN, SEG_LEN), SEG_LEN)

    @pl.when(index >= trunk_blocks)
    def _():
        size = 512
        for part in range(TRUNK // size):
            step(part * size, size)

        above = parent_ref[index]

        @pl.when(above >= 0)
        def _():
            step(pl.multiple_of(above * SEG_LEN, SEG_LEN), SEG_LEN)

    step(pl.multiple_of(index * SEG_LEN, SEG_LEN), SEG_LEN, True)
    total = acc_ref[:, HEAD_SIZE : HEAD_SIZE + 1]
    attended = acc_ref[:, :HEAD_SIZE] / total
    o_ref[...] = attended
    low_ref[...] = attended.astype(BF)
    spread = jnp.broadcast_to(total, (SEG_LEN, LANES))
    l_ref[0] = jnp.transpose(spread)[:8, :]


def attention_forward(parent_block, flag, got, theirs):
    length = theirs.shape[0]
    blocks = length // SEG_LEN
    whole = lambda i, p, f: (0, 0)
    part = lambda i, p, f: (i, 0)
    return pl.pallas_call(
        attention_forward_kernel,
        grid_spec=pltpu.PrefetchScalarGridSpec(
            num_scalar_prefetch=2,
            grid=(blocks,),
            in_specs=[
                pl.BlockSpec((SEG_LEN, HEAD_SIZE), part),
                pl.BlockSpec((length, HEAD_SIZE), lambda i, p, f: (0, 1)),
                pl.BlockSpec((length, HEAD_SIZE), whole),
            ],
            out_specs=[
                pl.BlockSpec((SEG_LEN, HEAD_SIZE), part),
                pl.BlockSpec((SEG_LEN, HEAD_SIZE), part),
                pl.BlockSpec((1, 8, SEG_LEN), lambda i, p, f: (i, 0, 0)),
            ],
            scratch_shapes=[
                pltpu.VMEM((length, HEAD_SIZE), BF),
                pltpu.VMEM((length, 2 * HEAD_SIZE), BF),
                pltpu.VMEM((SEG_LEN, 2 * HEAD_SIZE), F32),
            ],
        ),
        out_shape=[
            jax.ShapeDtypeStruct((length, HEAD_SIZE), F32),
            jax.ShapeDtypeStruct((length, HEAD_SIZE), BF),
            jax.ShapeDtypeStruct((blocks, 8, SEG_LEN), F32),
        ],
        compiler_params=pltpu.CompilerParams(vmem_limit_bytes=VMEM_LIMIT),
        cost_estimate=pl.CostEstimate(
            flops=160 * SEG_LEN * SEG_LEN * HEAD_SIZE * 4,
            bytes_accessed=length * HEAD_SIZE * 12,
            transcendentals=160 * SEG_LEN * SEG_LEN,
        ),
        name="attention_forward",
    )(parent_block, flag, got, got, theirs)


def attention_backward_kernel(
    parent_ref,
    flag_ref,
    q_ref,
    g_ref,
    o_ref,
    l_ref,
    mine_ref,
    theirs_ref,
    dq_ref,
    kept_ref,
    given_ref,
    k_ref,
    v_ref,
    kt_ref,
    dk_ref,
    dv_ref,
    acc_ref,
):
    index = pl.program_id(0)
    trunk_blocks = TRUNK // SEG_LEN

    @pl.when(index == 0)
    def _():
        dk_ref[...] = jnp.zeros_like(dk_ref)
        dv_ref[...] = jnp.zeros_like(dv_ref)

        @pl.when(flag_ref[0] == 1)
        def _():
            k_ref[...] = mine_ref[...]
            v_ref[...] = theirs_ref[...]

        @pl.when(flag_ref[0] != 1)
        def _():
            k_ref[...] = theirs_ref[...]
            v_ref[...] = mine_ref[...]

        @pl.loop(0, k_ref.shape[0] // SEG_LEN)
        def _(block):
            rows = pl.ds(pl.multiple_of(block * SEG_LEN, SEG_LEN), SEG_LEN)
            kt_ref[:, rows] = jnp.transpose(k_ref[rows, :])

    query = q_ref[...]
    grad = g_ref[...]
    delta = jnp.sum(grad.astype(F32) * o_ref[...], axis=1, keepdims=True)
    delta = jnp.transpose(jnp.broadcast_to(delta, (SEG_LEN, LANES)))[:1, :]
    inverse = 1.0 / l_ref[0, :1, :]
    acc_ref[...] = jnp.zeros_like(acc_ref)

    def step(start, size, causal=False):
        rows = pl.ds(start, size)
        probs = jnp.exp2(dot_nt(k_ref[rows, :], query) * SCALE_LOG2) * inverse
        if causal:
            behind = lax.broadcasted_iota(jnp.int32, probs.shape, 0)
            ahead = lax.broadcasted_iota(jnp.int32, probs.shape, 1)
            probs = jnp.where(behind <= ahead, probs, 0.0)
        dprobs = dot_nt(v_ref[rows, :], grad)
        dscores = (probs * (dprobs - delta)).astype(BF)
        dv_ref[rows, :] += dot(probs.astype(BF), grad)
        dk_ref[rows, :] += dot(dscores, query)
        acc_ref[...] += dot(kt_ref[:, rows], dscores)

    @pl.when(index < trunk_blocks)
    def _():
        @pl.loop(0, index)
        def _(block):
            step(pl.multiple_of(block * SEG_LEN, SEG_LEN), SEG_LEN)

    @pl.when(index >= trunk_blocks)
    def _():
        size = 512
        for part in range(TRUNK // size):
            step(part * size, size)

        above = parent_ref[index]

        @pl.when(above >= 0)
        def _():
            step(pl.multiple_of(above * SEG_LEN, SEG_LEN), SEG_LEN)

    step(pl.multiple_of(index * SEG_LEN, SEG_LEN), SEG_LEN, True)
    dq_ref[...] = (jnp.transpose(acc_ref[...]) * SCALE).astype(BF)

    @pl.when(index == pl.num_programs(0) - 1)
    def _():
        @pl.when(flag_ref[0] == 1)
        def _():
            kept_ref[...] = dk_ref[...] * SCALE
            given_ref[...] = dv_ref[...]

        @pl.when(flag_ref[0] != 1)
        def _():
            kept_ref[...] = dv_ref[...]
            given_ref[...] = dk_ref[...] * SCALE


def attention_backward(parent_block, flag, got, grad, attended, totals, theirs):
    length = theirs.shape[0]
    blocks = length // SEG_LEN
    whole = lambda i, p, f: (0, 0)
    part = lambda i, p, f: (i, 0)
    return pl.pallas_call(
        attention_backward_kernel,
        grid_spec=pltpu.PrefetchScalarGridSpec(
            num_scalar_prefetch=2,
            grid=(blocks,),
            in_specs=[
                pl.BlockSpec((SEG_LEN, HEAD_SIZE), part),
                pl.BlockSpec((SEG_LEN, HEAD_SIZE), part),
                pl.BlockSpec((SEG_LEN, HEAD_SIZE), part),
                pl.BlockSpec((1, 8, SEG_LEN), lambda i, p, f: (i, 0, 0)),
                pl.BlockSpec((length, HEAD_SIZE), lambda i, p, f: (0, 1)),
                pl.BlockSpec((length, HEAD_SIZE), whole),
            ],
            out_specs=[
                pl.BlockSpec((SEG_LEN, HEAD_SIZE), part),
                pl.BlockSpec((length, HEAD_SIZE), whole),
                pl.BlockSpec((length, HEAD_SIZE), whole),
            ],
            scratch_shapes=[
                pltpu.VMEM((length, HEAD_SIZE), BF),
                pltpu.VMEM((length, HEAD_SIZE), BF),
                pltpu.VMEM((HEAD_SIZE, length), BF),
                pltpu.VMEM((length, HEAD_SIZE), F32),
                pltpu.VMEM((length, HEAD_SIZE), F32),
                pltpu.VMEM((HEAD_SIZE, SEG_LEN), F32),
            ],
        ),
        out_shape=[
            jax.ShapeDtypeStruct((length, 2 * HEAD_SIZE), BF),
            jax.ShapeDtypeStruct((length, HEAD_SIZE), F32),
            jax.ShapeDtypeStruct((length, HEAD_SIZE), F32),
        ],
        compiler_params=pltpu.CompilerParams(vmem_limit_bytes=VMEM_LIMIT),
        cost_estimate=pl.CostEstimate(
            flops=160 * SEG_LEN * SEG_LEN * HEAD_SIZE * 10,
            bytes_accessed=length * HEAD_SIZE * 24,
            transcendentals=160 * SEG_LEN * SEG_LEN,
        ),
        name="attention_backward",
    )(parent_block, flag, got, grad, attended, totals, got, theirs)


def merge_kernel(lines_ref, kept_ref, got_ref, out_ref):
    out_ref[...] = (kept_ref[...] + got_ref[...]).astype(BF)


def merge(lines, kept, got):
    length = kept.shape[0]
    rows = 4 * SEG_LEN
    part = pl.BlockSpec((rows, HEAD_SIZE), lambda i: (i, 0))
    return pl.pallas_call(
        merge_kernel,
        grid=(length // rows,),
        in_specs=[pl.BlockSpec(memory_space=pl.ANY), part, part],
        out_specs=pl.BlockSpec((rows, HEAD_SIZE), lambda i: (i, 1)),
        out_shape=jax.ShapeDtypeStruct(lines.shape, lines.dtype),
        input_output_aliases={0: 0},
        cost_estimate=pl.CostEstimate(
            flops=length * HEAD_SIZE, bytes_accessed=length * HEAD_SIZE * 10, transcendentals=0
        ),
        name="merge",
    )(lines, kept, got)


def norm_scale(values):
    return lax.rsqrt(jnp.mean(values * values, axis=1, keepdims=True) + EPSILON)


def norm_back(values, scale, gain, gradient):
    weighted = gain * gradient
    inner_sum = jnp.sum(weighted * values, axis=1, keepdims=True)
    return scale * weighted - values * (scale**3 * (inner_sum * (1.0 / MODEL_WIDTH)))


def outmaps_of(w_ref, pieces, piece, used):
    at = pieces * piece
    return jnp.concatenate(
        [w_ref[0, 0, at + p * used : at + (p + 1) * used, :] for p in range(pieces)], axis=1
    )


def qkv_forward_kernel(
    x_ref,
    gain_ref,
    a_ref,
    cos_ref,
    sin_ref,
    hg_ref,
    w_ref,
    m_ref,
    pre_ref,
    sent_ref,
    hidden_ref,
):
    row_blocks = w_ref.shape[1]
    piece = w_ref.shape[3]
    pieces = w_ref.shape[2] // piece
    heads = sent_ref.shape[0]
    used = m_ref.shape[1]

    @pl.when(pl.program_id(0) == 0)
    def _():
        resid = x_ref[...].astype(F32)
        hidden_ref[...] = (resid * norm_scale(resid) * gain_ref[...]).astype(BF)
        m_ref[...] = dot(hidden_ref[...], a_ref[...]).astype(BF)

    hidden = hidden_ref[...]
    whole = jnp.concatenate(
        [
            dot(
                hidden,
                jnp.concatenate(
                    [w_ref[0, r, p * piece : (p + 1) * piece, :] for r in range(row_blocks)], axis=0
                ),
            )
            for p in range(pieces)
        ],
        axis=1,
    ) + ADAPTER_FACTOR * dot(m_ref[...], outmaps_of(w_ref, pieces, piece, used))
    pre_ref[0] = whole[:, : pre_ref.shape[2]]
    cosine = cos_ref[...]
    sine = sin_ref[...]

    def shaped(at, gain):
        lines = whole[:, at : at + HEAD_SIZE]
        normed = lines * norm_scale(lines) * gain
        return (normed * cosine + pltpu.roll(normed, HEAD_SIZE // 2, 1) * sine).astype(BF)

    for head in range(heads):
        sent_ref[head, :, :HEAD_SIZE] = shaped(head * HEAD_SIZE, hg_ref[0:1, :])
    key_at = heads * HEAD_SIZE
    value_at = key_at + heads // 2 * HEAD_SIZE
    for pair in range(heads // 2):
        at = pair * HEAD_SIZE
        sent_ref[2 * pair, :, HEAD_SIZE:] = shaped(key_at + at, hg_ref[1:2, :])
        sent_ref[2 * pair + 1, :, HEAD_SIZE:] = whole[
            :, value_at + at : value_at + at + HEAD_SIZE
        ].astype(BF)


def qkv_forward(x, gain, inmaps, cosine, sine, head_gains, weights):
    own = x.shape[0]
    cols, row_blocks, tall, piece = weights.shape
    wide = tall // piece * piece
    used = inmaps.shape[1]
    heads = QUERY_HEADS // cols
    whole = lambda c: (0, 0)
    step = lambda c: (c, 0, 0)
    return pl.pallas_call(
        qkv_forward_kernel,
        grid=(cols,),
        in_specs=[
            pl.BlockSpec(x.shape, whole),
            pl.BlockSpec(gain.shape, whole),
            pl.BlockSpec(inmaps.shape, whole),
            pl.BlockSpec(cosine.shape, whole),
            pl.BlockSpec(sine.shape, whole),
            pl.BlockSpec(head_gains.shape, whole),
            pl.BlockSpec((1, row_blocks, tall, piece), lambda c: (c, 0, 0, 0)),
        ],
        out_specs=[
            pl.BlockSpec((own, used), whole),
            pl.BlockSpec((1, own, wide * 3 // 4), step),
            pl.BlockSpec((heads, own, 2 * HEAD_SIZE), step),
        ],
        out_shape=[
            jax.ShapeDtypeStruct((own, used), BF),
            jax.ShapeDtypeStruct((cols, own, wide * 3 // 4), F32),
            jax.ShapeDtypeStruct((QUERY_HEADS, own, 2 * HEAD_SIZE), BF),
        ],
        scratch_shapes=[pltpu.VMEM((own, MODEL_WIDTH), BF)],
        compiler_params=pltpu.CompilerParams(vmem_limit_bytes=VMEM_LIMIT),
        cost_estimate=pl.CostEstimate(
            flops=2 * own * MODEL_WIDTH * cols * wide,
            bytes_accessed=cols * wide * MODEL_WIDTH * 2,
            transcendentals=own * cols * 8,
        ),
        name="qkv_forward",
    )(x, gain, inmaps, cosine, sine, head_gains, weights)


def qkv_unshape_kernel(
    ret_ref,
    pre_ref,
    m_ref,
    x_ref,
    gain_ref,
    cos_ref,
    sin_ref,
    hg_ref,
    w_ref,
    grads_ref,
    inner_ref,
    ga_ref,
    gb_ref,
    in_acc_ref,
):
    step = pl.program_id(0)
    row_blocks, used, piece = ga_ref.shape
    heads = ret_ref.shape[0]
    pieces = grads_ref.shape[2] // piece
    cosine = cos_ref[...]
    sine = sin_ref[...]

    @pl.when(step == 0)
    def _():
        in_acc_ref[...] = jnp.zeros_like(in_acc_ref)

    def unshaped(grad, at, gain):
        grad = grad.astype(F32)
        lines = pre_ref[0, :, at : at + HEAD_SIZE]
        turned = gain * (grad * cosine + pltpu.roll(grad * sine, HEAD_SIZE // 2, 1))
        scale = norm_scale(lines)
        inner_mean = jnp.mean(turned * lines, axis=1, keepdims=True)
        return (scale * turned - lines * (scale**3 * inner_mean)).astype(BF)

    parts = []
    for head in range(heads):
        parts.append(unshaped(ret_ref[head, :, :HEAD_SIZE], head * HEAD_SIZE, hg_ref[0:1, :]))
    for pair in range(heads // 2):
        at = (heads + pair) * HEAD_SIZE
        parts.append(unshaped(ret_ref[2 * pair, :, HEAD_SIZE:], at, hg_ref[1:2, :]))
    for pair in range(heads // 2):
        parts.append(ret_ref[2 * pair + 1, :, HEAD_SIZE:])
    grads = jnp.concatenate(parts, axis=1)
    grads_ref[0] = grads
    outmaps = jnp.concatenate(
        [w_ref[0, 0, p * used : (p + 1) * used, :] for p in range(pieces)], axis=1
    )
    in_acc_ref[...] += dot_nt(grads, outmaps)
    outer = ADAPTER_FACTOR * dot_tn(m_ref[...], grads)
    rank = ADAPTER_RANK
    edges = (0, heads * HEAD_SIZE, heads * HEAD_SIZE * 3 // 2, heads * HEAD_SIZE * 2)
    for i in range(3):
        gb_ref[0, :, edges[i] : edges[i + 1]] = outer[
            i * rank : (i + 1) * rank, edges[i] : edges[i + 1]
        ]

    @pl.when(step == pl.num_programs(0) - 1)
    def _():
        inner = (ADAPTER_FACTOR * in_acc_ref[...]).astype(BF)
        inner_ref[...] = inner
        resid = x_ref[...].astype(F32)
        hidden = (resid * norm_scale(resid) * gain_ref[...]).astype(BF)
        for r in range(row_blocks):
            ga_ref[r] = dot_tn(inner, hidden[:, r * piece : (r + 1) * piece])


def qkv_unshape(returned, pre, masked, x, gain, cosine, sine, head_gains, weights):
    own = x.shape[0]
    cols, row_blocks, tall, piece = weights.shape
    pieces = tall // piece
    wide = pieces * piece
    heads = QUERY_HEADS // cols
    used = 3 * ADAPTER_RANK
    map_rows = tall - wide
    at = wide // map_rows if wide % map_rows == 0 else None
    maps = weights[:, :1, wide:] if at is None else weights
    first = 0 if at is None else at
    whole = lambda c: (0, 0)
    step = lambda c: (c, 0, 0)
    return pl.pallas_call(
        qkv_unshape_kernel,
        grid=(cols,),
        in_specs=[
            pl.BlockSpec((heads, own, 2 * HEAD_SIZE), step),
            pl.BlockSpec((1, own, pre.shape[2]), step),
            pl.BlockSpec(masked.shape, whole),
            pl.BlockSpec(x.shape, whole),
            pl.BlockSpec(gain.shape, whole),
            pl.BlockSpec(cosine.shape, whole),
            pl.BlockSpec(sine.shape, whole),
            pl.BlockSpec(head_gains.shape, whole),
            pl.BlockSpec((1, 1, map_rows, piece), lambda c: (c, 0, first, 0)),
        ],
        out_specs=[
            pl.BlockSpec((1, own, wide), step),
            pl.BlockSpec((own, used), whole),
            pl.BlockSpec((row_blocks, used, piece), lambda c: (0, 0, 0)),
            pl.BlockSpec((1, ADAPTER_RANK, wide), step),
        ],
        out_shape=[
            jax.ShapeDtypeStruct((cols, own, wide), BF),
            jax.ShapeDtypeStruct((own, used), BF),
            jax.ShapeDtypeStruct((row_blocks, used, piece), F32),
            jax.ShapeDtypeStruct((cols, ADAPTER_RANK, wide), F32),
        ],
        scratch_shapes=[pltpu.VMEM((own, used), F32)],
        compiler_params=pltpu.CompilerParams(vmem_limit_bytes=VMEM_LIMIT),
        cost_estimate=pl.CostEstimate(
            flops=4 * own * 64 * cols * wide,
            bytes_accessed=cols * own * wide * 8,
            transcendentals=own * cols * 8,
        ),
        name="qkv_unshape",
    )(returned, pre, masked, x, gain, cosine, sine, head_gains, maps)


def qkv_backward_kernel(
    grads_ref, inner_ref, x_ref, gm_ref, gain_ref, a_ref, w_ref, grad_ref, acc_ref
):
    step = pl.program_id(0)
    row_blocks = w_ref.shape[1]
    piece = w_ref.shape[3]
    pieces = w_ref.shape[2] // piece

    @pl.when(step == 0)
    def _():
        acc_ref[...] = dot_nt(inner_ref[...], a_ref[...])

    for r in range(row_blocks):
        weights = jnp.concatenate(
            [w_ref[0, r, p * piece : (p + 1) * piece, :] for p in range(pieces)], axis=1
        )
        acc_ref[:, r * piece : (r + 1) * piece] += dot_nt(grads_ref[0], weights)

    @pl.when(step == pl.num_programs(0) - 1)
    def _():
        resid = x_ref[...].astype(F32)
        grad_ref[...] = (
            gm_ref[...] + norm_back(resid, norm_scale(resid), gain_ref[...], acc_ref[...])
        ).astype(BF)


def qkv_backward(grads, inner, x, grad_middle, gain, inmaps, weights):
    own = x.shape[0]
    cols, row_blocks, tall, piece = weights.shape
    wide = tall // piece * piece
    whole = lambda c: (0, 0)
    once = pl.Buffered(1)
    return pl.pallas_call(
        qkv_backward_kernel,
        grid=(cols,),
        in_specs=[
            pl.BlockSpec((1, own, wide), lambda c: (c, 0, 0)),
            pl.BlockSpec(inner.shape, whole),
            pl.BlockSpec(x.shape, whole, pipeline_mode=once),
            pl.BlockSpec(grad_middle.shape, whole, pipeline_mode=once),
            pl.BlockSpec(gain.shape, whole),
            pl.BlockSpec(inmaps.shape, whole),
            pl.BlockSpec((1, row_blocks, wide, piece), lambda c: (c, 0, 0, 0)),
        ],
        out_specs=pl.BlockSpec((own, MODEL_WIDTH), whole),
        out_shape=jax.ShapeDtypeStruct((own, MODEL_WIDTH), BF),
        scratch_shapes=[pltpu.VMEM((own, MODEL_WIDTH), F32)],
        compiler_params=pltpu.CompilerParams(vmem_limit_bytes=VMEM_LIMIT),
        cost_estimate=pl.CostEstimate(
            flops=2 * own * MODEL_WIDTH * cols * wide,
            bytes_accessed=cols * wide * MODEL_WIDTH * 2,
            transcendentals=own,
        ),
        name="qkv_backward",
    )(grads, inner, x, grad_middle, gain, inmaps, weights)


def joined(refs, tall):
    return jnp.concatenate(
        [ref[0, r, 0, :tall, :] for r in range(refs[0].shape[1]) for ref in refs], axis=1
    )


def output_specs(weights, first_unit, features):
    row_blocks, tall = weights.shape[1], weights.shape[3]

    def spec(unit):
        return pl.BlockSpec((1, row_blocks, 1, tall, LANES), lambda c: (c, 0, unit, 0, 0))

    return [spec(first_unit + j) for j in range(features // LANES)]


def output_forward_kernel(att_ref, x_ref, gain_ref, a_ref, b_ref, *refs):
    weight_refs = refs[:-5]
    middle_ref, hidden_ref, m_ref, acc_ref, m_acc_ref = refs[-5:]
    step = pl.program_id(0)
    heads = att_ref.shape[0]

    @pl.when(step == 0)
    def _():
        acc_ref[...] = x_ref[...].astype(F32)
        m_acc_ref[...] = jnp.zeros_like(m_acc_ref)

    attended = jnp.concatenate([att_ref[h] for h in range(heads)], axis=1)
    acc_ref[...] += dot(attended, joined(weight_refs, attended.shape[1]))
    m_acc_ref[...] += dot_nt(attended, a_ref[0])

    @pl.when(step == pl.num_programs(0) - 1)
    def _():
        masked = m_acc_ref[...].astype(BF)
        m_ref[...] = masked
        middle = acc_ref[...] + ADAPTER_FACTOR * dot_nt(masked, b_ref[...])
        middle_ref[...] = middle
        hidden_ref[...] = (middle * norm_scale(middle) * gain_ref[...]).astype(BF)


def output_forward(attended, x, gain, inmaps, outmaps, weights, first_unit):
    own = x.shape[0]
    cols, row_blocks = weights.shape[:2]
    features = MODEL_WIDTH // row_blocks
    heads = QUERY_HEADS // cols
    o_rows = heads * HEAD_SIZE
    specs = output_specs(weights, first_unit, features)
    whole = lambda c: (0, 0)
    step = lambda c: (c, 0, 0)
    return pl.pallas_call(
        output_forward_kernel,
        grid=(cols,),
        in_specs=[
            pl.BlockSpec((heads, own, HEAD_SIZE), step),
            pl.BlockSpec(x.shape, whole),
            pl.BlockSpec(gain.shape, whole),
            pl.BlockSpec((1, LANES, o_rows), step),
            pl.BlockSpec(outmaps.shape, whole),
            *specs,
        ],
        out_specs=[
            pl.BlockSpec((own, MODEL_WIDTH), whole),
            pl.BlockSpec((own, MODEL_WIDTH), whole),
            pl.BlockSpec((own, LANES), whole),
        ],
        out_shape=[
            jax.ShapeDtypeStruct((own, MODEL_WIDTH), F32),
            jax.ShapeDtypeStruct((own, MODEL_WIDTH), BF),
            jax.ShapeDtypeStruct((own, LANES), BF),
        ],
        scratch_shapes=[pltpu.VMEM((own, MODEL_WIDTH), F32), pltpu.VMEM((own, LANES), F32)],
        compiler_params=pltpu.CompilerParams(vmem_limit_bytes=VMEM_LIMIT),
        cost_estimate=pl.CostEstimate(
            flops=2 * own * MODEL_WIDTH * MODEL_WIDTH,
            bytes_accessed=2 * MODEL_WIDTH * MODEL_WIDTH,
            transcendentals=own,
        ),
        name="output_forward",
    )(attended, x, gain, inmaps, outmaps, *[weights] * len(specs))


def output_backward_kernel(
    gh_ref,
    got_ref,
    cot_ref,
    middle_ref,
    gain_ref,
    a_ref,
    b_ref,
    att_ref,
    m_ref,
    *refs,
):
    weight_refs = refs[:-6]
    gm_ref, sent_ref, gb_ref, ga_ref, low_ref, inner_ref = refs[-6:]
    heads = sent_ref.shape[0]
    row_blocks, rank, features = gb_ref.shape

    @pl.when(pl.program_id(0) == 0)
    def _():
        grad_hidden = gh_ref[...] + got_ref[...].astype(F32)
        middle = middle_ref[...]
        grad = cot_ref[...].astype(F32) + norm_back(
            middle, norm_scale(middle), gain_ref[...], grad_hidden
        )
        gm_ref[...] = grad
        low_ref[...] = grad.astype(BF)
        inner_ref[...] = (ADAPTER_FACTOR * dot(low_ref[...], b_ref[...])).astype(BF)
        outer = ADAPTER_FACTOR * dot_tn(m_ref[...], low_ref[...])
        for r in range(row_blocks):
            gb_ref[r] = outer[:rank, r * features : (r + 1) * features]

    attended = jnp.concatenate([att_ref[h] for h in range(heads)], axis=1)
    ga_ref[0] = dot_tn(inner_ref[...], attended)[:rank, :]
    weights = joined(weight_refs, heads * HEAD_SIZE)
    grad = (dot_nt(low_ref[...], weights) + dot(inner_ref[...], a_ref[0])).astype(BF)
    for head in range(heads):
        sent_ref[head] = grad[:, head * HEAD_SIZE : (head + 1) * HEAD_SIZE]


def output_backward(
    grad_hidden, got, cotangent, middle, gain, inmaps, outmaps, attended, masked, weights, first_unit
):
    own = middle.shape[0]
    cols, row_blocks = weights.shape[:2]
    features = MODEL_WIDTH // row_blocks
    heads = QUERY_HEADS // cols
    o_rows = heads * HEAD_SIZE
    specs = output_specs(weights, first_unit, features)
    whole = lambda c: (0, 0)
    step = lambda c: (c, 0, 0)
    once = pl.Buffered(1)
    return pl.pallas_call(
        output_backward_kernel,
        grid=(cols,),
        in_specs=[
            pl.BlockSpec((own, MODEL_WIDTH), whole, pipeline_mode=once),
            pl.BlockSpec((own, MODEL_WIDTH), whole, pipeline_mode=once),
            pl.BlockSpec((own, MODEL_WIDTH), whole, pipeline_mode=once),
            pl.BlockSpec((own, MODEL_WIDTH), whole, pipeline_mode=once),
            pl.BlockSpec(gain.shape, whole),
            pl.BlockSpec((1, LANES, o_rows), step),
            pl.BlockSpec(outmaps.shape, whole),
            pl.BlockSpec((heads, own, HEAD_SIZE), step),
            pl.BlockSpec(masked.shape, whole),
            *specs,
        ],
        out_specs=[
            pl.BlockSpec((own, MODEL_WIDTH), whole),
            pl.BlockSpec((heads, own, HEAD_SIZE), step),
            pl.BlockSpec((row_blocks, ADAPTER_RANK, features), lambda c: (0, 0, 0)),
            pl.BlockSpec((1, ADAPTER_RANK, o_rows), step),
        ],
        out_shape=[
            jax.ShapeDtypeStruct((own, MODEL_WIDTH), F32),
            jax.ShapeDtypeStruct((QUERY_HEADS, own, HEAD_SIZE), BF),
            jax.ShapeDtypeStruct((row_blocks, ADAPTER_RANK, features), F32),
            jax.ShapeDtypeStruct((cols, ADAPTER_RANK, o_rows), F32),
        ],
        scratch_shapes=[pltpu.VMEM((own, MODEL_WIDTH), BF), pltpu.VMEM((own, LANES), BF)],
        compiler_params=pltpu.CompilerParams(vmem_limit_bytes=VMEM_LIMIT),
        cost_estimate=pl.CostEstimate(
            flops=2 * own * MODEL_WIDTH * MODEL_WIDTH,
            bytes_accessed=2 * MODEL_WIDTH * MODEL_WIDTH,
            transcendentals=own,
        ),
        name="output_backward",
    )(
        grad_hidden,
        got,
        cotangent,
        middle,
        gain,
        inmaps,
        outmaps,
        attended,
        masked,
        *[weights] * len(specs),
    )


def feed_forward_kernel(
    first, last, h_ref, c_ref, mg_ref, mu_ref, nd_ref, mask_ref, ag_ref, au_ref, od_ref, *refs
):
    weight_refs, map_refs, refs = refs[:2], refs[2:4], refs[4:]
    if first:
        previous = None
    else:
        previous, refs = refs[:5], refs[5:]
    if last:
        (gh_ref, out_ref, rows_ref), refs = refs[:3], refs[3:]
    else:
        accs, refs = refs[:5], refs[5:]
    grads_refs, refs = refs[:2], refs[2:]
    gh_acc, out_acc, md_acc, ig_acc, iu_acc = scratch = refs[:5]
    sems = refs[5]
    step = pl.program_id(0)
    row_blocks = weight_refs[0].shape[1]
    deep = MODEL_WIDTH // row_blocks
    used = mg_ref.shape[1]

    @pl.when(step == 0)
    def _():
        if first:
            for ref in scratch:
                ref[...] = jnp.zeros_like(ref)
        else:
            copies = [
                pltpu.make_async_copy(previous[i], scratch[i], sems.at[i]) for i in range(5)
            ]
            for copy in copies:
                copy.start()
            for copy in copies:
                copy.wait()

    def side(kind, row):
        return jnp.concatenate([ref[0, row, kind] for ref in weight_refs], axis=1)

    def tall_side(kind):
        return jnp.concatenate([side(kind, row) for row in range(row_blocks)], axis=0)

    def down_side(row):
        return jnp.concatenate(
            [
                jnp.concatenate(
                    [ref[0, row, 2, at : at + LANES, :] for at in range(0, deep, LANES)], axis=1
                )
                for ref in weight_refs
            ],
            axis=0,
        )

    def maps(kind):
        return jnp.concatenate(
            [ref[0, kind * used : (kind + 1) * used, :] for ref in map_refs], axis=1
        )

    gate_map, up_map, down_map = maps(0), maps(1), maps(2)
    gate = dot(h_ref[...], tall_side(0)) + ADAPTER_FACTOR * dot(mg_ref[...], gate_map)
    upward = dot(h_ref[...], tall_side(1)) + ADAPTER_FACTOR * dot(mu_ref[...], up_map)
    down = jnp.concatenate([down_side(row) for row in range(row_blocks)], axis=1)
    grad_act = dot_nt(c_ref[...], down) + dot(nd_ref[...], down_map)
    sigma = 1.0 / (1.0 + jnp.exp(-gate))
    swish = gate * sigma
    act = (swish * upward).astype(BF)
    grad_gate = (grad_act * upward * (sigma * (1.0 + gate * (1.0 - sigma)))).astype(BF)
    grad_up = (grad_act * swish).astype(BF)
    both = jnp.concatenate([grad_gate, grad_up], axis=1)
    for row in range(row_blocks):
        at = slice(row * deep, (row + 1) * deep)
        gh_acc[:, at] += dot_nt(both, jnp.concatenate([side(0, row), side(1, row)], axis=1))
        out_acc[:, at] += dot(act, down_side(row))
    md_acc[...] += dot_nt(act, down_map)
    ig_acc[...] += dot_nt(grad_gate, gate_map)
    iu_acc[...] += dot_nt(grad_up, up_map)
    partial = (
        ADAPTER_FACTOR * dot_tn(mg_ref[...], grad_gate),
        ADAPTER_FACTOR * dot_tn(mu_ref[...], grad_up),
        dot_tn(nd_ref[...], act),
    )
    for kind in range(3):
        for i, ref in enumerate(grads_refs):
            ref[0, kind * used : (kind + 1) * used, :] = partial[kind][
                :, i * LANES : (i + 1) * LANES
            ]

    @pl.when(step == pl.num_programs(0) - 1)
    def _():
        if last:
            mask = mask_ref[...]
            inner_g = (ADAPTER_FACTOR * ig_acc[...] * mask).astype(BF)
            inner_u = (ADAPTER_FACTOR * iu_acc[...] * mask).astype(BF)
            masked = (md_acc[...] * mask).astype(BF)
            gh_ref[...] = (
                gh_acc[...] + dot_nt(inner_g, ag_ref[...]) + dot_nt(inner_u, au_ref[...])
            ).astype(gh_ref.dtype)
            out_ref[...] = (out_acc[...] + ADAPTER_FACTOR * dot_nt(masked, od_ref[...])).astype(
                out_ref.dtype
            )
            for row in range(row_blocks):
                at = slice(row * deep, (row + 1) * deep)
                rows_ref[row, :used, :] = dot_tn(inner_g, h_ref[:, at])
                rows_ref[row, used : 2 * used, :] = dot_tn(inner_u, h_ref[:, at])
                rows_ref[row, 2 * used :, :] = ADAPTER_FACTOR * dot_tn(masked, c_ref[:, at])
        else:
            copies = [pltpu.make_async_copy(scratch[i], accs[i], sems.at[i]) for i in range(5)]
            for copy in copies:
                copy.start()
            for copy in copies:
                copy.wait()


def feed_forward_chunk(hidden, cotangent, masks, tables, weights, maps, previous, last, dtype):
    first = previous is None
    cols, row_blocks, _, deep, _ = weights.shape
    slabs = maps.shape[0] // cols
    count, used = masks[0].shape
    whole = lambda i: (0, 0)
    once = pl.Buffered(1)
    steps = cols * slabs // 2
    acc_shapes = [(count, MODEL_WIDTH)] * 2 + [(count, used)] * 3

    def weight_spec(side):
        def at(i):
            return ((2 * i + side) // slabs, 0, (2 * i + side) % slabs, 0, 0)

        return pl.BlockSpec((1, row_blocks, 3, deep, LANES), at)

    def slab_spec(side):
        return pl.BlockSpec((1, 3 * used, LANES), lambda i: (2 * i + side, 0, 0))

    def half_spec(side):
        return pl.BlockSpec((1, 3 * used, LANES), lambda i: (i, 0, 0))

    in_specs = (
        [pl.BlockSpec((count, MODEL_WIDTH), whole, pipeline_mode=once)] * 2
        + [pl.BlockSpec((count, used), whole)] * 4
        + [pl.BlockSpec((MODEL_WIDTH, used), whole, pipeline_mode=once)] * 3
        + [weight_spec(0), weight_spec(1), slab_spec(0), slab_spec(1)]
    )
    operands = [hidden, cotangent, *masks, *tables, weights, weights, maps, maps]
    if not first:
        in_specs = in_specs + [pl.BlockSpec(memory_space=pl.ANY)] * 5
        operands = operands + list(previous)
    if last:
        out_specs = [pl.BlockSpec((count, MODEL_WIDTH), whole)] * 2 + [
            pl.BlockSpec((row_blocks, 3 * used, deep), lambda i: (0, 0, 0))
        ]
        out_shape = [jax.ShapeDtypeStruct(s, dtype) for s in acc_shapes[:2]] + [
            jax.ShapeDtypeStruct((row_blocks, 3 * used, deep), F32)
        ]
    else:
        out_specs = [pl.BlockSpec(memory_space=pl.ANY)] * 5
        out_shape = [jax.ShapeDtypeStruct(s, F32) for s in acc_shapes]
    outs = pl.pallas_call(
        functools.partial(feed_forward_kernel, first, last),
        grid=(steps,),
        in_specs=in_specs,
        out_specs=out_specs + [half_spec(0), half_spec(1)],
        out_shape=out_shape + [jax.ShapeDtypeStruct((steps, 3 * used, LANES), F32)] * 2,
        scratch_shapes=[pltpu.VMEM(s, F32) for s in acc_shapes]
        + [pltpu.SemaphoreType.DMA((5,))],
        compiler_params=pltpu.CompilerParams(vmem_limit_bytes=VMEM_LIMIT),
        cost_estimate=pl.CostEstimate(
            flops=24 * count * MODEL_WIDTH * steps * LANES,
            bytes_accessed=steps * row_blocks * 6 * deep * LANES * 2,
            transcendentals=count * steps * 2 * LANES,
        ),
        name="feed_forward",
    )(*operands)
    return outs[:-2], outs[-2:]


def place(first, first_at, second, second_at, columns):
    index = jnp.arange(columns)[:, None] // ADAPTER_RANK
    copies = columns // ADAPTER_RANK
    return jnp.where(index == first_at, jnp.tile(first, (copies, 1)), 0.0) + jnp.where(
        index == second_at, jnp.tile(second, (copies, 1)), 0.0
    )


def lane_pad(values):
    return jnp.pad(values, ((0, 0),) * (values.ndim - 1) + ((0, LANES - values.shape[-1]),))


def row_pad(values):
    return jnp.pad(
        values, ((0, 0),) * (values.ndim - 2) + ((0, LANES - values.shape[-2]), (0, 0))
    )


def thirds(values):
    parts = []
    for _ in range(3):
        part = lax.reduce_precision(values, 8, 7)
        parts.append(part.astype(BF)[:, None])
        values = values - part
    return parts


def summed(values, axis):
    size = lax.axis_size(axis)
    bit = 1
    while bit < size:
        pairs = [(i, i ^ bit) for i in range(size)]
        values = values + lax.ppermute(values, axis, pairs)
        bit = 2 * bit
    return values


def summed_block(blocks, axis):
    size = lax.axis_size(axis)
    at = lax.axis_index(axis)
    bit = size // 2
    while bit:
        pairs = [(i, i ^ bit) for i in range(size)]
        halves = blocks.reshape(2, bit, *blocks.shape[1:])
        upper = (at // bit) % 2
        kept = lax.dynamic_index_in_dim(halves, upper, 0, False)
        sent = lax.dynamic_index_in_dim(halves, 1 - upper, 0, False)
        blocks = kept + lax.ppermute(sent, axis, pairs)
        bit = bit // 2
    return blocks[0]


def on_device(
    tokens,
    cotangent,
    attention_norm_gain,
    feedfwd_norm_gain,
    query_norm_gain,
    key_norm_gain,
    query_matrix,
    key_matrix,
    value_matrix,
    output_matrix,
    gate_matrix,
    up_matrix,
    down_matrix,
    query_adapter_inmaps,
    query_adapter_outmaps,
    key_adapter_inmaps,
    key_adapter_outmaps,
    value_adapter_inmaps,
    value_adapter_outmaps,
    output_adapter_inmaps,
    output_adapter_outmaps,
    gate_adapter_inmaps,
    gate_adapter_outmaps,
    up_adapter_inmaps,
    up_adapter_outmaps,
    down_adapter_inmaps,
    down_adapter_outmaps,
    segment,
    depth,
    parent,
    adapter,
):
    rows = lax.axis_size("row")
    cols = lax.axis_size("col")
    devices = rows * cols
    repeat = devices // QUERY_HEADS
    plane = lax.axis_index("dp")
    row = lax.axis_index("row")
    col = lax.axis_index("col")
    length = segment.shape[0]
    own = tokens.shape[0] // rows
    columns = query_adapter_inmaps.shape[1]
    rank = ADAPTER_RANK
    swap = [(0, 1), (1, 0)]
    pairs = [(r, r ^ repeat) for r in range(rows)]
    q_local = query_matrix.shape[1]
    kv_local = key_matrix.shape[1]
    wide = q_local + 2 * kv_local
    features = gate_matrix.shape[0]

    own_adapter = adapter[0]
    other_adapter = lax.ppermute(adapter, "dp", swap)[0]
    both = (own_adapter, other_adapter)

    def inmap(table, at):
        return lax.dynamic_slice_in_dim(table, at * rank, rank, 1)

    def outmap(table, at):
        return lax.dynamic_slice_in_dim(table, at * rank, rank, 0)

    qkv_local = jnp.concatenate([query_matrix, key_matrix, value_matrix], axis=1)

    def block_of(table, before, after):
        return jnp.pad(outmap(table, own_adapter), ((0, 0), (before, after)))

    qkv_maps = jnp.concatenate(
        [
            block_of(query_adapter_outmaps, 0, 2 * kv_local),
            block_of(key_adapter_outmaps, q_local, kv_local),
            block_of(value_adapter_outmaps, q_local + kv_local, 0),
        ],
        axis=0,
    )
    attention_pack = jnp.concatenate(
        [
            table[:, at : at + features]
            for table in (qkv_local, qkv_maps)
            for at in range(0, wide, features)
        ],
        axis=0,
    )
    attention_weights = lax.all_gather(attention_pack, PLANE, axis=0, tiled=True).reshape(
        cols, rows, -1, features
    )
    o_rows = output_matrix.shape[0]
    ffn_half = gate_matrix.shape[1] // 2
    half_start = plane * ffn_half
    chunks = 2 if ffn_half % 256 == 0 else 3
    width = ffn_half // chunks
    slabs = width // LANES

    def plates(table):
        return [table[:, at : at + LANES] for at in range(0, table.shape[1], LANES)]

    def half_of(table):
        return lax.dynamic_slice_in_dim(table, half_start, ffn_half, 1)

    map_width = max(ffn_half, o_rows)

    def to_width(table):
        return jnp.pad(table, ((0, 0), (0, map_width - table.shape[1])))

    col_pack = jnp.concatenate(
        [
            *[to_width(half_of(outmap(gate_adapter_outmaps, a))) for a in both],
            *[to_width(half_of(outmap(up_adapter_outmaps, a))) for a in both],
            *[to_width(half_of(inmap(down_adapter_inmaps, a).T)) for a in both],
            to_width(inmap(output_adapter_inmaps, own_adapter).T),
            jnp.zeros((rank, map_width), BF),
        ],
        axis=0,
    )
    map_rows = col_pack.shape[0] // rows
    map_plates = plates(lax.dynamic_slice_in_dim(col_pack, row * map_rows, map_rows, 0))
    ffn_weights = []
    for chunk in range(chunks):
        pack = []
        for slab in range(slabs):
            start = half_start + (chunk * slabs + slab) * LANES
            pack.append(lax.dynamic_slice_in_dim(gate_matrix, start, LANES, 1))
            pack.append(lax.dynamic_slice_in_dim(up_matrix, start, LANES, 1))
            pack.extend(plates(lax.dynamic_slice_in_dim(down_matrix, start, LANES, 0)))
        if chunk == 0:
            spare = features - map_rows * len(map_plates)
            for plate in plates(output_matrix):
                pack.append(jnp.pad(plate, ((0, features - o_rows), (0, 0))))
            pack = pack + map_plates + [jnp.zeros((spare, LANES), BF)]
        pack = jnp.concatenate(pack, axis=0)
        ffn_weights.append(
            lax.all_gather(pack, PLANE, axis=0, tiled=True).reshape(
                cols, rows, -1, features, LANES
            )
        )
    o_unit = 3 * slabs
    col_maps = ffn_weights[0][:, :, -1, : map_rows * len(map_plates)].reshape(
        cols, rows, len(map_plates), map_rows, LANES
    )
    col_maps = jnp.transpose(col_maps, (0, 2, 1, 3, 4)).reshape(
        cols, len(map_plates), rows * map_rows, LANES
    )
    in_o = jnp.transpose(col_maps[:, : o_rows // LANES, 6 * rank : 7 * rank], (0, 2, 1, 3))
    in_o = row_pad(in_o.reshape(cols, rank, o_rows))

    row_pack = jnp.concatenate(
        [
            inmap(query_adapter_inmaps, own_adapter),
            inmap(key_adapter_inmaps, own_adapter),
            inmap(value_adapter_inmaps, own_adapter),
            *[inmap(gate_adapter_inmaps, a) for a in both],
            *[inmap(up_adapter_inmaps, a) for a in both],
            *[outmap(down_adapter_outmaps, a).T for a in both],
            outmap(output_adapter_outmaps, own_adapter).T,
            *thirds(attention_norm_gain),
            *thirds(feedfwd_norm_gain),
        ],
        axis=1,
    )

    row_maps = lax.all_gather(row_pack, "row", axis=0, tiled=True)
    in_qkv = row_maps[:, : 3 * rank]
    in_gate = row_maps[:, 3 * rank : 5 * rank]
    in_up = row_maps[:, 5 * rank : 7 * rank]
    out_down = row_maps[:, 7 * rank : 9 * rank]
    out_o = lane_pad(row_maps[:, 9 * rank : 10 * rank])
    gain_parts = row_maps[:, 10 * rank :].astype(F32)
    gain_one = (gain_parts[:, 0] + (gain_parts[:, 1] + gain_parts[:, 2])).reshape(1, -1)
    gain_two = (gain_parts[:, 3] + (gain_parts[:, 4] + gain_parts[:, 5])).reshape(1, -1)

    own_tokens = lax.all_to_all(tokens, "row", 0, 1, tiled=True)
    own_cotangent = lax.all_to_all(cotangent, "row", 0, 1, tiled=True)
    other_cotangent = lax.ppermute(own_cotangent, "dp", swap)
    head_gains = jnp.stack([query_norm_gain, key_norm_gain], axis=0)
    token_start = (col * rows + row) * own
    positions = lax.dynamic_slice_in_dim(depth, token_start, own, 0).astype(F32)
    half = HEAD_SIZE // 2
    freqs = THETA ** (-2.0 * jnp.arange(half).astype(F32) / HEAD_SIZE)
    angle = positions[:, None] * freqs[None, :]
    cosine = jnp.tile(jnp.cos(angle), (1, 2))
    sine = jnp.concatenate([-jnp.sin(angle), jnp.sin(angle)], axis=1)

    masked_qkv, pre, sent = qkv_forward(
        own_tokens, gain_one, in_qkv, cosine, sine, head_gains, attention_weights
    )

    def to_heads(sent):
        if repeat > 1:
            sent = jnp.repeat(sent, repeat, axis=0)
        return lax.all_to_all(sent, PLANE, 0, 0, tiled=True).reshape(length, sent.shape[2])

    def to_tokens(lines):
        got = lax.all_to_all(
            lines.reshape(devices, own, lines.shape[1]), PLANE, 0, 0, tiled=True
        )
        return got[::repeat] if repeat > 1 else got

    got = to_heads(sent)
    theirs = lax.ppermute(got[:, HEAD_SIZE:], "row", pairs)
    flag = (1 - (row // repeat) % 2).astype(jnp.int32).reshape(1)

    block_node = segment.reshape(-1, SEG_LEN)[:, 0]
    nodes = jnp.arange(parent.shape[1])
    node_parent = jnp.sum(jnp.where(block_node[:, None] == nodes, parent.reshape(1, -1), 0), axis=1)
    block_index = jnp.arange(block_node.shape[0])
    parent_block = jnp.max(
        jnp.where(node_parent[:, None] == block_node[None, :], block_index[None, :], 0), axis=1
    )
    parent_block = jnp.where(node_parent > 0, parent_block, -1).astype(jnp.int32)
    head_attended, head_low, totals = attention_forward(parent_block, flag, got, theirs)
    attended = to_tokens(head_low)

    middle, hidden_ffn, masked_o = output_forward(
        attended, own_tokens, gain_two, in_o, out_o, ffn_weights[0], o_unit
    )

    other_ffn = lax.ppermute(hidden_ffn, "dp", swap)
    tables = (in_gate, in_up, out_down)
    column_tree = jnp.arange(2 * rank)[None, :] // rank

    def masks_of(hidden, cot, tree):
        mask = jnp.broadcast_to((column_tree == tree).astype(F32), (own, 2 * rank))
        return (
            (dot(hidden, in_gate) * mask).astype(BF),
            (dot(hidden, in_up) * mask).astype(BF),
            (ADAPTER_FACTOR * dot(cot, out_down) * mask).astype(BF),
            mask,
        )

    parts = []

    def run(chunk, side, masks, accs):
        hidden, cot = side
        maps = col_maps[:, chunk * slabs : (chunk + 1) * slabs].reshape(cols * slabs, -1, LANES)
        last = chunk == chunks - 1
        return feed_forward_chunk(
            hidden,
            cot,
            masks,
            tables,
            ffn_weights[chunk],
            maps,
            accs,
            last,
            F32 if side is own_side else BF,
        )

    own_side = (hidden_ffn, own_cotangent)
    own_masks = masks_of(*own_side, 0)
    here, own_part = run(0, own_side, own_masks, None)
    other_ffn, here = lax.optimization_barrier((other_ffn, here))
    other_side = (other_ffn, other_cotangent)
    other_masks = masks_of(*other_side, 1)
    there, other_part = run(0, other_side, other_masks, None)
    parts = [(own_part, other_part)]
    for chunk in range(1, chunks):
        there, other_part = run(chunk, other_side, other_masks, there)
        here, own_part = run(chunk, own_side, own_masks, here)
        parts.append((own_part, other_part))

    def slab_order(part):
        even, odd = (part[0][i] + part[1][i] for i in range(2))
        part = jnp.stack([even, odd], axis=1).reshape(cols, slabs, 6 * rank, LANES)
        return jnp.transpose(part, (0, 2, 1, 3)).reshape(cols, 6 * rank, width)

    parts = [slab_order(part) for part in parts]
    gh_other = lax.ppermute(there[0], "dp", swap)

    grad_middle, sent, grad_o_rows, grad_o_cols = output_backward(
        here[0],
        gh_other,
        own_cotangent,
        middle,
        gain_two,
        in_o,
        out_o,
        attended,
        masked_o,
        ffn_weights[0],
        o_unit,
    )
    out_sent, sent = lax.optimization_barrier((there[1], sent))
    out_other = lax.ppermute(out_sent, "dp", swap)
    head_grad = to_heads(sent)

    row_mid = jnp.concatenate([here[2] + there[2], grad_o_rows], axis=1).reshape(-1, features)

    def to_map_width(table):
        return jnp.pad(table, ((0, 0), (0, 0), (0, map_width - table.shape[2])))

    col_mid = jnp.concatenate(
        [to_map_width(jnp.concatenate(parts, axis=2)), to_map_width(grad_o_cols)], axis=1
    ).reshape(-1, map_width)
    head_grad, row_mid, col_mid = lax.optimization_barrier((head_grad, row_mid, col_mid))
    row_mid = lax.psum_scatter(row_mid, "row", scatter_dimension=0, tiled=True)
    col_mid = lax.psum_scatter(col_mid, "col", scatter_dimension=0, tiled=True)

    lines, kept, given = attention_backward(
        parent_block, flag, got, head_grad, head_attended, totals, theirs
    )
    lines, kept, given, row_mid, col_mid, out_other = lax.optimization_barrier(
        (lines, kept, given, row_mid, col_mid, out_other)
    )
    returned = to_tokens(merge(lines, kept, lax.ppermute(given, "row", pairs)))
    output = (middle + here[1] + out_other.astype(F32)).astype(BF)
    row_mid = summed(row_mid, "col")
    col_mid = summed(col_mid, "row")
    row_got, col_got = lax.ppermute((row_mid, col_mid), "dp", swap)
    returned, row_mid, col_mid, row_got, col_got, output = lax.optimization_barrier(
        (returned, row_mid, col_mid, row_got, col_got, output)
    )
    output = lax.all_to_all(output, "row", 1, 0, tiled=True)

    grads_qkv, inner_qkv, row_end, col_end = qkv_unshape(
        returned,
        pre,
        masked_qkv,
        own_tokens,
        gain_one,
        cosine,
        sine,
        head_gains,
        attention_weights,
    )
    grad_low = qkv_backward(
        grads_qkv, inner_qkv, own_tokens, grad_middle, gain_one, in_qkv, attention_weights
    )
    grad_low, output = lax.optimization_barrier((grad_low, output))
    input_gradient = lax.all_to_all(grad_low, "row", 1, 0, tiled=True).astype(F32)
    row_end = summed(summed_block(row_end, "row"), "col")
    col_end = summed(summed_block(col_end, "col"), "row")
    row_end_got, col_end_got = lax.ppermute((row_end, col_end), "dp", swap)

    def placed(first, second):
        return place(first, own_adapter, second, other_adapter, columns)

    def row_sum(at):
        first = row_mid[at : at + rank] + row_got[at + rank : at + 2 * rank]
        second = row_mid[at + rank : at + 2 * rank] + row_got[at : at + rank]
        return placed(first, second)

    grad_a_gate = row_sum(0).T
    grad_a_up = row_sum(2 * rank).T
    grad_b_down = row_sum(4 * rank)
    grad_b_o = placed(row_mid[6 * rank :], row_got[6 * rank :])
    at = 6 * rank
    grad_a_o = placed(col_mid[at:, :o_rows], col_got[at:, :o_rows]).T

    def ffn_placed(kind):
        at = 2 * rank * kind
        mine = placed(col_mid[at : at + rank], col_mid[at + rank : at + 2 * rank])
        theirs = placed(col_got[at + rank : at + 2 * rank], col_got[at : at + rank])
        low = jnp.where(plane == 0, mine, theirs)
        high = jnp.where(plane == 0, theirs, mine)
        return jnp.concatenate([low[:, :ffn_half], high[:, :ffn_half]], axis=1)

    grad_b_gate = ffn_placed(0)
    grad_b_up = ffn_placed(1)
    grad_a_down = ffn_placed(2).T

    grad_a_q, grad_a_k, grad_a_v = (
        placed(row_end[i * rank : (i + 1) * rank], row_end_got[i * rank : (i + 1) * rank]).T
        for i in range(3)
    )
    grad_b = placed(col_end, col_end_got)
    grad_b_q = grad_b[:, :q_local]
    grad_b_k = grad_b[:, q_local : q_local + kv_local]
    grad_b_v = grad_b[:, q_local + kv_local :]

    return (
        output,
        input_gradient,
        grad_a_q,
        grad_b_q,
        grad_a_k,
        grad_b_k,
        grad_a_v,
        grad_b_v,
        grad_a_o,
        grad_b_o,
        grad_a_gate,
        grad_b_gate,
        grad_a_up,
        grad_b_up,
        grad_a_down,
        grad_b_down,
    )


def solution(mesh):
    return jax.shard_map(
        on_device,
        mesh=mesh,
        in_specs=(
            P(("dp", "col"), "row"),
            P(("dp", "col"), "row"),
            P("row"),
            P("row"),
            P(),
            P(),
            P("row", "col"),
            P("row", "col"),
            P("row", "col"),
            P("col", "row"),
            P("row", "col"),
            P("row", "col"),
            P("col", "row"),
            P("row", None),
            P(None, "col"),
            P("row", None),
            P(None, "col"),
            P("row", None),
            P(None, "col"),
            P("col", None),
            P(None, "row"),
            P("row", None),
            P(None, "col"),
            P("row", None),
            P(None, "col"),
            P("col", None),
            P(None, "row"),
            P("dp"),
            P("dp"),
            P("dp", None),
            P("dp"),
        ),
        out_specs=(
            P(("dp", "col"), "row"),
            P(("dp", "col"), "row"),
            P("row", None),
            P(None, "col"),
            P("row", None),
            P(None, "col"),
            P("row", None),
            P(None, "col"),
            P("col", None),
            P(None, "row"),
            P("row", None),
            P(None, "col"),
            P("row", None),
            P(None, "col"),
            P("col", None),
            P(None, "row"),
        ),
        check_vma=False,
    )
```

time: 1130 us -> 832 us (0.74)
  waiting for transfers between devices: 407 us -> 223 us
  Pallas kernels: 196 us -> 270 us
  matrix products: 77.9 us -> 13 us
  local copies, waits for them, and re-layouts: 132 us -> 83.4 us
  other arithmetic: 74.6 us -> 27.2 us
  blocking collectives: 169 us -> 128 us
  starting transfers between devices: 47.4 us -> 59.7 us
    all_to_all x2, waiting for transfers between devices: 89.3 us -> 0.01 us  [to_tokens(): lax.all_to_all(lines.reshape(devices, own, lines.shape[1]), PLANE, 0, 0,...]
    psum x2 -> x0, waiting for transfers between devices: 84.4 us -> none  [the longest x1 54.3 us: over_rows(): return lax.psum(mine, 'col')]
    pallas_call x3 -> x10, Pallas kernels: 110 us -> 182 us  [the longest x4 113 us: feed_forward_chunk(): pl.pallas_call(functools.partial(feed_forward_kernel, first, last), grid=...]
    all_gather x2 -> x0, blocking collectives: 65.8 us -> none  [the longest x1 41.1 us: on_device(): col_maps = lax.all_gather(col_pack, 'col', axis=0, tiled=False)]
    dot_general x24 -> x0, matrix products: 48.6 us -> none  [the longest x16 39.5 us: dot_nt(): lax.dot_general(left, right, (((1,), (1,)), ((), ())), preferred_element_...]
    all_gather x3 -> x2, waiting for transfers between devices: 84.2 us -> 58 us  [on_device(): lax.all_gather(pack, PLANE, axis=0, tiled=True)]
    ppermute x1, waiting for transfers between devices: 0.01 us -> 25.9 us  [on_device(): other_cotangent = lax.ppermute(own_cotangent, 'dp', swap)]
    ppermute x6 -> x20, waiting for transfers between devices: 55.8 us -> 79.3 us  [the longest x8 63 us: summed(): values = values + lax.ppermute(values, axis, pairs)]
  transfers between devices with their start and end apart: 25 -> 35, of which waited for: 14 -> 14; matrix products, arithmetic and copies ran while one was open for 20% -> 12% of each run, Pallas kernels for 10% -> 27%
where the time goes in v2:
time: 832 us; the launch traced here: 821 us
  Pallas kernels  270 us (32%)
  waiting for transfers between devices  223 us (27%)
  blocking collectives  128 us (15%)
  local copies, waits for them, and re-layouts  83.4 us (10%)
  starting transfers between devices  59.7 us (7%)
  other arithmetic  27.2 us (3%)
  between operations  16.8 us (2%)
  matrix products  13 us (2%)
    pallas_call x4, Pallas kernels, feed_forward_chunk(): pl.pallas_call(functools.partial(feed_forward_kernel, first, last), grid=...  113 us
    all_to_all x1, blocking collectives, to_heads(): lax.all_to_all(sent, PLANE, 0, 0, tiled=True).reshape(length, sent.shape[2])  95 us
    ppermute x8, waiting for transfers between devices, summed(): values = values + lax.ppermute(values, axis, pairs)  63 us
    all_gather x2, waiting for transfers between devices, on_device(): lax.all_gather(pack, PLANE, axis=0, tiled=True)  58 us
    pallas_call x1, Pallas kernels, attention_backward(): pl.pallas_call(attention_backward_kernel, grid_spec=pltpu.PrefetchScalarG...  52.9 us
    unnamed x173, local copies, waits for them, and re-layouts  43.8 us
    pallas_call x1, Pallas kernels, attention_forward(): pl.pallas_call(attention_forward_kernel, grid_spec=pltpu.PrefetchScalarGr...  35.3 us
    all_gather x1, blocking collectives, on_device(): row_maps = lax.all_gather(row_pack, 'row', axis=0, tiled=True)  32.8 us
  transfers between devices with their start and end apart: 35, of which 14 were waited for; matrix products, arithmetic and copies ran while one was open for 12% of the time, Pallas kernels for 27%

profile of v2, /device:TPU:0, one launch (start us, length us, event | category | flops | bytes accessed | tf_op | source)
XLA Modules:
  0.0 820.9 jit_solution(10321764536500015759)
XLA Ops:
  62.6 32.8 %all_gather.12 = bf16[2048,166]{1,0:T(8,128)(2,1)S(1)} all-gather(bf16[512,166]{1,0:T(8,128)(2,1)S(1)} %concatenate.42), channel_id=1, replica_groups=mesh['dp'=2,'row'=4,'col'=4] {'row'}, dimensions={0}, use_global_device_ids=true | all-gather | bytes 849920 | tf_op jit(solution)/shard_map/all_gather | solution.py:1165
  100.7 29.3 %all-gather.4.cloned.1.call-done = bf16[17920,512]{1,0:T(8,128)(2,1)} async-done(((bf16[1120,512]{1,0:T(8,128)(2,1)}), bf16[17920,512]{1,0:T(8,128)(2,1)}) %all-gather.4.cloned.1.call-update) | async-done | bytes 18350096 | tf_op jit(solution)/shard_map/all_gather | solution.py:1088
  130.0 18.0 %qkv_forward.1 = (bf16[320,48]{1,0:T(8,128)(2,1)}, f32[4,320,768]{2,1,0:T(8,128)}, bf16[16,320,256]{2,1,0:T(8,128)(2,1)}) custom-call(bf16[320,2048]{1,0:T(8,128)(2,1)} %bitcast.305, f32[1,2048]{1,0:T(1,128)} %bitcast.357, bf16[2048,48]{1,0:T(8,128)(2,1)} %slice.375.a_ref, f32[320,128]{1,0:T(8,128)} %copy.285.cos_ref, f32[320,128]{1,0:T(8,128)} %pad_maximum_fusion.6.sin_ref, ...), custom_call_target="tpu_custom_call" | custom-call | flops 5368709120 | bytes 16777216 | tf_op jit(solution)/shard_map/qkv_forward/pallas_call | solution.py:395
  148.0 95.0 %all_to_all.90 = bf16[16,320,256]{2,1,0:T(8,128)(2,1)S(1)} all-to-all(bf16[16,320,256]{2,1,0:T(8,128)(2,1)} %get-tuple-element.85), channel_id=1, replica_groups=mesh['dp'=2,'row'=4,'col'=4] {'col','row'}, dimensions={0} | all-to-all | bytes 5242880 | tf_op jit(solution)/shard_map/all_to_all | solution.py:1194
  251.6 35.3 %attention_forward.1 = (f32[5120,128]{1,0:T(8,128)}, bf16[5120,128]{1,0:T(8,128)(2,1)}, f32[20,8,256]{2,1,0:T(8,128)}) custom-call(s32[20]{0:T(128)} %compare_select_fusion.parent_ref, s32[1]{0:T(128)} %bitcast.1.flag_ref, bf16[5120,256]{1,0:T(8,128)(2,1)} %bitcast.324, bf16[5120,256]{1,0:T(8,128)(2,1)} %bitcast.325, bf16[5120,128]{1,0:T(8,128)(2,1)} %copy-done.60), custom_call_target="tpu_custom_call" | custom-call | flops 5368709120 | bytes 7864320 | tf_op jit(solution)/shard_map/attention_forward/pallas_call | solution.py:110
  298.5 25.9 %collective-permute-done.3.c_ref = bf16[320,2048]{1,0:T(8,128)(2,1)S(1)} collective-permute-done((bf16[320,2048]{1,0:T(8,128)(2,1)S(1)}, bf16[320,2048]{1,0:T(8,128)(2,1)S(1)}, u32[]{:S(2)}, u32[]{:S(2)}) %collective-permute-start.3) | collective-permute-done | bytes 1310752 | tf_op jit(solution)/shard_map/ppermute | solution.py:1177
  326.6 25.7 %all-gather.6.cloned.1.call-done = bf16[114688,128]{1,0:T(8,128)(2,1)} async-done(((bf16[7168,128]{1,0:T(8,128)(2,1)}), bf16[114688,128]{1,0:T(8,128)(2,1)}) %all-gather.6.cloned.1.call-update) | async-done | bytes 29360144 | tf_op jit(solution)/shard_map/all_gather | solution.py:1136
  354.4 9.9 %output_forward.1 = (f32[320,2048]{1,0:T(8,128)}, bf16[320,2048]{1,0:T(8,128)(2,1)}, bf16[320,128]{1,0:T(8,128)(2,1)}) custom-call(bf16[16,320,128]{2,1,0:T(8,128)(2,1)} %all-to-all-done.2.att_ref, bf16[320,2048]{1,0:T(8,128)(2,1)} %bitcast.306, f32[1,2048]{1,0:T(1,128)} %bitcast.360, bf16[4,128,512]{2,1,0:T(8,128)(2,1)} %pad.32.a_ref, ...), custom_call_target="tpu_custom_call" | custom-call | flops 2684354560 | bytes 8388608 | tf_op jit(solution)/shard_map/output_forward/pallas_call | solution.py:650
  372.7 26.3 %feed_forward.4 = (f32[320,2048]{1,0:T(8,128)}, f32[320,2048]{1,0:T(8,128)}, f32[320,32]{1,0:T(8,128)}, f32[320,32]{1,0:T(8,128)}, f32[320,32]{1,0:T(8,128)}, /*...) custom-call(bf16[320,2048]{1,0:T(8,128)(2,1)} %get-tuple-element.87.h_ref, bf16[320,2048]{1,0:T(8,128)(2,1)} %bitcast.311, ...), custom_call_target="tpu_custom_call" | custom-call | flops 12079595520 | bytes 18874368 | tf_op jit(solution)/shard_map/feed_forward/pallas_call | solution.py:935
  405.0 26.7 %feed_forward.5 = (f32[320,2048]{1,0:T(8,128)}, f32[320,2048]{1,0:T(8,128)}, f32[320,32]{1,0:T(8,128)}, f32[320,32]{1,0:T(8,128)}, f32[320,32]{1,0:T(8,128)}, /*...) custom-call(bf16[320,2048]{1,0:T(8,128)(2,1)} %collective-permute-done.2.h_ref, bf16[320,2048]{1,0:T(8,128)(2,1)} %copy-done.10, ...), custom_call_target="tpu_custom_call" | custom-call | flops 12079595520 | bytes 18874368 | tf_op jit(solution)/shard_map/feed_forward/pallas_call | solution.py:935
  431.7 32.4 %all-gather.8.cloned.1.call-done = bf16[73728,128]{1,0:T(8,128)(2,1)} async-done(((bf16[4608,128]{1,0:T(8,128)(2,1)}), bf16[73728,128]{1,0:T(8,128)(2,1)}) %all-gather.8.cloned.1.call-update) | async-done | bytes 18874384 | tf_op jit(solution)/shard_map/all_gather | solution.py:1136
  464.1 29.4 %feed_forward.6 = (bf16[320,2048]{1,0:T(8,128)(2,1)}, bf16[320,2048]{1,0:T(8,128)(2,1)}, f32[4,96,512]{2,1,0:T(8,128)}, f32[6,96,128]{2,1,0:T(8,128)}, f32[6,96,128]{2,1,0:T(8,128)}) custom-call(bf16[320,2048]{1,0:T(8,128)(2,1)} %collective-permute-done.2.h_ref, bf16[320,2048]{1,0:T(8,128)(2,1)} %copy-done.10, bf16[320,32]{1,0:T(8,128)(2,1)} %fusion.2.mg_ref, ...), custom_call_target="tpu_custom_call" | custom-call | flops 12079595520 | bytes 18874368 | tf_op jit(solution)/shard_map/feed_forward/pallas_call | solution.py:935
  495.0 30.2 %feed_forward.7 = (f32[320,2048]{1,0:T(8,128)}, f32[320,2048]{1,0:T(8,128)}, f32[4,96,512]{2,1,0:T(8,128)}, f32[6,96,128]{2,1,0:T(8,128)}, f32[6,96,128]{2,1,0:T(8,128)}) custom-call(bf16[320,2048]{1,0:T(8,128)(2,1)} %get-tuple-element.87.h_ref, bf16[320,2048]{1,0:T(8,128)(2,1)} %bitcast.312, bf16[320,32]{1,0:T(8,128)(2,1)} %fusion.mg_ref, ...), custom_call_target="tpu_custom_call" | custom-call | flops 12079595520 | bytes 18874368 | tf_op jit(solution)/shard_map/feed_forward/pallas_call | solution.py:935
  525.3 11.8 %output_backward.1 = (f32[320,2048]{1,0:T(8,128)}, bf16[16,320,128]{2,1,0:T(8,128)(2,1)}, f32[4,16,512]{2,1,0:T(8,128)}, f32[4,16,512]{2,1,0:T(8,128)}) custom-call(f32[320,2048]{1,0:T(8,128)} %get-tuple-element.105.gh_ref, bf16[320,2048]{1,0:T(8,128)(2,1)} %collective-permute-done.4.got_ref, bf16[320,2048]{1,0:T(8,128)(2,1)} %bitcast.313, ...), custom_call_target="tpu_custom_call" | custom-call | flops 2684354560 | bytes 8388608 | tf_op jit(solution)/shard_map/output_backward/pallas_call | solution.py:733
  537.2 4.9 all-to-all-start.4
  547.3 22.2 %all-to-all-done.4 = bf16[16,320,128]{2,1,0:T(8,128)(2,1)} async-done(((bf16[16,320,128]{2,1,0:T(8,128)(2,1)}), bf16[16,320,128]{2,1,0:T(8,128)(2,1)}, u32[]{:S(2)}, u32[]{:S(2)}) %all-to-all-start.4) | async-done | bytes 1310752 | tf_op jit(solution)/shard_map/all_to_all | solution.py:1194
  571.2 52.9 %attention_backward.1 = (bf16[5120,256]{1,0:T(8,128)(2,1)}, f32[5120,128]{1,0:T(8,128)}, f32[5120,128]{1,0:T(8,128)}) custom-call(s32[20]{0:T(128)} %compare_select_fusion.parent_ref, s32[1]{0:T(128)} %bitcast.1.flag_ref, bf16[5120,256]{1,0:T(8,128)(2,1)} %bitcast.326, bf16[5120,128]{1,0:T(8,128)(2,1)} %bitcast.31.g_ref, ...), custom_call_target="tpu_custom_call" | custom-call | flops 13421772800 | bytes 15728640 | tf_op jit(solution)/shard_map/attention_backward/pallas_call | solution.py:247
  624.1 7.1 reduce-scatter.5.cloned.1.call-done
  631.2 5.1 collective-permute-done.6.got_ref
  650.3 44.7 %collective-permute-done.7 = f32[112,512]{1,0:T(8,128)S(1)} collective-permute-done((f32[112,512]{1,0:T(8,128)}, f32[112,512]{1,0:T(8,128)S(1)}, u32[]{:S(2)}, u32[]{:S(2)}) %collective-permute-start.7) | collective-permute-done | bytes 229408 | tf_op jit(solution)/shard_map/ppermute | solution.py:986
  702.8 13.9 %collective-permute-done.8 = f32[112,512]{1,0:T(8,128)S(1)} collective-permute-done((f32[112,512]{1,0:T(8,128)S(1)}, f32[112,512]{1,0:T(8,128)S(1)}, u32[]{:S(2)}, u32[]{:S(2)}) %collective-permute-start.8) | collective-permute-done | bytes 229408 | tf_op jit(solution)/shard_map/ppermute | solution.py:986
  726.1 5.3 collective-permute-done.12
  740.8 10.7 %qkv_unshape.1 = (bf16[4,320,1024]{2,1,0:T(8,128)(2,1)}, bf16[320,48]{1,0:T(8,128)(2,1)}, f32[4,48,512]{2,1,0:T(8,128)}, f32[4,16,1024]{2,1,0:T(8,128)}) custom-call(bf16[16,320,256]{2,1,0:T(8,128)(2,1)} %copy-done.7, f32[4,320,768]{2,1,0:T(8,128)} %get-tuple-element.140.pre_ref, bf16[320,48]{1,0:T(8,128)(2,1)} %get-tuple-element.141.m_ref, ...), custom_call_target="tpu_custom_call" | custom-call | flops 335544320 | bytes 10485760 | tf_op jit(solution)/shard_map/qkv_unshape/pallas_call | solution.py:508
  756.7 13.6 %qkv_backward.1 = bf16[320,2048]{1,0:T(8,128)(2,1)} custom-call(bf16[4,320,1024]{2,1,0:T(8,128)(2,1)} %get-tuple-element.142.grads_ref, bf16[320,48]{1,0:T(8,128)(2,1)} %get-tuple-element.143.inner_ref, bf16[320,2048]{1,0:T(8,128)(2,1)} %bitcast.308, f32[320,2048]{1,0:T(8,128)} %get-tuple-element.144.gm_ref, f32[1,2048]{1,0:T(1,128)} %bitcast.359, ...), custom_call_target="tpu_custom_call" | custom-call | flops 5368709120 | bytes 16777216 | tf_op jit(solution)/shard_map/qkv_backward/pallas_call | solution.py:577
  (361 shorter events, 194.9 us)
Async XLA Ops:
  7.2 122.8 %all-gather.4.cloned.1.call-start = ((), (), s32[]{:S(2)}) async-start(), calls=%async_computation.10 | async-start | bytes 19496960 | tf_op jit(solution)/shard_map/all_gather | solution.py:1088
  11.2 341.1 %all-gather.6.cloned.1.call-start = ((), (), s32[]{:S(2)}) async-start(), calls=%async_computation.11 | async-start | bytes 31195136 | tf_op jit(solution)/shard_map/all_gather | solution.py:1136
  11.2 24.6 %collective-permute-start = (s32[1]{0:T(128)}, s32[1]{0:T(128)}, u32[]{:S(2)}, u32[]{:S(2)}) collective-permute-start(s32[1]{0:T(128)} %param.61), channel_id=1, source_target_pairs={{0,16},{16,0},{1,17},{17,1},{2,18},{18,2},{3,19},{19,3},{4,20},{20... | collective-permute-start | bytes 20 | tf_op jit(solution)/shard_map/ppermute | solution.py:1058
  47.2 416.9 %all-gather.8.cloned.1.call-start = ((), (), s32[]{:S(2)}) async-start(), calls=%async_computation.12 | async-start | bytes 20054016 | tf_op jit(solution)/shard_map/all_gather | solution.py:1136
  48.0 51.4 %all-to-all-start = ((bf16[4,320,512]{2,1,0:T(8,128)(2,1)}), bf16[4,320,512]{2,1,0:T(8,128)(2,1)S(1)}, u32[]{:S(2)}, u32[]{:S(2)}) async-start(bf16[4,320,512]{2,1,0:T(8,128)(2,1)} %bitcast.2), calls=%async_computation | async-start | bytes 2621440 | tf_op jit(solution)/shard_map/all_to_all | solution.py:1175
  244.7 42.2 %all-to-all-start.3 = ((bf16[4,320,512]{2,1,0:T(8,128)(2,1)}), bf16[4,320,512]{2,1,0:T(8,128)(2,1)}, u32[]{:S(2)}, u32[]{:S(2)}) async-start(bf16[4,320,512]{2,1,0:T(8,128)(2,1)} %bitcast.23), calls=%async_computation.3 | async-start | bytes 2621440 | tf_op jit(solution)/shard_map/all_to_all | solution.py:1176
  286.9 67.5 %all-to-all-start.2 = ((bf16[16,320,128]{2,1,0:T(8,128)(2,1)}), bf16[16,320,128]{2,1,0:T(8,128)(2,1)}, u32[]{:S(2)}, u32[]{:S(2)}) async-start(bf16[16,320,128]{2,1,0:T(8,128)(2,1)} %bitcast.342), calls=%async_computation.2 | async-start | bytes 2621440 | tf_op jit(solution)/shard_map/all_to_all | solution.py:1197
  292.9 31.4 %collective-permute-start.3 = (bf16[320,2048]{1,0:T(8,128)(2,1)S(1)}, bf16[320,2048]{1,0:T(8,128)(2,1)S(1)}, u32[]{:S(2)}, u32[]{:S(2)}) collective-permute-start(bf16[320,2048]{1,0:T(8,128)(2,1)S(1)} %bitcast.309), channel_id=1, source_target_pairs={{0,16},{16,0},{1,17},{17,1},{2,18},{18,2},{3,19},{19,3},{4,20},{20... | collective-permute-start | bytes 3932168 | tf_op jit(solution)/shard_map/ppermute | solution.py:1177
  364.3 34.7 %collective-permute-start.2 = (bf16[320,2048]{1,0:T(8,128)(2,1)}, bf16[320,2048]{1,0:T(8,128)(2,1)}, u32[]{:S(2)}, u32[]{:S(2)}) collective-permute-start(bf16[320,2048]{1,0:T(8,128)(2,1)} %get-tuple-element.87.h_ref), channel_id=1, source_target_pairs={{0,16},{16,0},{1,17},{17,1},{2,18},{18,2},{3,19},{19,3},{4,20},{20... | collective-permute-start | bytes 3932168 | tf_op jit(solution)/shard_map/ppermute | solution.py:1221
  493.5 31.8 %collective-permute-start.4 = (bf16[320,2048]{1,0:T(8,128)(2,1)}, bf16[320,2048]{1,0:T(8,128)(2,1)}, u32[]{:S(2)}, u32[]{:S(2)}) collective-permute-start(bf16[320,2048]{1,0:T(8,128)(2,1)} %get-tuple-element.106), channel_id=1, source_target_pairs={{0,16},{16,0},{1,17},{17,1},{2,18},{18,2},{3,19},{19,3},{4,20},{20... | collective-permute-start | bytes 3932168 | tf_op jit(solution)/shard_map/ppermute | solution.py:1271
  537.2 32.4 %all-to-all-start.4 = ((bf16[16,320,128]{2,1,0:T(8,128)(2,1)}), bf16[16,320,128]{2,1,0:T(8,128)(2,1)}, u32[]{:S(2)}, u32[]{:S(2)}) async-start(bf16[16,320,128]{2,1,0:T(8,128)(2,1)} %get-tuple-element.110), calls=%async_computation.4 | async-start | bytes 2621440 | tf_op jit(solution)/shard_map/all_to_all | solution.py:1194
  542.1 82.0 %reduce-scatter.3.cloned.1.call-start = ((), (), s32[]{:S(2)}) async-start(), calls=%async_computation.13 | async-start | bytes 1146880 | tf_op jit(solution)/shard_map/reduce_scatter | solution.py:1299
  569.6 61.6 %reduce-scatter.5.cloned.1.call-start = ((), (), s32[]{:S(2)}) async-start(), calls=%async_computation.14 | async-start | bytes 1720320 | tf_op jit(solution)/shard_map/reduce_scatter | solution.py:1300
  570.2 53.9 %collective-permute-start.5 = (bf16[320,2048]{1,0:T(8,128)(2,1)}, bf16[320,2048]{1,0:T(8,128)(2,1)}, u32[]{:S(2)}, u32[]{:S(2)}) collective-permute-start(bf16[320,2048]{1,0:T(8,128)(2,1)} %get-tuple-element.131), channel_id=1, source_target_pairs={{0,16},{16,0},{1,17},{17,1},{2,18},{18,2},{3,19},{19,3},{4,20},{20... | collective-permute-start | bytes 3932168 | tf_op jit(solution)/shard_map/ppermute | solution.py:1287
  642.7 88.7 %all-to-all-start.5 = ((bf16[16,320,256]{2,1,0:T(8,128)(2,1)}), bf16[16,320,256]{2,1,0:T(8,128)(2,1)S(1)}, u32[]{:S(2)}, u32[]{:S(2)}) async-start(bf16[16,320,256]{2,1,0:T(8,128)(2,1)} %bitcast.314), calls=%async_computation.7 | async-start | bytes 5242880 | tf_op jit(solution)/shard_map/all_to_all | solution.py:1197
  647.0 48.0 %collective-permute-start.7 = (f32[112,512]{1,0:T(8,128)}, f32[112,512]{1,0:T(8,128)S(1)}, u32[]{:S(2)}, u32[]{:S(2)}) collective-permute-start(f32[112,512]{1,0:T(8,128)} %reduce-scatter.3.cloned.1.call-done), channel_id=1, source_target_pairs={{0,1},{1,0},{2,3},{3,2},{4,5},{5,4},{6,7},{7,6},{8,9},{9,8},{10,11... | collective-permute-start | bytes 688136 | tf_op jit(solution)/shard_map/ppermute | solution.py:986
  648.7 69.6 %collective-permute-start.10 = (f32[112,768]{1,0:T(8,128)S(1)}, f32[112,768]{1,0:T(8,128)}, u32[]{:S(2)}, u32[]{:S(2)}) collective-permute-start(f32[112,768]{1,0:T(8,128)S(1)} %add.390), channel_id=1, source_target_pairs={{0,8},{4,12},{8,0},{12,4},{1,9},{5,13},{9,1},{13,5},{2,10},{6,14},... | collective-permute-start | bytes 1032200 | tf_op jit(solution)/shard_map/ppermute | solution.py:986
  695.9 20.9 %collective-permute-start.8 = (f32[112,512]{1,0:T(8,128)S(1)}, f32[112,512]{1,0:T(8,128)S(1)}, u32[]{:S(2)}, u32[]{:S(2)}) collective-permute-start(f32[112,512]{1,0:T(8,128)S(1)} %add.388), channel_id=1, source_target_pairs={{0,2},{1,3},{2,0},{3,1},{4,6},{5,7},{6,4},{7,5},{8,10},{9,11},{10,... | collective-permute-start | bytes 688136 | tf_op jit(solution)/shard_map/ppermute | solution.py:986
  716.8 8.6 %collective-permute-start.11 = (f32[112,512]{1,0:T(8,128)S(1)}, f32[112,512]{1,0:T(8,128)S(1)}, u32[]{:S(2)}, u32[]{:S(2)}) collective-permute-start(f32[112,512]{1,0:T(8,128)S(1)} %add.389), channel_id=1, source_target_pairs={{0,16},{16,0},{1,17},{17,1},{2,18},{18,2},{3,19},{19,3},{4,20},{20... | collective-permute-start | bytes 688136 | tf_op jit(solution)/shard_map/ppermute | solution.py:1312
  719.3 12.0 %collective-permute-start.12 = (f32[112,768]{1,0:T(8,128)S(1)}, f32[112,768]{1,0:T(8,128)S(1)}, u32[]{:S(2)}, u32[]{:S(2)}) collective-permute-start(f32[112,768]{1,0:T(8,128)S(1)} %add.391), channel_id=1, source_target_pairs={{0,16},{16,0},{1,17},{17,1},{2,18},{18,2},{3,19},{19,3},{4,20},{20... | collective-permute-start | bytes 1032200 | tf_op jit(solution)/shard_map/ppermute | solution.py:1312
  734.9 44.5 %all-to-all-start.6 = ((bf16[320,4,512]{2,0,1:T(8,128)(2,1)}), bf16[320,4,512]{2,0,1:T(8,128)(2,1)}, u32[]{:S(2)}, u32[]{:S(2)}) async-start(bf16[320,4,512]{2,0,1:T(8,128)(2,1)} %bitcast.329), calls=%async_computation.8 | async-start | bytes 2621440 | tf_op jit(solution)/shard_map/all_to_all | solution.py:1316
  753.1 18.0 %collective-permute-start.18 = (f32[2,16,1024]{2,1,0:T(8,128)}, f32[2,16,1024]{2,1,0:T(8,128)}, u32[]{:S(2)}, u32[]{:S(2)}) collective-permute-start(f32[2,16,1024]{2,1,0:T(8,128)} %dynamic-slice_bitcast_fusion.3), channel_id=1, source_target_pairs={{0,2},{1,3},{2,0},{3,1},{4,6},{5,7},{6,4},{7,5},{8,10},{9,11},{10,... | collective-permute-start | bytes 393224 | tf_op jit(solution)/shard_map/ppermute | solution.py:1001
  754.7 22.1 %collective-permute-start.13 = (f32[2,48,512]{2,1,0:T(8,128)}, f32[2,48,512]{2,1,0:T(8,128)}, u32[]{:S(2)}, u32[]{:S(2)}) collective-permute-start(f32[2,48,512]{2,1,0:T(8,128)} %dynamic-slice_bitcast_fusion), channel_id=1, source_target_pairs={{0,8},{4,12},{8,0},{12,4},{1,9},{5,13},{9,1},{13,5},{2,10},{6,14},... | collective-permute-start | bytes 589832 | tf_op jit(solution)/shard_map/ppermute | solution.py:1001
  780.6 29.1 %all-to-all-start.7 = ((bf16[320,4,512]{2,0,1:T(8,128)(2,1)}), bf16[320,4,512]{2,0,1:T(8,128)(2,1)S(1)}, u32[]{:S(2)}, u32[]{:S(2)}) async-start(bf16[320,4,512]{2,0,1:T(8,128)(2,1)} %bitcast.279), calls=%async_computation.9 | async-start | bytes 2621440 | tf_op jit(solution)/shard_map/all_to_all | solution.py:1333
  (73 other events, 528.9 us)
Sparse Core Ops, SparseCore 0:
  11.3 118.6 all-gather.3
  131.6 220.6 all-gather.5
  353.9 110.1 all-gather.7
  569.7 26.8 reduce-scatter.2
  598.9 32.2 reduce-scatter.4

commit v3 on v2

--- a/solution.py
+++ b/solution.py
@@ -16,6 +16,8 @@
 TREE_LEN = 5120
 TRUNK = 2048
 SEG_LEN = 256
+QUERY_BLOCK = 512
+KEY_BLOCK = 1024
 
 EPSILON = 1e-06
 THETA = 1000000.0
@@ -41,11 +43,37 @@
     return lax.dot_general(left, right, (((0,), (0,)), ((), ())), preferred_element_type=F32)
 
 
+def walk_keys(index, parent_ref, step):
+    trunk_blocks = TRUNK // QUERY_BLOCK
+
+    @pl.when(index < trunk_blocks)
+    def _():
+        @pl.loop(0, index)
+        def _(block):
+            step(pl.multiple_of(block * QUERY_BLOCK, QUERY_BLOCK), QUERY_BLOCK)
+
+        step(pl.multiple_of(index * QUERY_BLOCK, QUERY_BLOCK), QUERY_BLOCK, causal=True)
+
+    @pl.when(index >= trunk_blocks)
+    def _():
+        for part in range(TRUNK // KEY_BLOCK):
+            step(part * KEY_BLOCK, KEY_BLOCK)
+        for side in range(QUERY_BLOCK // SEG_LEN):
+            block = index * (QUERY_BLOCK // SEG_LEN) + side
+            first = side * SEG_LEN
+            start = pl.multiple_of(block * SEG_LEN, SEG_LEN)
+            step(start, SEG_LEN, first, SEG_LEN, True)
+            above = parent_ref[block]
+
+            @pl.when(above >= 0)
+            def _():
+                step(pl.multiple_of(above * SEG_LEN, SEG_LEN), SEG_LEN, first, SEG_LEN)
+
+
 def attention_forward_kernel(
     parent_ref, flag_ref, q_ref, mine_ref, theirs_ref, o_ref, low_ref, l_ref, k_ref, v_ref, acc_ref
 ):
     index = pl.program_id(0)
-    trunk_blocks = TRUNK // SEG_LEN
 
     @pl.when(index == 0)
     def _():
@@ -62,49 +90,31 @@
             k_ref[...] = theirs_ref[...]
             v_ref[:, :HEAD_SIZE] = mine_ref[...]
 
-    query = q_ref[...]
     acc_ref[...] = jnp.zeros_like(acc_ref)
 
-    def step(start, size, causal=False):
+    def step(start, size, first=0, count=QUERY_BLOCK, causal=False):
         rows = pl.ds(start, size)
-        scores = dot_nt(query, k_ref[rows, :])
+        at = pl.ds(first, count)
+        scores = dot_nt(q_ref[at, :], k_ref[rows, :])
         probs = jnp.exp2(scores * SCALE_LOG2)
         if causal:
             ahead = lax.broadcasted_iota(jnp.int32, probs.shape, 0)
             behind = lax.broadcasted_iota(jnp.int32, probs.shape, 1)
             probs = jnp.where(behind <= ahead, probs, 0.0)
-        acc_ref[...] += dot(probs.astype(BF), v_ref[rows, :])
-
-    @pl.when(index < trunk_blocks)
-    def _():
-        @pl.loop(0, index)
-        def _(block):
-            step(pl.multiple_of(block * SEG_LEN, SEG_LEN), SEG_LEN)
-
-    @pl.when(index >= trunk_blocks)
-    def _():
-        size = 512
-        for part in range(TRUNK // size):
-            step(part * size, size)
-
-        above = parent_ref[index]
-
-        @pl.when(above >= 0)
-        def _():
-            step(pl.multiple_of(above * SEG_LEN, SEG_LEN), SEG_LEN)
-
-    step(pl.multiple_of(index * SEG_LEN, SEG_LEN), SEG_LEN, True)
+        acc_ref[at, :] += dot(probs.astype(BF), v_ref[rows, :])
+
+    walk_keys(index, parent_ref, step)
     total = acc_ref[:, HEAD_SIZE : HEAD_SIZE + 1]
     attended = acc_ref[:, :HEAD_SIZE] / total
     o_ref[...] = attended
     low_ref[...] = attended.astype(BF)
-    spread = jnp.broadcast_to(total, (SEG_LEN, LANES))
+    spread = jnp.broadcast_to(total, (QUERY_BLOCK, LANES))
     l_ref[0] = jnp.transpose(spread)[:8, :]
 
 
 def attention_forward(parent_block, flag, got, theirs):
     length = theirs.shape[0]
-    blocks = length // SEG_LEN
+    blocks = length // QUERY_BLOCK
     whole = lambda i, p, f: (0, 0)
     part = lambda i, p, f: (i, 0)
     return pl.pallas_call(
@@ -113,25 +123,25 @@
             num_scalar_prefetch=2,
             grid=(blocks,),
             in_specs=[
-                pl.BlockSpec((SEG_LEN, HEAD_SIZE), part),
+                pl.BlockSpec((QUERY_BLOCK, HEAD_SIZE), part),
                 pl.BlockSpec((length, HEAD_SIZE), lambda i, p, f: (0, 1)),
                 pl.BlockSpec((length, HEAD_SIZE), whole),
             ],
             out_specs=[
-                pl.BlockSpec((SEG_LEN, HEAD_SIZE), part),
-                pl.BlockSpec((SEG_LEN, HEAD_SIZE), part),
-                pl.BlockSpec((1, 8, SEG_LEN), lambda i, p, f: (i, 0, 0)),
+                pl.BlockSpec((QUERY_BLOCK, HEAD_SIZE), part),
+                pl.BlockSpec((QUERY_BLOCK, HEAD_SIZE), part),
+                pl.BlockSpec((1, 8, QUERY_BLOCK), lambda i, p, f: (i, 0, 0)),
             ],
             scratch_shapes=[
                 pltpu.VMEM((length, HEAD_SIZE), BF),
                 pltpu.VMEM((length, 2 * HEAD_SIZE), BF),
-                pltpu.VMEM((SEG_LEN, 2 * HEAD_SIZE), F32),
+                pltpu.VMEM((QUERY_BLOCK, 2 * HEAD_SIZE), F32),
             ],
         ),
         out_shape=[
             jax.ShapeDtypeStruct((length, HEAD_SIZE), F32),
             jax.ShapeDtypeStruct((length, HEAD_SIZE), BF),
-            jax.ShapeDtypeStruct((blocks, 8, SEG_LEN), F32),
+            jax.ShapeDtypeStruct((blocks, 8, QUERY_BLOCK), F32),
         ],
         compiler_params=pltpu.CompilerParams(vmem_limit_bytes=VMEM_LIMIT),
         cost_estimate=pl.CostEstimate(
@@ -161,9 +171,10 @@
     dk_ref,
     dv_ref,
     acc_ref,
+    delta_ref,
+    inverse_ref,
 ):
     index = pl.program_id(0)
-    trunk_blocks = TRUNK // SEG_LEN
 
     @pl.when(index == 0)
     def _():
@@ -185,45 +196,28 @@
             rows = pl.ds(pl.multiple_of(block * SEG_LEN, SEG_LEN), SEG_LEN)
             kt_ref[:, rows] = jnp.transpose(k_ref[rows, :])
 
-    query = q_ref[...]
-    grad = g_ref[...]
-    delta = jnp.sum(grad.astype(F32) * o_ref[...], axis=1, keepdims=True)
-    delta = jnp.transpose(jnp.broadcast_to(delta, (SEG_LEN, LANES)))[:1, :]
-    inverse = 1.0 / l_ref[0, :1, :]
+    delta = jnp.sum(g_ref[...].astype(F32) * o_ref[...], axis=1, keepdims=True)
+    delta_ref[...] = jnp.transpose(jnp.broadcast_to(delta, (QUERY_BLOCK, LANES)))[:8, :]
+    inverse_ref[...] = 1.0 / l_ref[0]
     acc_ref[...] = jnp.zeros_like(acc_ref)
 
-    def step(start, size, causal=False):
+    def step(start, size, first=0, count=QUERY_BLOCK, causal=False):
         rows = pl.ds(start, size)
-        probs = jnp.exp2(dot_nt(k_ref[rows, :], query) * SCALE_LOG2) * inverse
+        at = pl.ds(first, count)
+        query = q_ref[at, :]
+        grad = g_ref[at, :]
+        probs = jnp.exp2(dot_nt(k_ref[rows, :], query) * SCALE_LOG2) * inverse_ref[:1, at]
         if causal:
             behind = lax.broadcasted_iota(jnp.int32, probs.shape, 0)
             ahead = lax.broadcasted_iota(jnp.int32, probs.shape, 1)
             probs = jnp.where(behind <= ahead, probs, 0.0)
         dprobs = dot_nt(v_ref[rows, :], grad)
-        dscores = (probs * (dprobs - delta)).astype(BF)
+        dscores = (probs * (dprobs - delta_ref[:1, at])).astype(BF)
         dv_ref[rows, :] += dot(probs.astype(BF), grad)
         dk_ref[rows, :] += dot(dscores, query)
-        acc_ref[...] += dot(kt_ref[:, rows], dscores)
-
-    @pl.when(index < trunk_blocks)
-    def _():
-        @pl.loop(0, index)
-        def _(block):
-            step(pl.multiple_of(block * SEG_LEN, SEG_LEN), SEG_LEN)
-
-    @pl.when(index >= trunk_blocks)
-    def _():
-        size = 512
-        for part in range(TRUNK // size):
-            step(part * size, size)
-
-        above = parent_ref[index]
-
-        @pl.when(above >= 0)
-        def _():
-            step(pl.multiple_of(above * SEG_LEN, SEG_LEN), SEG_LEN)
-
-    step(pl.multiple_of(index * SEG_LEN, SEG_LEN), SEG_LEN, True)
+        acc_ref[:, at] += dot(kt_ref[:, rows], dscores)
+
+    walk_keys(index, parent_ref, step)
     dq_ref[...] = (jnp.transpose(acc_ref[...]) * SCALE).astype(BF)
 
     @pl.when(index == pl.num_programs(0) - 1)
@@ -231,17 +225,17 @@
         @pl.when(flag_ref[0] == 1)
         def _():
             kept_ref[...] = dk_ref[...] * SCALE
-            given_ref[...] = dv_ref[...]
+            given_ref[...] = dv_ref[...].astype(BF)
 
         @pl.when(flag_ref[0] != 1)
         def _():
             kept_ref[...] = dv_ref[...]
-            given_ref[...] = dk_ref[...] * SCALE
+            given_ref[...] = (dk_ref[...] * SCALE).astype(BF)
 
 
 def attention_backward(parent_block, flag, got, grad, attended, totals, theirs):
     length = theirs.shape[0]
-    blocks = length // SEG_LEN
+    blocks = length // QUERY_BLOCK
     whole = lambda i, p, f: (0, 0)
     part = lambda i, p, f: (i, 0)
     return pl.pallas_call(
@@ -250,15 +244,15 @@
             num_scalar_prefetch=2,
             grid=(blocks,),
             in_specs=[
-                pl.BlockSpec((SEG_LEN, HEAD_SIZE), part),
-                pl.BlockSpec((SEG_LEN, HEAD_SIZE), part),
-                pl.BlockSpec((SEG_LEN, HEAD_SIZE), part),
-                pl.BlockSpec((1, 8, SEG_LEN), lambda i, p, f: (i, 0, 0)),
+                pl.BlockSpec((QUERY_BLOCK, HEAD_SIZE), part),
+                pl.BlockSpec((QUERY_BLOCK, HEAD_SIZE), part),
+                pl.BlockSpec((QUERY_BLOCK, HEAD_SIZE), part),
+                pl.BlockSpec((1, 8, QUERY_BLOCK), lambda i, p, f: (i, 0, 0)),
                 pl.BlockSpec((length, HEAD_SIZE), lambda i, p, f: (0, 1)),
                 pl.BlockSpec((length, HEAD_SIZE), whole),
             ],
             out_specs=[
-                pl.BlockSpec((SEG_LEN, HEAD_SIZE), part),
+                pl.BlockSpec((QUERY_BLOCK, HEAD_SIZE), part),
                 pl.BlockSpec((length, HEAD_SIZE), whole),
                 pl.BlockSpec((length, HEAD_SIZE), whole),
             ],
@@ -268,13 +262,15 @@
                 pltpu.VMEM((HEAD_SIZE, length), BF),
                 pltpu.VMEM((length, HEAD_SIZE), F32),
                 pltpu.VMEM((length, HEAD_SIZE), F32),
-                pltpu.VMEM((HEAD_SIZE, SEG_LEN), F32),
+                pltpu.VMEM((HEAD_SIZE, QUERY_BLOCK), F32),
+                pltpu.VMEM((8, QUERY_BLOCK), F32),
+                pltpu.VMEM((8, QUERY_BLOCK), F32),
             ],
         ),
         out_shape=[
             jax.ShapeDtypeStruct((length, 2 * HEAD_SIZE), BF),
             jax.ShapeDtypeStruct((length, HEAD_SIZE), F32),
-            jax.ShapeDtypeStruct((length, HEAD_SIZE), F32),
+            jax.ShapeDtypeStruct((length, HEAD_SIZE), BF),
         ],
         compiler_params=pltpu.CompilerParams(vmem_limit_bytes=VMEM_LIMIT),
         cost_estimate=pl.CostEstimate(
@@ -287,7 +283,7 @@
 
 
 def merge_kernel(lines_ref, kept_ref, got_ref, out_ref):
-    out_ref[...] = (kept_ref[...] + got_ref[...]).astype(BF)
+    out_ref[...] = (kept_ref[...] + got_ref[...].astype(F32)).astype(BF)
 
 
 def merge(lines, kept, got):
@@ -599,24 +595,32 @@
     )(grads, inner, x, grad_middle, gain, inmaps, weights)
 
 
-def joined(refs, tall):
+def whole_output_weights(flag_ref, own_ref, other_ref):
+    own, other = (
+        jnp.concatenate([ref[0, r] for r in range(ref.shape[1])], axis=1)
+        for ref in (own_ref, other_ref)
+    )
+    first = flag_ref[0] == 0
     return jnp.concatenate(
-        [ref[0, r, 0, :tall, :] for r in range(refs[0].shape[1]) for ref in refs], axis=1
-    )
-
-
-def output_specs(weights, first_unit, features):
-    row_blocks, tall = weights.shape[1], weights.shape[3]
-
-    def spec(unit):
-        return pl.BlockSpec((1, row_blocks, 1, tall, LANES), lambda c: (c, 0, unit, 0, 0))
-
-    return [spec(first_unit + j) for j in range(features // LANES)]
-
-
-def output_forward_kernel(att_ref, x_ref, gain_ref, a_ref, b_ref, *refs):
-    weight_refs = refs[:-5]
-    middle_ref, hidden_ref, m_ref, acc_ref, m_acc_ref = refs[-5:]
+        [jnp.where(first, own, other), jnp.where(first, other, own)], axis=0
+    )
+
+
+def output_forward_kernel(
+    flag_ref,
+    att_ref,
+    x_ref,
+    gain_ref,
+    a_ref,
+    b_ref,
+    own_ref,
+    other_ref,
+    middle_ref,
+    hidden_ref,
+    m_ref,
+    acc_ref,
+    m_acc_ref,
+):
     step = pl.program_id(0)
     heads = att_ref.shape[0]
 
@@ -626,7 +630,7 @@
         m_acc_ref[...] = jnp.zeros_like(m_acc_ref)
 
     attended = jnp.concatenate([att_ref[h] for h in range(heads)], axis=1)
-    acc_ref[...] += dot(attended, joined(weight_refs, attended.shape[1]))
+    acc_ref[...] += dot(attended, whole_output_weights(flag_ref, own_ref, other_ref))
     m_acc_ref[...] += dot_nt(attended, a_ref[0])
 
     @pl.when(step == pl.num_programs(0) - 1)
@@ -638,25 +642,26 @@
         hidden_ref[...] = (middle * norm_scale(middle) * gain_ref[...]).astype(BF)
 
 
-def output_forward(attended, x, gain, inmaps, outmaps, weights, first_unit):
+def output_forward(flag, attended, x, gain, inmaps, outmaps, weights):
     own = x.shape[0]
-    cols, row_blocks = weights.shape[:2]
-    features = MODEL_WIDTH // row_blocks
+    cols = weights[0].shape[0]
     heads = QUERY_HEADS // cols
     o_rows = heads * HEAD_SIZE
-    specs = output_specs(weights, first_unit, features)
+    half = pl.BlockSpec((1, *weights[0].shape[1:]), lambda c: (c, 0, 0, 0))
     whole = lambda c: (0, 0)
     step = lambda c: (c, 0, 0)
     return pl.pallas_call(
         output_forward_kernel,
         grid=(cols,),
         in_specs=[
+            pl.BlockSpec(memory_space=pltpu.SMEM),
             pl.BlockSpec((heads, own, HEAD_SIZE), step),
             pl.BlockSpec(x.shape, whole),
             pl.BlockSpec(gain.shape, whole),
             pl.BlockSpec((1, LANES, o_rows), step),
             pl.BlockSpec(outmaps.shape, whole),
-            *specs,
+            half,
+            half,
         ],
         out_specs=[
             pl.BlockSpec((own, MODEL_WIDTH), whole),
@@ -676,10 +681,11 @@
             transcendentals=own,
         ),
         name="output_forward",
-    )(attended, x, gain, inmaps, outmaps, *[weights] * len(specs))
+    )(flag, attended, x, gain, inmaps, outmaps, *weights)
 
 
 def output_backward_kernel(
+    flag_ref,
     gh_ref,
     got_ref,
     cot_ref,
@@ -689,10 +695,15 @@
     b_ref,
     att_ref,
     m_ref,
-    *refs,
+    own_ref,
+    other_ref,
+    gm_ref,
+    sent_ref,
+    gb_ref,
+    ga_ref,
+    low_ref,
+    inner_ref,
 ):
-    weight_refs = refs[:-6]
-    gm_ref, sent_ref, gb_ref, ga_ref, low_ref, inner_ref = refs[-6:]
     heads = sent_ref.shape[0]
     row_blocks, rank, features = gb_ref.shape
 
@@ -712,21 +723,21 @@
 
     attended = jnp.concatenate([att_ref[h] for h in range(heads)], axis=1)
     ga_ref[0] = dot_tn(inner_ref[...], attended)[:rank, :]
-    weights = joined(weight_refs, heads * HEAD_SIZE)
+    weights = whole_output_weights(flag_ref, own_ref, other_ref)
     grad = (dot_nt(low_ref[...], weights) + dot(inner_ref[...], a_ref[0])).astype(BF)
     for head in range(heads):
         sent_ref[head] = grad[:, head * HEAD_SIZE : (head + 1) * HEAD_SIZE]
 
 
 def output_backward(
-    grad_hidden, got, cotangent, middle, gain, inmaps, outmaps, attended, masked, weights, first_unit
+    flag, grad_hidden, got, cotangent, middle, gain, inmaps, outmaps, attended, masked, weights
 ):
     own = middle.shape[0]
-    cols, row_blocks = weights.shape[:2]
+    cols, row_blocks = weights[0].shape[:2]
     features = MODEL_WIDTH // row_blocks
     heads = QUERY_HEADS // cols
     o_rows = heads * HEAD_SIZE
-    specs = output_specs(weights, first_unit, features)
+    half = pl.BlockSpec((1, *weights[0].shape[1:]), lambda c: (c, 0, 0, 0))
     whole = lambda c: (0, 0)
     step = lambda c: (c, 0, 0)
     once = pl.Buffered(1)
@@ -734,6 +745,7 @@
         output_backward_kernel,
         grid=(cols,),
         in_specs=[
+            pl.BlockSpec(memory_space=pltpu.SMEM),
             pl.BlockSpec((own, MODEL_WIDTH), whole, pipeline_mode=once),
             pl.BlockSpec((own, MODEL_WIDTH), whole, pipeline_mode=once),
             pl.BlockSpec((own, MODEL_WIDTH), whole, pipeline_mode=once),
@@ -743,7 +755,8 @@
             pl.BlockSpec(outmaps.shape, whole),
             pl.BlockSpec((heads, own, HEAD_SIZE), step),
             pl.BlockSpec(masked.shape, whole),
-            *specs,
+            half,
+            half,
         ],
         out_specs=[
             pl.BlockSpec((own, MODEL_WIDTH), whole),
@@ -766,6 +779,7 @@
         ),
         name="output_backward",
     )(
+        flag,
         grad_hidden,
         got,
         cotangent,
@@ -775,7 +789,7 @@
         outmaps,
         attended,
         masked,
-        *[weights] * len(specs),
+        *weights,
     )
 
 
@@ -805,13 +819,8 @@
             for ref in scratch:
                 ref[...] = jnp.zeros_like(ref)
         else:
-            copies = [
-                pltpu.make_async_copy(previous[i], scratch[i], sems.at[i]) for i in range(5)
-            ]
-            for copy in copies:
-                copy.start()
-            for copy in copies:
-                copy.wait()
+            for i in range(5):
+                pltpu.make_async_copy(previous[i], scratch[i], sems.at[i]).start()
 
     def side(kind, row):
         return jnp.concatenate([ref[0, row, kind] for ref in weight_refs], axis=1)
@@ -846,6 +855,13 @@
     grad_gate = (grad_act * upward * (sigma * (1.0 + gate * (1.0 - sigma)))).astype(BF)
     grad_up = (grad_act * swish).astype(BF)
     both = jnp.concatenate([grad_gate, grad_up], axis=1)
+    if not first:
+
+        @pl.when(step == 0)
+        def _():
+            for i in range(5):
+                pltpu.make_async_copy(previous[i], scratch[i], sems.at[i]).wait()
+
     for row in range(row_blocks):
         at = slice(row * deep, (row + 1) * deep)
         gh_acc[:, at] += dot_nt(both, jnp.concatenate([side(0, row), side(1, row)], axis=1))
@@ -976,31 +992,6 @@
         parts.append(part.astype(BF)[:, None])
         values = values - part
     return parts
-
-
-def summed(values, axis):
-    size = lax.axis_size(axis)
-    bit = 1
-    while bit < size:
-        pairs = [(i, i ^ bit) for i in range(size)]
-        values = values + lax.ppermute(values, axis, pairs)
-        bit = 2 * bit
-    return values
-
-
-def summed_block(blocks, axis):
-    size = lax.axis_size(axis)
-    at = lax.axis_index(axis)
-    bit = size // 2
-    while bit:
-        pairs = [(i, i ^ bit) for i in range(size)]
-        halves = blocks.reshape(2, bit, *blocks.shape[1:])
-        upper = (at // bit) % 2
-        kept = lax.dynamic_index_in_dim(halves, upper, 0, False)
-        sent = lax.dynamic_index_in_dim(halves, 1 - upper, 0, False)
-        blocks = kept + lax.ppermute(sent, axis, pairs)
-        bit = bit // 2
-    return blocks[0]
 
 
 def on_device(
@@ -1082,6 +1073,11 @@
             table[:, at : at + features]
             for table in (qkv_local, qkv_maps)
             for at in range(0, wide, features)
+        ]
+        + [
+            lax.dynamic_slice_in_dim(
+                output_matrix, plane * (output_matrix.shape[0] // 2), output_matrix.shape[0] // 2, 0
+            )
         ],
         axis=0,
     )
@@ -1089,6 +1085,8 @@
         cols, rows, -1, features
     )
     o_rows = output_matrix.shape[0]
+    own_output_weights = attention_weights[:, :, -(o_rows // 2) :]
+    plane_flag = plane.astype(jnp.int32).reshape(1)
     ffn_half = gate_matrix.shape[1] // 2
     half_start = plane * ffn_half
     chunks = 2 if ffn_half % 256 == 0 else 3
@@ -1128,8 +1126,6 @@
             pack.extend(plates(lax.dynamic_slice_in_dim(down_matrix, start, LANES, 0)))
         if chunk == 0:
             spare = features - map_rows * len(map_plates)
-            for plate in plates(output_matrix):
-                pack.append(jnp.pad(plate, ((0, features - o_rows), (0, 0))))
             pack = pack + map_plates + [jnp.zeros((spare, LANES), BF)]
         pack = jnp.concatenate(pack, axis=0)
         ffn_weights.append(
@@ -1137,7 +1133,6 @@
                 cols, rows, -1, features, LANES
             )
         )
-    o_unit = 3 * slabs
     col_maps = ffn_weights[0][:, :, -1, : map_rows * len(map_plates)].reshape(
         cols, rows, len(map_plates), map_rows, LANES
     )
@@ -1175,6 +1170,10 @@
     own_tokens = lax.all_to_all(tokens, "row", 0, 1, tiled=True)
     own_cotangent = lax.all_to_all(cotangent, "row", 0, 1, tiled=True)
     other_cotangent = lax.ppermute(own_cotangent, "dp", swap)
+    own_tokens, other_cotangent, own_output_weights = lax.optimization_barrier(
+        (own_tokens, other_cotangent, own_output_weights)
+    )
+    other_output_weights = lax.ppermute(own_output_weights, "dp", swap)
     head_gains = jnp.stack([query_norm_gain, key_norm_gain], axis=0)
     token_start = (col * rows + row) * own
     positions = lax.dynamic_slice_in_dim(depth, token_start, own, 0).astype(F32)
@@ -1199,7 +1198,8 @@
         )
         return got[::repeat] if repeat > 1 else got
 
-    got = to_heads(sent)
+    got, other_output_weights = lax.optimization_barrier((to_heads(sent), other_output_weights))
+    output_weights = (own_output_weights, other_output_weights)
     theirs = lax.ppermute(got[:, HEAD_SIZE:], "row", pairs)
     flag = (1 - (row // repeat) % 2).astype(jnp.int32).reshape(1)
 
@@ -1215,7 +1215,7 @@
     attended = to_tokens(head_low)
 
     middle, hidden_ffn, masked_o = output_forward(
-        attended, own_tokens, gain_two, in_o, out_o, ffn_weights[0], o_unit
+        plane_flag, attended, own_tokens, gain_two, in_o, out_o, output_weights
     )
 
     other_ffn = lax.ppermute(hidden_ffn, "dp", swap)
@@ -1271,6 +1271,7 @@
     gh_other = lax.ppermute(there[0], "dp", swap)
 
     grad_middle, sent, grad_o_rows, grad_o_cols = output_backward(
+        plane_flag,
         here[0],
         gh_other,
         own_cotangent,
@@ -1280,40 +1281,78 @@
         out_o,
         attended,
         masked_o,
-        ffn_weights[0],
-        o_unit,
+        output_weights,
     )
     out_sent, sent = lax.optimization_barrier((there[1], sent))
     out_other = lax.ppermute(out_sent, "dp", swap)
     head_grad = to_heads(sent)
 
-    row_mid = jnp.concatenate([here[2] + there[2], grad_o_rows], axis=1).reshape(-1, features)
+    def pieces_of(row_table, col_table):
+        row_table = jnp.swapaxes(row_table.astype(BF).reshape(rows, cols, -1, LANES), 0, 1)
+        col_table = col_table.astype(BF).reshape(cols, rows, -1, LANES)
+        return jnp.concatenate([row_table, col_table], axis=2).reshape(devices, -1, LANES)
+
+    def gathered(values, axis, at):
+        size = lax.axis_size(axis)
+        whole = jnp.zeros((2, size, *values.shape[1:]), values.dtype)
+        for k in range(size):
+            block = values
+            if k:
+                block = lax.ppermute(values, axis, [(i, i ^ k) for i in range(size)])
+            whole = lax.dynamic_update_index_in_dim(whole, block, at ^ k, 1)
+        return whole
+
+    def summed(pieces):
+        mine = jnp.sum(pieces.astype(F32), axis=0).astype(BF)
+        return jnp.stack([mine, lax.ppermute(mine, "dp", swap)], axis=0)
+
+    def gathered_tables(both_trees, row_high):
+        row_part = row_high * features // (cols * LANES)
+        row_table = gathered(both_trees[:, :row_part], "col", col)
+        col_table = gathered(both_trees[:, row_part:], "row", row)
+        return row_table, col_table
+
+    def tables_of(tables, row_high, col_high):
+        row_table, col_table = tables
+        row_table = row_table.reshape(2, row_high, features).astype(F32)
+        col_table = col_table.reshape(2, col_high, -1).astype(F32)
+        return row_table[0], col_table[0], row_table[1], col_table[1]
+
+    def to_own_features(lines):
+        blocks = lines.reshape(own, rows, features)
+        whole = jnp.zeros((rows, own, features), lines.dtype)
+        for k in range(rows):
+            block = lax.dynamic_index_in_dim(blocks, row ^ k, 1, False)
+            if k:
+                block = lax.ppermute(block, "row", [(r, r ^ k) for r in range(rows)])
+            whole = lax.dynamic_update_index_in_dim(whole, block, row ^ k, 0)
+        return whole.reshape(rows * own, features)
 
     def to_map_width(table):
         return jnp.pad(table, ((0, 0), (0, 0), (0, map_width - table.shape[2])))
 
-    col_mid = jnp.concatenate(
-        [to_map_width(jnp.concatenate(parts, axis=2)), to_map_width(grad_o_cols)], axis=1
-    ).reshape(-1, map_width)
-    head_grad, row_mid, col_mid = lax.optimization_barrier((head_grad, row_mid, col_mid))
-    row_mid = lax.psum_scatter(row_mid, "row", scatter_dimension=0, tiled=True)
-    col_mid = lax.psum_scatter(col_mid, "col", scatter_dimension=0, tiled=True)
+    mid_pieces = pieces_of(
+        jnp.concatenate([here[2] + there[2], grad_o_rows], axis=1),
+        jnp.concatenate(
+            [to_map_width(jnp.concatenate(parts, axis=2)), to_map_width(grad_o_cols)], axis=1
+        ),
+    )
+    head_grad, mid_pieces = lax.optimization_barrier((head_grad, mid_pieces))
+    mid_pieces = lax.all_to_all(mid_pieces, PLANE, 0, 0, tiled=True)
 
     lines, kept, given = attention_backward(
         parent_block, flag, got, head_grad, head_attended, totals, theirs
     )
-    lines, kept, given, row_mid, col_mid, out_other = lax.optimization_barrier(
-        (lines, kept, given, row_mid, col_mid, out_other)
+    lines, kept, given, mid_pieces, out_other = lax.optimization_barrier(
+        (lines, kept, given, mid_pieces, out_other)
     )
     returned = to_tokens(merge(lines, kept, lax.ppermute(given, "row", pairs)))
     output = (middle + here[1] + out_other.astype(F32)).astype(BF)
-    row_mid = summed(row_mid, "col")
-    col_mid = summed(col_mid, "row")
-    row_got, col_got = lax.ppermute((row_mid, col_mid), "dp", swap)
-    returned, row_mid, col_mid, row_got, col_got, output = lax.optimization_barrier(
-        (returned, row_mid, col_mid, row_got, col_got, output)
-    )
-    output = lax.all_to_all(output, "row", 1, 0, tiled=True)
+    output = to_own_features(output)
+    returned, output, mid_pieces = lax.optimization_barrier(
+        (returned, output, summed(mid_pieces))
+    )
+    mid_tables = gathered_tables(mid_pieces, 7 * rank)
 
     grads_qkv, inner_qkv, row_end, col_end = qkv_unshape(
         returned,
@@ -1326,14 +1365,14 @@
         head_gains,
         attention_weights,
     )
+    end_pieces = lax.all_to_all(pieces_of(row_end, col_end), PLANE, 0, 0, tiled=True)
     grad_low = qkv_backward(
         grads_qkv, inner_qkv, own_tokens, grad_middle, gain_one, in_qkv, attention_weights
     )
-    grad_low, output = lax.optimization_barrier((grad_low, output))
+    grad_low, end_pieces, mid_tables = lax.optimization_barrier((grad_low, end_pieces, mid_tables))
     input_gradient = lax.all_to_all(grad_low, "row", 1, 0, tiled=True).astype(F32)
-    row_end = summed(summed_block(row_end, "row"), "col")
-    col_end = summed(summed_block(col_end, "col"), "row")
-    row_end_got, col_end_got = lax.ppermute((row_end, col_end), "dp", swap)
+    end_tables = gathered_tables(summed(end_pieces), 3 * rank)
+    row_mid, col_mid, row_got, col_got = tables_of(mid_tables, 7 * rank, 7 * rank)
 
     def placed(first, second):
         return place(first, own_adapter, second, other_adapter, columns)
@@ -1362,6 +1401,7 @@
     grad_b_up = ffn_placed(1)
     grad_a_down = ffn_placed(2).T
 
+    row_end, col_end, row_end_got, col_end_got = tables_of(end_tables, 3 * rank, rank)
     grad_a_q, grad_a_k, grad_a_v = (
         placed(row_end[i * rank : (i + 1) * rank], row_end_got[i * rank : (i + 1) * rank]).T
         for i in range(3)

time: 832 us -> 776 us (0.933)
  blocking collectives: 128 us -> 35.4 us
  waiting for transfers between devices: 223 us -> 246 us
  Pallas kernels: 270 us -> 248 us
  starting transfers between devices: 59.7 us -> 81.3 us
  local copies, waits for them, and re-layouts: 83.4 us -> 97.8 us
    all_to_all x1 -> x0, blocking collectives: 95 us -> none  [to_heads(): lax.all_to_all(sent, PLANE, 0, 0, tiled=True).reshape(length, sent.shape[2])]
    ppermute x16 -> x18, waiting for transfers between devices: 74.2 us -> 118 us  [the longest x1 91.8 us: on_device(): other_output_weights = lax.ppermute(own_output_weights, 'dp', swap)]
    all_gather x2, waiting for transfers between devices: 58 us -> 18.1 us  [on_device(): lax.all_gather(pack, PLANE, axis=0, tiled=True)]
    all_to_all x2, waiting for transfers between devices: 0.01 us -> 30.5 us  [to_tokens(): lax.all_to_all(lines.reshape(devices, own, lines.shape[1]), PLANE, 0, 0,...]
    ppermute x1, waiting for transfers between devices: 25.9 us -> 0.01 us  [on_device(): other_cotangent = lax.ppermute(own_cotangent, 'dp', swap)]
    all_to_all x1, waiting for transfers between devices: 0.01 us -> 23 us  [on_device(): own_cotangent = lax.all_to_all(cotangent, 'row', 0, 1, tiled=True)]
    pallas_call x1, Pallas kernels: 35.3 us -> 24.7 us  [attention_forward(): pl.pallas_call(attention_forward_kernel, grid_spec=pltpu.PrefetchScalarGr...]
    pallas_call x1, Pallas kernels: 52.9 us -> 43.8 us  [attention_backward(): pl.pallas_call(attention_backward_kernel, grid_spec=pltpu.PrefetchScalarG...]
  transfers between devices with their start and end apart: 35 -> 37, of which waited for: 14 -> 15; matrix products, arithmetic and copies ran while one was open for 12% -> 16% of each run, Pallas kernels for 27% -> 27%
where the time goes in v3:
time: 776 us; the launch traced here: 764 us
  Pallas kernels  248 us (32%)
  waiting for transfers between devices  246 us (32%)
  local copies, waits for them, and re-layouts  97.8 us (13%)
  starting transfers between devices  81.3 us (10%)
  blocking collectives  35.4 us (5%)
  other arithmetic  25.6 us (3%)
  between operations  16.7 us (2%)
  matrix products  13.1 us (2%)
    pallas_call x4, Pallas kernels, feed_forward_chunk(): pl.pallas_call(functools.partial(feed_forward_kernel, first, last), grid=...  111 us
    ppermute x1, waiting for transfers between devices, on_device(): other_output_weights = lax.ppermute(own_output_weights, 'dp', swap)  91.8 us
    pallas_call x1, Pallas kernels, attention_backward(): pl.pallas_call(attention_backward_kernel, grid_spec=pltpu.PrefetchScalarG...  43.8 us
    unnamed x156, local copies, waits for them, and re-layouts  41 us
    all_gather x1, blocking collectives, on_device(): row_maps = lax.all_gather(row_pack, 'row', axis=0, tiled=True)  35.4 us
    all_to_all x2, waiting for transfers between devices, to_tokens(): lax.all_to_all(lines.reshape(devices, own, lines.shape[1]), PLANE, 0, 0,...  30.5 us
    all_gather x1, waiting for transfers between devices, on_device(): lax.all_gather(attention_pack, PLANE, axis=0, tiled=True)  27.5 us
    pallas_call x1, Pallas kernels, attention_forward(): pl.pallas_call(attention_forward_kernel, grid_spec=pltpu.PrefetchScalarGr...  24.7 us
  transfers between devices with their start and end apart: 37, of which 15 were waited for; matrix products, arithmetic and copies ran while one was open for 16% of the time, Pallas kernels for 27%

profile of v3, /device:TPU:0, one launch (start us, length us, event | category | flops | bytes accessed | tf_op | source)
XLA Modules:
  0.0 764.1 jit_solution(2062142230071581003)
XLA Ops:
  59.5 23.0 %all-to-all-done.1 = bf16[4,320,512]{2,1,0:T(8,128)(2,1)S(1)} async-done(((bf16[4,320,512]{2,1,0:T(8,128)(2,1)}), bf16[4,320,512]{2,1,0:T(8,128)(2,1)S(1)}, u32[]{:S(2)}, u32[]{:S(2)}) %all-to-all-start.1) | async-done | bytes 1310752 | tf_op jit(solution)/shard_map/all_to_all | solution.py:1171
  95.1 35.4 %all_gather.13 = bf16[2048,166]{1,0:T(8,128)(2,1)S(1)} all-gather(bf16[512,166]{1,0:T(8,128)(2,1)S(1)} %concatenate.62), channel_id=1, replica_groups=mesh['dp'=2,'row'=4,'col'=4] {'row'}, dimensions={0}, use_global_device_ids=true | all-gather | bytes 849920 | tf_op jit(solution)/shard_map/all_gather | solution.py:1160
  137.2 27.5 %all-gather.4.cloned.1.call-done = bf16[22016,512]{1,0:T(8,128)(2,1)} async-done(((bf16[1376,512]{1,0:T(8,128)(2,1)}), bf16[22016,512]{1,0:T(8,128)(2,1)}) %all-gather.4.cloned.1.call-update) | async-done | bytes 22544400 | tf_op jit(solution)/shard_map/all_gather | solution.py:1084
  170.3 17.9 %qkv_forward.1 = (bf16[320,48]{1,0:T(8,128)(2,1)}, f32[4,320,768]{2,1,0:T(8,128)}, bf16[16,320,256]{2,1,0:T(8,128)(2,1)}) custom-call(bf16[320,2048]{1,0:T(8,128)(2,1)} %bitcast.426, f32[1,2048]{1,0:T(1,128)} %bitcast.479, bf16[2048,48]{1,0:T(8,128)(2,1)} %slice.470.a_ref, f32[320,128]{1,0:T(8,128)} %copy.364.cos_ref, f32[320,128]{1,0:T(8,128)} %pad_maximum_fusion.7.sin_ref, ...), custom_call_target="tpu_custom_call" | custom-call | flops 5368709120 | bytes 16777216 | tf_op jit(solution)/shard_map/qkv_forward/pallas_call | solution.py:391
  195.0 91.8 %collective-permute-done.2.other_ref = bf16[4,4,256,512]{3,2,1,0:T(8,128)(2,1)} collective-permute-done((bf16[4,4,256,512]{3,2,1,0:T(8,128)(2,1)}, bf16[4,4,256,512]{3,2,1,0:T(8,128)(2,1)}, u32[]{:S(2)}, u32[]{:S(2)}) %collective-permute-start.2) | collective-permute-done | bytes 4194336 | tf_op jit(solution)/shard_map/ppermute | solution.py:1176
  292.1 24.7 %attention_forward.1 = (f32[5120,128]{1,0:T(8,128)}, bf16[5120,128]{1,0:T(8,128)(2,1)}, f32[10,8,512]{2,1,0:T(8,128)}) custom-call(s32[20]{0:T(128)} %compare_select_fusion.parent_ref, s32[1]{0:T(128)} %bitcast.1.flag_ref, bf16[5120,256]{1,0:T(8,128)(2,1)} %bitcast.445, bf16[5120,256]{1,0:T(8,128)(2,1)} %bitcast.446, ...), custom_call_target="tpu_custom_call" | custom-call | flops 5368709120 | bytes 7864320 | tf_op jit(solution)/shard_map/attention_forward/pallas_call | solution.py:120
  316.8 6.0 all-to-all-start.3
  332.5 21.6 %all-to-all-done.3.att_ref = bf16[16,320,128]{2,1,0:T(8,128)(2,1)} async-done(((bf16[16,320,128]{2,1,0:T(8,128)(2,1)}), bf16[16,320,128]{2,1,0:T(8,128)(2,1)}, u32[]{:S(2)}, u32[]{:S(2)}) %all-to-all-start.3) | async-done | bytes 1310752 | tf_op jit(solution)/shard_map/all_to_all | solution.py:1196
  354.1 10.1 %output_forward.1 = (f32[320,2048]{1,0:T(8,128)}, bf16[320,2048]{1,0:T(8,128)(2,1)}, bf16[320,128]{1,0:T(8,128)(2,1)}) custom-call(s32[1]{0:T(128)} %bitcast.16.flag_ref, bf16[16,320,128]{2,1,0:T(8,128)(2,1)} %all-to-all-done.3.att_ref, bf16[320,2048]{1,0:T(8,128)(2,1)} %bitcast.427, f32[1,2048]{1,0:T(1,128)} %bitcast.482, bf16[4,128,512]{2,1,0:T(8,128)(2,1)} %pad.33.a_ref, ...), custom_call_target="tpu_custom_call" | custom-call | flops 2684354560 | bytes 8388608 | tf_op jit(solution)/shard_map/output_forward/pallas_call | solution.py:653
  371.6 26.5 %feed_forward.4 = (f32[320,2048]{1,0:T(8,128)}, f32[320,2048]{1,0:T(8,128)}, f32[320,32]{1,0:T(8,128)}, f32[320,32]{1,0:T(8,128)}, f32[320,32]{1,0:T(8,128)}, /*...) custom-call(bf16[320,2048]{1,0:T(8,128)(2,1)} %get-tuple-element.93.h_ref, bf16[320,2048]{1,0:T(8,128)(2,1)} %bitcast.431, ...), custom_call_target="tpu_custom_call" | custom-call | flops 12079595520 | bytes 18874368 | tf_op jit(solution)/shard_map/feed_forward/pallas_call | solution.py:951
  404.2 26.6 %feed_forward.5 = (f32[320,2048]{1,0:T(8,128)}, f32[320,2048]{1,0:T(8,128)}, f32[320,32]{1,0:T(8,128)}, f32[320,32]{1,0:T(8,128)}, f32[320,32]{1,0:T(8,128)}, /*...) custom-call(bf16[320,2048]{1,0:T(8,128)(2,1)} %collective-permute-done.4.h_ref, bf16[320,2048]{1,0:T(8,128)(2,1)} %copy-done.10, ...), custom_call_target="tpu_custom_call" | custom-call | flops 12079595520 | bytes 18874368 | tf_op jit(solution)/shard_map/feed_forward/pallas_call | solution.py:951
  430.9 18.1 %all-gather.8.cloned.1.call-done = bf16[73728,128]{1,0:T(8,128)(2,1)} async-done(((bf16[4608,128]{1,0:T(8,128)(2,1)}), bf16[73728,128]{1,0:T(8,128)(2,1)}) %all-gather.8.cloned.1.call-update) | async-done | bytes 18874384 | tf_op jit(solution)/shard_map/all_gather | solution.py:1132
  448.9 28.5 %feed_forward.6 = (bf16[320,2048]{1,0:T(8,128)(2,1)}, bf16[320,2048]{1,0:T(8,128)(2,1)}, f32[4,96,512]{2,1,0:T(8,128)}, f32[6,96,128]{2,1,0:T(8,128)}, f32[6,96,128]{2,1,0:T(8,128)}) custom-call(bf16[320,2048]{1,0:T(8,128)(2,1)} %collective-permute-done.4.h_ref, bf16[320,2048]{1,0:T(8,128)(2,1)} %copy-done.10, bf16[320,32]{1,0:T(8,128)(2,1)} %fusion.3.mg_ref, ...), custom_call_target="tpu_custom_call" | custom-call | flops 12079595520 | bytes 18874368 | tf_op jit(solution)/shard_map/feed_forward/pallas_call | solution.py:951
  478.9 29.3 %feed_forward.7 = (f32[320,2048]{1,0:T(8,128)}, f32[320,2048]{1,0:T(8,128)}, f32[4,96,512]{2,1,0:T(8,128)}, f32[6,96,128]{2,1,0:T(8,128)}, f32[6,96,128]{2,1,0:T(8,128)}) custom-call(bf16[320,2048]{1,0:T(8,128)(2,1)} %get-tuple-element.93.h_ref, bf16[320,2048]{1,0:T(8,128)(2,1)} %bitcast.432, bf16[320,32]{1,0:T(8,128)(2,1)} %fusion.1.mg_ref, ...), custom_call_target="tpu_custom_call" | custom-call | flops 12079595520 | bytes 18874368 | tf_op jit(solution)/shard_map/feed_forward/pallas_call | solution.py:951
  508.7 11.9 %output_backward.1 = (f32[320,2048]{1,0:T(8,128)}, bf16[16,320,128]{2,1,0:T(8,128)(2,1)}, f32[4,16,512]{2,1,0:T(8,128)}, f32[4,16,512]{2,1,0:T(8,128)}) custom-call(s32[1]{0:T(128)} %bitcast.16.flag_ref, f32[320,2048]{1,0:T(8,128)} %get-tuple-element.112.gh_ref, bf16[320,2048]{1,0:T(8,128)(2,1)} %collective-permute-done.5.got_ref, ...), custom_call_target="tpu_custom_call" | custom-call | flops 2684354560 | bytes 8388608 | tf_op jit(solution)/shard_map/output_backward/pallas_call | solution.py:744
  530.7 22.3 %all-to-all-done.4 = bf16[16,320,128]{2,1,0:T(8,128)(2,1)} async-done(((bf16[16,320,128]{2,1,0:T(8,128)(2,1)}), bf16[16,320,128]{2,1,0:T(8,128)(2,1)}, u32[]{:S(2)}, u32[]{:S(2)}) %all-to-all-start.4) | async-done | bytes 1310752 | tf_op jit(solution)/shard_map/all_to_all | solution.py:1193
  553.0 8.1 %all-to-all-start.5 = ((bf16[16,280,128]{2,1,0:T(8,128)(2,1)}), bf16[16,280,128]{2,1,0:T(8,128)(2,1)}, u32[]{:S(2)}, u32[]{:S(2)}) async-start(bf16[16,280,128]{2,1,0:T(8,128)(2,1)} %pad_maximum_fusion), calls=%async_computation.5 | async-start | bytes 2293760 | tf_op jit(solution)/shard_map/all_to_all | solution.py:1341
  562.6 43.8 %attention_backward.1 = (bf16[5120,256]{1,0:T(8,128)(2,1)}, f32[5120,128]{1,0:T(8,128)}, bf16[5120,128]{1,0:T(8,128)(2,1)}) custom-call(s32[20]{0:T(128)} %compare_select_fusion.parent_ref, s32[1]{0:T(128)} %bitcast.1.flag_ref, bf16[5120,256]{1,0:T(8,128)(2,1)} %bitcast.447, bf16[5120,128]{1,0:T(8,128)(2,1)} %bitcast.30.g_ref, ...), custom_call_target="tpu_custom_call" | custom-call | flops 13421772800 | bytes 15728640 | tf_op jit(solution)/shard_map/attention_backward/pallas_call | solution.py:241
  640.5 10.9 %collective-permute-done.9 = bf16[320,512]{1,0:T(8,128)(2,1)S(1)} collective-permute-done((bf16[320,512]{1,0:T(8,128)(2,1)S(1)}, bf16[320,512]{1,0:T(8,128)(2,1)S(1)}, u32[]{:S(2)}, u32[]{:S(2)}) %collective-permute-start.9) | collective-permute-done | bytes 327712 | tf_op jit(solution)/shard_map/ppermute | solution.py:1327
  652.2 9.9 %collective-permute-done.10 = bf16[320,512]{1,0:T(8,128)(2,1)S(1)} collective-permute-done((bf16[320,512]{1,0:T(8,128)(2,1)S(1)}, bf16[320,512]{1,0:T(8,128)(2,1)S(1)}, u32[]{:S(2)}, u32[]{:S(2)}) %collective-permute-start.10) | collective-permute-done | bytes 327712 | tf_op jit(solution)/shard_map/ppermute | solution.py:1327
  662.9 8.9 %all-to-all-done.6.ret_ref = bf16[16,320,256]{2,1,0:T(8,128)(2,1)} async-done(((bf16[16,320,256]{2,1,0:T(8,128)(2,1)}), bf16[16,320,256]{2,1,0:T(8,128)(2,1)}, u32[]{:S(2)}, u32[]{:S(2)}) %all-to-all-start.6) | async-done | bytes 2621472 | tf_op jit(solution)/shard_map/all_to_all | solution.py:1196
  671.7 8.7 %collective-permute-start.12 = (bf16[2,112,128]{2,1,0:T(8,128)(2,1)S(1)}, bf16[2,112,128]{2,1,0:T(8,128)(2,1)}, u32[]{:S(2)}, u32[]{:S(2)}) collective-permute-start(bf16[2,112,128]{2,1,0:T(8,128)(2,1)S(1)} %slice.417), channel_id=1, source_target_pairs={{0,1},{1,0},{2,3},{3,2},{4,5},{5,4},{6,7},{7,6},{8,9},{9,8},{10,11... | collective-permute-start | bytes 172040 | tf_op jit(solution)/shard_map/ppermute | solution.py:1301
  685.9 10.8 %qkv_unshape.1 = (bf16[4,320,1024]{2,1,0:T(8,128)(2,1)}, bf16[320,48]{1,0:T(8,128)(2,1)}, f32[4,48,512]{2,1,0:T(8,128)}, f32[4,16,1024]{2,1,0:T(8,128)}) custom-call(bf16[16,320,256]{2,1,0:T(8,128)(2,1)} %all-to-all-done.6.ret_ref, f32[4,320,768]{2,1,0:T(8,128)} %get-tuple-element.146.pre_ref, bf16[320,48]{1,0:T(8,128)(2,1)} %get-tuple-element.147.m_ref, ...), custom_call_target="tpu_custom_call" | custom-call | flops 335544320 | bytes 10485760 | tf_op jit(solution)/shard_map/qkv_unshape/pallas_call | solution.py:504
  704.0 13.6 %qkv_backward.1 = bf16[320,2048]{1,0:T(8,128)(2,1)} custom-call(bf16[4,320,1024]{2,1,0:T(8,128)(2,1)} %get-tuple-element.148.grads_ref, bf16[320,48]{1,0:T(8,128)(2,1)} %get-tuple-element.149.inner_ref, bf16[320,2048]{1,0:T(8,128)(2,1)} %bitcast.429, f32[320,2048]{1,0:T(8,128)} %get-tuple-element.150.gm_ref, f32[1,2048]{1,0:T(1,128)} %bitcast.481, ...), custom_call_target="tpu_custom_call" | custom-call | flops 5368709120 | bytes 16777216 | tf_op jit(solution)/shard_map/qkv_backward/pallas_call | solution.py:573
  (383 shorter events, 211.7 us)
Async XLA Ops:
  7.2 157.4 %all-gather.4.cloned.1.call-start = ((), (), s32[]{:S(2)}) async-start(), calls=%async_computation.9 | async-start | bytes 23953408 | tf_op jit(solution)/shard_map/all_gather | solution.py:1084
  12.1 314.7 %all-gather.6.cloned.1.call-start = ((), (), s32[]{:S(2)}) async-start(), calls=%async_computation.10 | async-start | bytes 22282240 | tf_op jit(solution)/shard_map/all_gather | solution.py:1132
  12.1 24.4 %collective-permute-start.1 = (s32[1]{0:T(128)}, s32[1]{0:T(128)}, u32[]{:S(2)}, u32[]{:S(2)}) collective-permute-start(s32[1]{0:T(128)} %param.61), channel_id=1, source_target_pairs={{0,16},{16,0},{1,17},{17,1},{2,18},{18,2},{3,19},{19,3},{4,20},{20... | collective-permute-start | bytes 20 | tf_op jit(solution)/shard_map/ppermute | solution.py:1049
  46.4 402.5 %all-gather.8.cloned.1.call-start = ((), (), s32[]{:S(2)}) async-start(), calls=%async_computation.11 | async-start | bytes 20054016 | tf_op jit(solution)/shard_map/all_gather | solution.py:1132
  47.1 35.3 %all-to-all-start.1 = ((bf16[4,320,512]{2,1,0:T(8,128)(2,1)}), bf16[4,320,512]{2,1,0:T(8,128)(2,1)S(1)}, u32[]{:S(2)}, u32[]{:S(2)}) async-start(bf16[4,320,512]{2,1,0:T(8,128)(2,1)} %bitcast.456), calls=%async_computation.1 | async-start | bytes 2621440 | tf_op jit(solution)/shard_map/all_to_all | solution.py:1171
  82.4 52.1 %all-to-all-start = ((bf16[4,320,512]{2,1,0:T(8,128)(2,1)}), bf16[4,320,512]{2,1,0:T(8,128)(2,1)}, u32[]{:S(2)}, u32[]{:S(2)}) async-start(bf16[4,320,512]{2,1,0:T(8,128)(2,1)} %bitcast.2), calls=%async_computation | async-start | bytes 2621440 | tf_op jit(solution)/shard_map/all_to_all | solution.py:1170
  86.9 82.3 %collective-permute-start = (bf16[320,2048]{1,0:T(8,128)(2,1)S(1)}, bf16[320,2048]{1,0:T(8,128)(2,1)S(1)}, u32[]{:S(2)}, u32[]{:S(2)}) collective-permute-start(bf16[320,2048]{1,0:T(8,128)(2,1)S(1)} %bitcast.430), channel_id=1, source_target_pairs={{0,16},{16,0},{1,17},{17,1},{2,18},{18,2},{3,19},{19,3},{4,20},{20... | collective-permute-start | bytes 3932168 | tf_op jit(solution)/shard_map/ppermute | solution.py:1172
  188.2 98.7 %all-to-all-start.2 = ((bf16[16,320,256]{2,1,0:T(8,128)(2,1)}), bf16[16,320,256]{2,1,0:T(8,128)(2,1)S(1)}, u32[]{:S(2)}, u32[]{:S(2)}) async-start(bf16[16,320,256]{2,1,0:T(8,128)(2,1)} %get-tuple-element.88), calls=%async_computation.2 | async-start | bytes 5242880 | tf_op jit(solution)/shard_map/all_to_all | solution.py:1193
  193.5 93.4 %collective-permute-start.2 = (bf16[4,4,256,512]{3,2,1,0:T(8,128)(2,1)}, bf16[4,4,256,512]{3,2,1,0:T(8,128)(2,1)}, u32[]{:S(2)}, u32[]{:S(2)}) collective-permute-start(bf16[4,4,256,512]{3,2,1,0:T(8,128)(2,1)} %slice.465.own_ref), channel_id=1, source_target_pairs={{0,16},{16,0},{1,17},{17,1},{2,18},{18,2},{3,19},{19,3},{4,20},{20... | collective-permute-start | bytes 12582920 | tf_op jit(solution)/shard_map/ppermute | solution.py:1176
  316.8 37.3 %all-to-all-start.3 = ((bf16[16,320,128]{2,1,0:T(8,128)(2,1)}), bf16[16,320,128]{2,1,0:T(8,128)(2,1)}, u32[]{:S(2)}, u32[]{:S(2)}) async-start(bf16[16,320,128]{2,1,0:T(8,128)(2,1)} %bitcast.457), calls=%async_computation.3 | async-start | bytes 2621440 | tf_op jit(solution)/shard_map/all_to_all | solution.py:1196
  364.2 34.0 %collective-permute-start.4 = (bf16[320,2048]{1,0:T(8,128)(2,1)}, bf16[320,2048]{1,0:T(8,128)(2,1)}, u32[]{:S(2)}, u32[]{:S(2)}) collective-permute-start(bf16[320,2048]{1,0:T(8,128)(2,1)} %get-tuple-element.93.h_ref), channel_id=1, source_target_pairs={{0,16},{16,0},{1,17},{17,1},{2,18},{18,2},{3,19},{19,3},{4,20},{20... | collective-permute-start | bytes 3932168 | tf_op jit(solution)/shard_map/ppermute | solution.py:1221
  477.4 31.3 %collective-permute-start.5 = (bf16[320,2048]{1,0:T(8,128)(2,1)}, bf16[320,2048]{1,0:T(8,128)(2,1)}, u32[]{:S(2)}, u32[]{:S(2)}) collective-permute-start(bf16[320,2048]{1,0:T(8,128)(2,1)} %get-tuple-element.113), channel_id=1, source_target_pairs={{0,16},{16,0},{1,17},{17,1},{2,18},{18,2},{3,19},{19,3},{4,20},{20... | collective-permute-start | bytes 3932168 | tf_op jit(solution)/shard_map/ppermute | solution.py:1271
  520.6 32.4 %all-to-all-start.4 = ((bf16[16,320,128]{2,1,0:T(8,128)(2,1)}), bf16[16,320,128]{2,1,0:T(8,128)(2,1)}, u32[]{:S(2)}, u32[]{:S(2)}) async-start(bf16[16,320,128]{2,1,0:T(8,128)(2,1)} %get-tuple-element.117), calls=%async_computation.4 | async-start | bytes 2621440 | tf_op jit(solution)/shard_map/all_to_all | solution.py:1193
  553.0 53.4 %all-to-all-start.5 = ((bf16[16,280,128]{2,1,0:T(8,128)(2,1)}), bf16[16,280,128]{2,1,0:T(8,128)(2,1)}, u32[]{:S(2)}, u32[]{:S(2)}) async-start(bf16[16,280,128]{2,1,0:T(8,128)(2,1)} %pad_maximum_fusion), calls=%async_computation.5 | async-start | bytes 2293760 | tf_op jit(solution)/shard_map/all_to_all | solution.py:1341
  561.1 45.3 %collective-permute-start.6 = (bf16[320,2048]{1,0:T(8,128)(2,1)}, bf16[320,2048]{1,0:T(8,128)(2,1)}, u32[]{:S(2)}, u32[]{:S(2)}) collective-permute-start(bf16[320,2048]{1,0:T(8,128)(2,1)} %get-tuple-element.137), channel_id=1, source_target_pairs={{0,16},{16,0},{1,17},{17,1},{2,18},{18,2},{3,19},{19,3},{4,20},{20... | collective-permute-start | bytes 3932168 | tf_op jit(solution)/shard_map/ppermute | solution.py:1287
  615.4 56.3 %all-to-all-start.6 = ((bf16[16,320,256]{2,1,0:T(8,128)(2,1)}), bf16[16,320,256]{2,1,0:T(8,128)(2,1)}, u32[]{:S(2)}, u32[]{:S(2)}) async-start(bf16[16,320,256]{2,1,0:T(8,128)(2,1)} %bitcast.435), calls=%async_computation.6 | async-start | bytes 5242880 | tf_op jit(solution)/shard_map/all_to_all | solution.py:1196
  633.6 28.5 %collective-permute-start.10 = (bf16[320,512]{1,0:T(8,128)(2,1)S(1)}, bf16[320,512]{1,0:T(8,128)(2,1)S(1)}, u32[]{:S(2)}, u32[]{:S(2)}) collective-permute-start(bf16[320,512]{1,0:T(8,128)(2,1)S(1)} %bitcast.473), channel_id=1, source_target_pairs={{0,12},{4,8},{8,4},{12,0},{1,13},{5,9},{9,5},{13,1},{2,14},{6,10},... | collective-permute-start | bytes 983048 | tf_op jit(solution)/shard_map/ppermute | solution.py:1327
  671.7 45.9 %collective-permute-start.12 = (bf16[2,112,128]{2,1,0:T(8,128)(2,1)S(1)}, bf16[2,112,128]{2,1,0:T(8,128)(2,1)}, u32[]{:S(2)}, u32[]{:S(2)}) collective-permute-start(bf16[2,112,128]{2,1,0:T(8,128)(2,1)S(1)} %slice.417), channel_id=1, source_target_pairs={{0,1},{1,0},{2,3},{3,2},{4,5},{5,4},{6,7},{7,6},{8,9},{9,8},{10,11... | collective-permute-start | bytes 172040 | tf_op jit(solution)/shard_map/ppermute | solution.py:1301
  680.4 39.7 %collective-permute-start.13 = (bf16[2,112,128]{2,1,0:T(8,128)(2,1)S(1)}, bf16[2,112,128]{2,1,0:T(8,128)(2,1)}, u32[]{:S(2)}, u32[]{:S(2)}) collective-permute-start(bf16[2,112,128]{2,1,0:T(8,128)(2,1)S(1)} %slice.417), channel_id=1, source_target_pairs={{0,2},{1,3},{2,0},{3,1},{4,6},{5,7},{6,4},{7,5},{8,10},{9,11},{10,... | collective-permute-start | bytes 172040 | tf_op jit(solution)/shard_map/ppermute | solution.py:1301
  683.2 37.8 %collective-permute-start.14 = (bf16[2,112,128]{2,1,0:T(8,128)(2,1)S(1)}, bf16[2,112,128]{2,1,0:T(8,128)(2,1)}, u32[]{:S(2)}, u32[]{:S(2)}) collective-permute-start(bf16[2,112,128]{2,1,0:T(8,128)(2,1)S(1)} %slice.417), channel_id=1, source_target_pairs={{0,3},{1,2},{2,1},{3,0},{4,7},{5,6},{6,5},{7,4},{8,11},{9,10},{10,... | collective-permute-start | bytes 172040 | tf_op jit(solution)/shard_map/ppermute | solution.py:1301
  684.6 37.2 %collective-permute-start.15 = (bf16[2,168,128]{2,1,0:T(8,128)(2,1)S(1)}, bf16[2,168,128]{2,1,0:T(8,128)(2,1)S(1)}, u32[]{:S(2)}, u32[]{:S(2)}) collective-permute-start(bf16[2,168,128]{2,1,0:T(8,128)(2,1)S(1)} %slice.418), channel_id=1, source_target_pairs={{0,4},{4,0},{8,12},{12,8},{1,5},{5,1},{9,13},{13,9},{2,6},{6,2},{1... | collective-permute-start | bytes 258056 | tf_op jit(solution)/shard_map/ppermute | solution.py:1301
  684.7 37.3 %collective-permute-start.16 = (bf16[2,168,128]{2,1,0:T(8,128)(2,1)S(1)}, bf16[2,168,128]{2,1,0:T(8,128)(2,1)S(1)}, u32[]{:S(2)}, u32[]{:S(2)}) collective-permute-start(bf16[2,168,128]{2,1,0:T(8,128)(2,1)S(1)} %slice.418), channel_id=1, source_target_pairs={{0,8},{4,12},{8,0},{12,4},{1,9},{5,13},{9,1},{13,5},{2,10},{6,14},... | collective-permute-start | bytes 258056 | tf_op jit(solution)/shard_map/ppermute | solution.py:1301
  699.7 22.9 %all-to-all-start.7 = ((bf16[16,80,128]{2,1,0:T(8,128)(2,1)}), bf16[16,80,128]{2,1,0:T(8,128)(2,1)}, u32[]{:S(2)}, u32[]{:S(2)}) async-start(bf16[16,80,128]{2,1,0:T(8,128)(2,1)} %pad_maximum_fusion.4), calls=%async_computation.7 | async-start | bytes 655360 | tf_op jit(solution)/shard_map/all_to_all | solution.py:1368
  725.2 30.4 %all-to-all-start.8 = ((bf16[320,4,512]{2,0,1:T(8,128)(2,1)}), bf16[320,4,512]{2,0,1:T(8,128)(2,1)S(1)}, u32[]{:S(2)}, u32[]{:S(2)}) async-start(bf16[320,4,512]{2,0,1:T(8,128)(2,1)} %bitcast.405), calls=%async_computation.8 | async-start | bytes 2621440 | tf_op jit(solution)/shard_map/all_to_all | solution.py:1373
  (66 other events, 482.6 us)
Sparse Core Ops, SparseCore 0:
  12.2 152.3 all-gather.3
  166.2 157.3 all-gather.5
  325.2 123.6 all-gather.7
